TPU v7x, 512 devices: a whole 4x8x8 slice. The times are simulated.
512 devices in a mesh: dp: 32 (over z, x), tensor: 16 (over y, core).
Axes of the slice: x: 4, y: 8, z: 8, core: 2. Of those that a mesh axis runs over, the one named last changes fastest.
Arguments:
- activations: bfloat16 [16384, 4096], P('dp', 'tensor'), may hold values from -6 to 6
- base_weight: bfloat16 [4096, 4096], P('tensor'), may hold values from -8.4375 to 8.4375
- adapter_in: float32 [4096, 64], P('tensor'), may hold values from -0.09375 to 0.09375
- adapter_out: float32 [64, 4096], replicated, may hold values from -0.75 to 0.75
- magnitude: float32 [4096], replicated, may hold values from 0.5 to 2
- cotangent: bfloat16 [16384, 4096], P(('dp', 'tensor')), may hold values from -1.5 to 1.5
Outputs:
- output: bfloat16 [16384, 4096], P(('dp', 'tensor'))
- grad_act: bfloat16 [16384, 4096], P('dp', 'tensor')
- grad_in: float32 [4096, 64], P('tensor')
- grad_out: float32 [64, 4096], replicated
- grad_mag: float32 [4096], replicated
All inputs are finite; a program needn't handle non-finite values.
Results may differ from a plain program's by a relative error of at most 0.0057.
Values may be sent and summed in bfloat16 or wider, within the bound.
No kernel may reach another device: no remote copies, remote signals or barrier semaphores. Data moves between devices by JAX's collectives and lax.ppermute only.
A program may use at most 128 MiB of HBM per device.

v0:
```python
import jax
import jax.numpy as jnp
from jax import lax
from jax.sharding import PartitionSpec as P

epsilon = 1e-06


def shards(activations, base_weight, adapter_in, adapter_out, magnitude, cotangent):
    highest = lax.Precision.HIGHEST
    lowrank = jnp.dot(adapter_in, adapter_out, precision=highest)
    merged = base_weight.astype(jnp.float32) + lowrank
    squares = jnp.sum(merged * merged, axis=0)
    square_sum = lax.psum(squares, "tensor")
    col_norm = jnp.sqrt(square_sum + epsilon)
    col_scale = magnitude / col_norm
    merged_low = merged.astype(jnp.bfloat16)
    act_rows = activations
    summed = lax.psum_scatter(
        jnp.dot(act_rows, merged_low, preferred_element_type=jnp.float32),
        "tensor",
        scatter_dimension=0,
        tiled=True,
    )
    output = (summed * col_scale).astype(jnp.bfloat16)
    cot_float = cotangent.astype(jnp.float32)
    grad_scaled = (cot_float * col_scale).astype(jnp.bfloat16)
    mag_slope = jnp.sum(cot_float * summed, axis=0) / col_norm
    block_part = lax.all_gather(grad_scaled, "tensor", axis=0, tiled=True)
    act_rows = activations
    product = lax.dot_general(
        block_part, merged_low, (((1,), (1,)), ((), ())), preferred_element_type=jnp.float32
    )
    act_total = product
    dir_total = lax.dot_general(
        act_rows, block_part, (((0,), (0,)), ((), ())), preferred_element_type=jnp.float32
    )
    act_total, grad_dir = (act_total, dir_total)
    grad_act = act_total.astype(jnp.bfloat16)
    slope_replica = lax.psum(mag_slope, "tensor")
    norm_coeff = -slope_replica * magnitude / (col_norm * col_norm)
    full_dir = grad_dir + merged * norm_coeff
    in_replica = jnp.dot(full_dir, adapter_out.T, precision=highest)
    cross_term = jnp.dot(adapter_in.T, full_dir, precision=highest)
    out_replica = lax.psum(cross_term, "tensor")
    grad_in, grad_out, grad_mag = lax.psum((in_replica, out_replica, slope_replica), "dp")
    return (output, grad_act, grad_in, grad_out, grad_mag)


def solution(mesh):
    in_specs = (
        P("dp", "tensor"),
        P("tensor", None),
        P("tensor", None),
        P(),
        P(),
        P(("dp", "tensor"), None),
    )
    out_specs = (P(("dp", "tensor"), None), P("dp", "tensor"), P("tensor", None), P(), P())
    return jax.shard_map(shards, mesh=mesh, in_specs=in_specs, out_specs=out_specs, check_vma=False)
```

profile of v0, /device:TPU:16, one launch (start us, length us, event | category | flops | bytes accessed | tf_op | source)
XLA Modules:
  0.0 470.0 jit_solution(9922781715581071053)
XLA Ops:
  7.2 0.0 copy-start
  7.2 0.0 copy-start.4
  7.2 0.0 reduce-scatter.4.cloned.1.call-start
  7.2 1.2 copy-done
  8.4 5.5 %multiply_reduce_fusion = (f32[4096]{0:T(1024)S(1)}, f32[256,4096]{1,0:T(8,128)S(1)}) fusion(f32[256,64]{0,1:T(8,128)} %param.8, f32[64,4096]{1,0:T(8,128)S(1)} %copy-done, bf16[256,4096]{1,0:T(8,128)(2,1)} %param.7), kind=kOutput, calls=%fused_computation.5 | convolution fusion | flops 809496576 | bytes 7421952 | tf_op jit(solution)/shard_map/dot_general | solution.py:11
  13.9 0.0 copy-start.1
  13.9 1.9 copy-done.1
  15.9 0.0 copy-done.4
  15.9 4.5 convolution_bitcast_fusion
  20.4 9.0 %copy.19 = f32[512,4096]{1,0:T(8,128)} copy(f32[512,4096]{0,1:T(8,128)} %convolution_bitcast_fusion) | data formatting | bytes 16777216
  29.4 0.0 copy-start.5
  29.4 0.0 copy-start.7
  29.5 0.0 reduce-scatter.4.cloned.1.call-update
  29.5 0.0 all-gather.2.cloned.1.call-start
  29.5 0.9 copy-done.5
  30.4 1.3 copy.14
  31.7 45.2 %psum.42 = f32[4096]{0:T(1024)S(1)} all-reduce(f32[4096]{0:T(1024)S(1)} %get-tuple-element.20), channel_id=1, replica_groups=mesh['dp'=32,'tensor'=16] {'tensor'}, use_global_device_ids=true, to_apply=%region_2.0 | all-reduce | flops 4096 | bytes 32768 | tf_op jit(solution)/shard_map/psum | solution.py:14
  76.9 0.0 copy-done.7
  76.9 25.0 %reduce-scatter.4.cloned.1.call-done = f32[32,4096]{1,0:T(8,128)} async-done(((f32[512,4096]{1,0:T(8,128)}), f32[32,4096]{1,0:T(8,128)}) %reduce-scatter.4.cloned.1.call-update) | async-done | bytes 524304
  101.9 1.6 copy.20
  103.5 3.3 fusion.2
  106.8 2.2 copy.15
  109.1 0.0 all-gather.2.cloned.1.call-update
  109.1 0.0 all-reduce.4.cloned.1.call-start
  109.2 49.6 %psum.43 = f32[4096]{0:T(1024)S(1)} all-reduce(f32[4096]{0:T(1024)S(1)} %fusion.5), channel_id=1, replica_groups=mesh['dp'=32,'tensor'=16] {'tensor'}, use_global_device_ids=true, to_apply=%region_4.0 | all-reduce | flops 4096 | bytes 32768 | tf_op jit(solution)/shard_map/psum | solution.py:40
  158.7 0.0 copy-start.6
  158.8 0.0 all-gather.2.cloned.1.call-done
  158.8 5.0 %fusion = f32[256,4096]{1,0:T(8,128)S(1)} fusion(bf16[512,4096]{1,0:T(8,128)(2,1)} %all-gather.2.cloned.1.call-done, bf16[512,256]{1,0:T(8,128)(2,1)S(1)} %copy-done.4, f32[256,4096]{1,0:T(8,128)} %copy-done.1, f32[4096]{0:T(1024)S(1)} %multiply_divide_fusion), kind=kOutput, calls=%fused_computation.2 | convolution fusion | flops 1075838976 | bytes 12861440 | tf_op jit(solution)/shard_map/dot_general | solution.py:35
  163.8 0.0 copy-start.2
  163.8 2.0 copy-done.2
  165.8 0.0 copy-done.6
  165.8 3.8 convolution_bitcast_fusion.2
  169.6 0.0 copy-start.3
  169.6 0.0 all-reduce.4.cloned.1.call-update
  169.6 0.2 all-reduce.6.cloned.1.call-start
  169.8 6.8 %fusion.7 = f32[256,64]{0,1:T(8,128)} fusion(f32[256,4096]{1,0:T(8,128)} %copy-done.2, f32[64,4096]{1,0:T(8,128)S(1)} %copy-done), kind=kOutput, calls=%fused_computation.18 | convolution fusion | flops 805306368 | bytes 5308416 | tf_op jit(solution)/shard_map/dot_general | solution.py:43
  176.6 113.8 %all-reduce.4.cloned.1.call-done = f32[64,4096]{1,0:T(8,128)} async-done(((f32[64,4096]{1,0:T(8,128)}), f32[64,4096]{1,0:T(8,128)}) %all-reduce.4.cloned.1.call-update) | async-done | bytes 1048592 | tf_op jit(solution)/shard_map/psum | solution.py:45
  290.4 0.0 all-reduce.6.cloned.1.call-update
  290.4 0.0 copy-done.3
  290.4 1.0 copy.17
  291.5 143.8 %psum.47 = f32[4096]{0:T(1024)} all-reduce(f32[4096]{0:T(1024)S(1)} %psum.43), channel_id=1, replica_groups=mesh['dp'=32,'tensor'=16] {'dp'}, use_global_device_ids=true, to_apply=%region_8.0 | all-reduce | flops 4096 | bytes 32768 | tf_op jit(solution)/shard_map/psum | solution.py:46
  435.2 5.5 %convolution_convert_fusion = bf16[512,256]{1,0:T(8,128)(2,1)} fusion(bf16[512,4096]{1,0:T(8,128)(2,1)} %all-gather.2.cloned.1.call-done, f32[256,4096]{1,0:T(8,128)} %copy-done.1), kind=kOutput, calls=%fused_computation.11 | convolution fusion | flops 1074921472 | bytes 8650752 | tf_op jit(solution)/shard_map/dot_general | solution.py:31
  440.7 19.0 %all-reduce.6.cloned.1.call-done = (f32[256,64]{0,1:T(8,128)}, f32[64,4096]{1,0:T(8,128)}) async-done(((f32[256,64]{0,1:T(8,128)}, f32[64,4096]{1,0:T(8,128)}), (f32[256,64]{0,1:T(8,128)}, f32[64,4096]{1,0:T(8,128)})) %all-reduce.6.cloned.1.call-update) | async-done | bytes 1114128 | tf_op jit(solution)/shard_map/psum | solution.py:46
  459.8 1.5 copy.24
  461.2 2.3 copy.25
  (3 shorter events, 0.0 us)
Async XLA Ops:
  7.2 1.2 copy-start
  7.2 8.7 %copy-start.4 = (bf16[512,256]{1,0:T(8,128)(2,1)S(1)}, bf16[512,256]{1,0:T(8,128)(2,1)}, u32[]{:S(2)}) copy-start(bf16[512,256]{1,0:T(8,128)(2,1)} %param.6) | copy-start | bytes 786436
  7.2 94.7 %reduce-scatter.4.cloned.1.call-start = ((), (), s32[]{:S(2)}) async-start(), calls=%async_computation.3 | async-start | bytes 8912896
  13.9 1.9 copy-start.1
  29.4 0.9 copy-start.5
  29.4 47.5 %copy-start.7 = (f32[4096]{0:T(1024)S(1)}, f32[4096]{0:T(1024)}, u32[]{:S(2)}) copy-start(f32[4096]{0:T(1024)} %param.10) | copy-start | bytes 49156
  29.5 129.3 %all-gather.2.cloned.1.call-start = ((), (), s32[]{:S(2)}) async-start(), calls=%async_computation.1 | async-start | bytes 4456448 | tf_op jit(solution)/shard_map/all_gather | solution.py:29
  109.1 181.3 %all-reduce.4.cloned.1.call-start = ((), (), s32[]{:S(2)}) async-start(), calls=%async_computation.2 | async-start | bytes 2097152 | tf_op jit(solution)/shard_map/psum | solution.py:45
  158.7 7.0 %copy-start.6 = (f32[256,64]{0,1:T(8,128)S(1)}, f32[256,64]{0,1:T(8,128)}, u32[]{:S(2)}) copy-start(f32[256,64]{0,1:T(8,128)} %param.8) | copy-start | bytes 196612
  163.8 2.0 copy-start.2
  169.6 120.8 %copy-start.3 = (bf16[32,4096]{0,1:T(8,128)(2,1)S(1)}, bf16[32,4096]{0,1:T(8,128)(2,1)}, u32[]{:S(2)}) copy-start(bf16[32,4096]{0,1:T(8,128)(2,1)} %get-tuple-element.18) | copy-start | bytes 786436
  169.6 290.2 %all-reduce.6.cloned.1.call-start = ((), (), s32[]{:S(2)}) async-start(), calls=%async_computation.4 | async-start | bytes 2228224 | tf_op jit(solution)/shard_map/psum | solution.py:46
Sparse Core Ops, SparseCore 0:
  29.6 72.2 reduce-scatter.3
  109.2 48.3 all-gather.1
  169.7 120.6 all-reduce.3
  294.3 165.3 all-reduce.5
where the time goes:
time: 471 us; the launch traced here: 470 us
  blocking collectives  239 us (51%)
  waiting for transfers between devices  158 us (34%)
  matrix products  31.2 us (7%)
  local copies, waits for them, and re-layouts  24.9 us (5%)
  between operations  13.9 us (3%)
    psum x1, blocking collectives, shards(): lax.psum((in_replica, out_replica, slope_replica), 'dp')  144 us
    psum x1, waiting for transfers between devices, shards(): out_replica = lax.psum(cross_term, 'tensor')  114 us
    psum x1, blocking collectives, shards(): slope_replica = lax.psum(mag_slope, 'tensor')  49.6 us
    psum x1, blocking collectives, shards(): square_sum = lax.psum(squares, 'tensor')  45.2 us
    unnamed x5, waiting for transfers between devices  25 us
    unnamed x22, local copies, waits for them, and re-layouts  22.7 us
    psum x1, waiting for transfers between devices, shards(): lax.psum((in_replica, out_replica, slope_replica), 'dp')  19 us
  transfers between devices with their start and end apart: 4, of which 3 were waited for; matrix products, arithmetic and copies ran while one was open for 3% of the time, Pallas kernels for 0%

commit v1 on v0

v1 whole, which is shorter than its diff:
```python
import jax
import jax.numpy as jnp
from jax import lax
from jax.experimental import pallas as pl
from jax.experimental.pallas import tpu as pltpu
from jax.sharding import Mesh, PartitionSpec as P


epsilon = 1e-06
F32, BF16 = jnp.float32, jnp.bfloat16
REPLICA = ("z", "x")
TENSOR = ("y", "core")
TILE = 512


def split(value):
    high = value.astype(BF16)
    return high, (value - high.astype(F32)).astype(BF16)


def contract(left, right, dims):
    return lax.dot_general(left, right, ((dims[:1], dims[1:]), ((), ())), preferred_element_type=F32)


def merge_kernel(base_ref, wide_ref, pick_ref, out_ref, zt, low_ref, first_ref):
    step = pl.program_id(0)
    ah, al = split(out_ref[...])
    low = contract(wide_ref[...], jnp.concatenate([ah, al, ah, al], 0), (1, 0))
    merged = base_ref[...].astype(F32) + low
    squares = jnp.sum(merged * merged, axis=0, keepdims=True)
    rounded = merged.astype(BF16)

    low_ref[...] = rounded
    picked = contract(pick_ref[...], rounded, (1, 0))
    picked = picked[0:8] + picked[8:16]
    ranks = zt[pl.ds(pl.multiple_of(step * 16, 16), 16), :]
    for k in range(4):
        for q in range(4):
            first_ref[k, 4 * q : 4 * q + 4, :] = ranks[4 * k : 4 * k + 4, 128 * q : 128 * q + 128]
        for r in range(2):
            span = slice(256 * k + 128 * r, 256 * k + 128 * r + 128)
            first_ref[k, 16 + r : 17 + r, :] = squares[:, span]
            first_ref[k, 18 + r : 19 + r, :] = picked[0:1, span]
            first_ref[k, 20 + r : 21 + r, :] = picked[1:2, span]
        first_ref[k, 22:24, :] = jnp.zeros((2, 128), F32)


def merge(base, wide, pick, adapter_out, zt):
    rows, cols = base.shape
    tokens = zt.shape[1]
    steps = cols // 1024
    tile = lambda i: (0, i)
    whole = lambda i: (0, 0)
    return pl.pallas_call(
        merge_kernel,
        out_shape=(
            jax.ShapeDtypeStruct((rows, cols), BF16),
            jax.ShapeDtypeStruct((16, 24, 128), F32),
        ),
        grid_spec=pltpu.PrefetchScalarGridSpec(
            num_scalar_prefetch=0,
            grid=(steps,),
            in_specs=[
                pl.BlockSpec((rows, 1024), tile),
                pl.BlockSpec((rows, 256), whole),
                pl.BlockSpec((16, rows), whole),
                pl.BlockSpec((64, 1024), tile),
                pl.BlockSpec((64, tokens), whole),
            ],
            out_specs=(
                pl.BlockSpec((rows, 1024), tile),
                pl.BlockSpec((4, 24, 128), lambda i: (i, 0, 0)),
            ),
        ),
        cost_estimate=pl.CostEstimate(flops=1400000000, bytes_accessed=7000000, transcendentals=0),
        name="merge",
    )(base, wide, pick, adapter_out, zt)


def forward_kernel(at_ref, a_ref, b_ref, wa_ref, wb_ref, r4_ref, r3_ref, r2_ref, r1_ref, r0_ref, acts):
    @pl.when(pl.program_id(0) == 0)
    def _():
        for k in range(8):
            rows = pl.ds(pl.multiple_of(at_ref[17 + k] * 32, 32), 32)
            acts[32 * k : 32 * k + 32, :256] = a_ref[rows, :]
            acts[32 * k : 32 * k + 32, 256:] = b_ref[rows, :]

    part = contract(acts[...], jnp.concatenate([wa_ref[...], wb_ref[...]], 0), (1, 0))
    r4_ref[...] = part[0:32].astype(BF16)
    r3_ref[...] = part[32:96]
    r2_ref[...] = part[96:160]
    r1_ref[...] = part[160:224]
    r0_ref[...] = part[224:256]


def forward(at, act_own, act_peer, w_own, w_peer):
    tokens, feats = act_own.shape
    cols = w_own.shape[1]
    whole = pl.BlockSpec((tokens, feats), lambda i, c: (0, 0))
    tile = lambda rows: pl.BlockSpec((rows, 1024), lambda i, c: (0, i))
    rows = (32, 64, 64, 64, 32)
    kinds = (BF16, F32, F32, F32, F32)
    return pl.pallas_call(
        forward_kernel,
        out_shape=tuple(jax.ShapeDtypeStruct((r, cols), k) for r, k in zip(rows, kinds)),
        grid_spec=pltpu.PrefetchScalarGridSpec(
            num_scalar_prefetch=1,
            grid=(cols // 1024,),
            in_specs=[whole, whole, tile(feats), tile(feats)],
            out_specs=tuple(tile(r) for r in rows),
            scratch_shapes=[pltpu.VMEM((256, 512), BF16)],
        ),
        cost_estimate=pl.CostEstimate(flops=2 * tokens * feats * cols, bytes_accessed=5000000, transcendentals=0),
        name="forward",
    )(at, act_own, act_peer, w_own, w_peer)


def backward_kernel(
    at_ref, block_ref, hop1_ref, hop2_ref, hop3_ref, hop4_ref, cross_ref, scale_ref,
    wo_ref, wp_ref, ato_ref, atp_ref, second_ref, out_ref,
    gao_ref, gap_ref, in_ref, gm_ref, p_ref, cots, sum_own, sum_peer, sum_y, zt,
):
    step = pl.program_id(0)

    @pl.when(step == 0)
    def _():
        for m in range(16):
            for q in range(4):
                zt[4 * m : 4 * m + 4, 128 * q : 128 * q + 128] = second_ref[m, 4 * q : 4 * q + 4, :]

    parts = [block_ref, hop1_ref, hop2_ref, hop3_ref, hop4_ref]
    parts = [(part, r) for part in parts for r in (0, 32)] + [(cross_ref, r) for r in range(0, 192, 32)]
    for k, (part, r) in enumerate(parts):
        cots[pl.ds(pl.multiple_of(at_ref[1 + k] * 32, 32), 32), :] = part[r : r + 32, :]
    cot = cots[...]
    scaled = (cot.astype(F32) * scale_ref[...]).astype(BF16)
    w_own, w_peer = wo_ref[...], wp_ref[...]
    slope = jnp.sum(contract(ato_ref[...], cot, (1, 0)) * w_own.astype(F32), axis=0, keepdims=True)
    gm_ref[...] = slope + jnp.sum(contract(atp_ref[...], cot, (1, 0)) * w_peer.astype(F32), axis=0, keepdims=True)
    zh, zl = split(zt[...])
    both = contract(jnp.concatenate([zh, zl], 0), scaled, (1, 0))
    p_ref[...] = (both[:64] + both[64:]).astype(BF16)
    ah, al = split(out_ref[...])
    own = contract(scaled, w_own, (1, 1))
    peer = contract(scaled, w_peer, (1, 1))
    y = contract(scaled, jnp.concatenate([ah, al], 0), (1, 1))

    @pl.when(step == 0)
    def _():
        sum_own[...] = own
        sum_peer[...] = peer
        sum_y[...] = y

    @pl.when(step > 0)
    def _():
        sum_own[...] += own
        sum_peer[...] += peer
        sum_y[...] += y

    @pl.when(step == pl.num_programs(0) - 1)
    def _():
        gao_ref[...] = sum_own[...]
        gap_ref[...] = sum_peer[...].astype(BF16)
        pair = jnp.concatenate(split(sum_y[...]), 0)
        for k, ref in enumerate((ato_ref, atp_ref)):
            both = contract(jnp.concatenate([ref[...], ref[...]], 1), pair, (1, 0))
            in_ref[256 * k : 256 * k + 256, :] = (both[:, :64] + both[:, 64:]).astype(BF16)


def backward(at, block, hops, hop4, crossed, scale, w_own, w_peer, at_own, at_peer, second, adapter_out):
    cols = hop4.shape[1]
    feats, tokens = at_own.shape
    steps = cols // TILE
    whole = lambda i, c: (0, 0)
    tile = lambda i, c: (0, i)
    side = lambda i, c: (0, c[0] * steps + i)
    return pl.pallas_call(
        backward_kernel,
        out_shape=(
            jax.ShapeDtypeStruct((tokens, feats), F32),
            jax.ShapeDtypeStruct((tokens, feats), BF16),
            jax.ShapeDtypeStruct((2 * feats, 64), BF16),
            jax.ShapeDtypeStruct((1, cols), F32),
            jax.ShapeDtypeStruct((64, cols), BF16),
        ),
        grid_spec=pltpu.PrefetchScalarGridSpec(
            num_scalar_prefetch=1,
            grid=(steps,),
            in_specs=[pl.BlockSpec((64, TILE), side)] * 4
            + [
                pl.BlockSpec((64, TILE), tile),
                pl.BlockSpec((192, TILE), tile),
                pl.BlockSpec((1, TILE), side),
                pl.BlockSpec((feats, TILE), side),
                pl.BlockSpec((feats, TILE), side),
                pl.BlockSpec((feats, tokens), whole),
                pl.BlockSpec((feats, tokens), whole),
                pl.BlockSpec((16, 24, 128), lambda i, c: (0, 0, 0)),
                pl.BlockSpec((64, TILE), side),
            ],
            out_specs=(
                pl.BlockSpec((tokens, feats), whole),
                pl.BlockSpec((tokens, feats), whole),
                pl.BlockSpec((2 * feats, 64), whole),
                pl.BlockSpec((1, TILE), tile),
                pl.BlockSpec((64, TILE), tile),
            ),
            scratch_shapes=[
                pltpu.VMEM((tokens, TILE), BF16),
                pltpu.VMEM((tokens, feats), F32),
                pltpu.VMEM((tokens, feats), F32),
                pltpu.VMEM((tokens, 128), F32),
                pltpu.VMEM((64, tokens), F32),
            ],
        ),
        cost_estimate=pl.CostEstimate(flops=5000000000, bytes_accessed=8000000, transcendentals=0),
        name="backward",
    )(at, block, *hops, hop4, crossed, scale, w_own, w_peer, at_own, at_peer, second, adapter_out)


def finish_kernel(at_ref, wo_ref, wp_ref, a_ref, c_ref, o_ref):
    high, low = split(a_ref[...] * c_ref[...])
    pair = jnp.concatenate([high, low], 0)
    own = contract(wo_ref[...], pair, (1, 1))
    o_ref[0:256, :] = own[:, :64] + own[:, 64:]
    peer = contract(wp_ref[...], pair, (1, 1))
    o_ref[256:512, :] = peer[:, :64] + peer[:, 64:]


def finish(at, w_own, w_peer, adapter_out, coeff):
    cols = coeff.shape[1]
    side = lambda i, c: (0, c[0])
    return pl.pallas_call(
        finish_kernel,
        out_shape=jax.ShapeDtypeStruct((512, 64), F32),
        grid_spec=pltpu.PrefetchScalarGridSpec(
            num_scalar_prefetch=1,
            grid=(1,),
            in_specs=[
                pl.BlockSpec((256, cols), side),
                pl.BlockSpec((256, cols), side),
                pl.BlockSpec((64, cols), side),
                pl.BlockSpec((1, cols), lambda i, c: (0, 0)),
            ],
            out_specs=pl.BlockSpec((512, 64), lambda i, c: (0, 0)),
        ),
        cost_estimate=pl.CostEstimate(flops=600000000, bytes_accessed=3000000, transcendentals=0),
        name="finish",
    )(at, w_own, w_peer, adapter_out, coeff)


def program(activations, base_weight, adapter_in, adapter_out, magnitude, cotangent):
    core = lax.axis_index("core")
    y = lax.axis_index("y")
    replica = lax.axis_index(REPLICA)
    sides = lax.axis_size("y")
    replicas = lax.axis_size(REPLICA)
    half = adapter_out.shape[1] // 2
    hops = [(2 * s, 2 * ((s + 1) % sides)) for s in range(sides)]
    hops += [(2 * s + 1, 2 * ((s - 1) % sides) + 1) for s in range(sides)]

    def swap(value):
        return lax.ppermute(value, "core", [(0, 1), (1, 0)])

    def shift(value):
        return lax.ppermute(value, TENSOR, hops)

    def exchange(value, axes):
        return lax.all_to_all(value, axes, 0, 0)

    def spread(value, axes):
        return exchange(jnp.broadcast_to(value, (lax.axis_size(axes),) + value.shape), axes)

    mine = lambda value: lax.dynamic_slice_in_dim(value, core * half, half, 1)
    other = lambda value: lax.dynamic_slice_in_dim(value, (1 - core) * half, half, 1)

    block = jnp.concatenate([cotangent, swap(cotangent)], 0)
    hop1 = shift(block)
    hop2 = shift(hop1)
    hop3 = shift(hop2)
    sign = 1 - 2 * core
    near, far = [], []
    for k in range(5):
        chip = lax.rem(y - sign * k + sides, sides) * 2
        near += [chip + core, chip + 1 - core]
    for k in range(1, 4):
        chip = lax.rem(y + sign * k + sides, sides) * 2
        far += [chip + 1 - core, chip + core]
    rows = [lax.rem(y + sign * 4 + sides, sides) * 2 + core]
    for k in (3, 2, 1):
        chip = lax.rem(y + sign * k + sides, sides) * 2
        rows += [chip + core, chip + 1 - core]
    rows += [2 * y + core]
    at = jnp.stack([core] + near + far + rows).astype(jnp.int32)

    act_peer = swap(activations)
    high = lax.reduce_precision(adapter_in, 8, 7)
    rest = (adapter_in - high).astype(BF16)
    high = high.astype(BF16)
    wide = jnp.concatenate([high, high, rest, rest], 1)
    pair = jnp.concatenate([high.T, rest.T], 0)
    none = jnp.zeros((6, 256), BF16)
    pick = [lax.dynamic_slice_in_dim(pair, 64 * k + replica * 2, 2, 0) for k in range(2)]
    pick = jnp.concatenate([pick[0], none, pick[1], none], 0)
    at_own = activations.T
    z = contract(pair, at_own, (1, 0))
    w_own, first = merge(base_weight, wide, pick, adapter_out, z[:64] + z[64:])
    w_peer = swap(w_own)
    first = jnp.sum(exchange(first, TENSOR), axis=0)
    second = spread(first, TENSOR)
    hop4 = shift(mine(hop3))
    crossed = swap(jnp.concatenate([other(hop1), other(hop2), other(hop3)], 0))

    square_sum = second[:, 16:18].reshape(1, 2 * half)
    col_norm = jnp.sqrt(square_sum + epsilon)
    magnitude = magnitude.reshape(1, 2 * half)
    col_scale = magnitude / col_norm
    norm, size = mine(col_norm), mine(magnitude)
    q_mine = lax.dynamic_slice_in_dim(second, core * 8, 8, 0)[:, 18:22].reshape(8, 2, 256)
    q_mine = q_mine.transpose(1, 0, 2).reshape(32, 128).astype(BF16)
    q_half = spread(q_mine, REPLICA).reshape(64, half).astype(F32)

    r4, r3, r2, r1, r0 = forward(at, activations, act_peer, w_own, w_peer)
    got = shift(r4).astype(F32)
    got = shift(jnp.concatenate([r3[:32] + got, r3[32:]], 0).astype(BF16)).astype(F32)
    got = shift((r2 + got).astype(BF16)).astype(F32)
    got = shift((r1 + got).astype(BF16))
    summed = r0 + got[:32].astype(F32) + swap(got[32:]).astype(F32)
    output = (summed * col_scale).astype(BF16)

    at_peer = act_peer.T
    act_own, act_send, in_part, slope, p_part = backward(
        at, block, (hop1, hop2, hop3), hop4, crossed, col_scale, w_own, w_peer, at_own, at_peer, second, adapter_out
    )
    low = jnp.concatenate([p_part.reshape(replicas, 32, 128), in_part.reshape(replicas, 8, 128)], 1)
    low, q_half = lax.optimization_barrier((low, q_half))
    low = jnp.sum(exchange(low, REPLICA).astype(F32), axis=0).astype(BF16)
    slope = lax.psum(slope, "y")
    high = lax.reduce_precision(slope, 8, 7)
    pair = jnp.concatenate([high.reshape(16, 128), (slope - high).reshape(16, 128)], 0).astype(BF16)
    low = spread(jnp.concatenate([low, pair], 0), REPLICA)
    act_add = swap(act_send)

    slope = jnp.sum(low[:, 40:56].astype(F32) + low[:, 56:].astype(F32), axis=0).reshape(1, half)
    mag_mine = slope / norm
    coeff = -mag_mine * size / (norm * norm)
    in_sum = low[:, 32:40].reshape(512, 64).astype(F32) + finish(at, w_own, w_peer, adapter_out, coeff)
    out_mine = low[:, :32].reshape(64, half).astype(F32) + q_half * coeff
    last = swap(jnp.concatenate([out_mine, in_sum[256:].reshape(8, half), mag_mine], 0))
    grad_in = in_sum[:256] + last[64:72].reshape(256, 64)
    join = lambda a, b: jnp.where(core == 0, jnp.concatenate([a, b], 1), jnp.concatenate([b, a], 1))
    grad_out = join(out_mine, last[:64])
    grad_mag = join(mag_mine, last[72:]).reshape(2 * half)
    grad_act = (act_own + act_add.astype(F32)).astype(BF16)
    return (output, grad_act, grad_in, grad_out, grad_mag)


def solution(mesh):
    grid = Mesh(mesh.devices.reshape(8, 4, 8, 2), ("z", "x", "y", "core"))
    every = ("z", "x", "y", "core")
    in_specs = (P(REPLICA, TENSOR), P(TENSOR, None), P(TENSOR, None), P(), P(), P(every, None))
    out_specs = (P(every, None), P(REPLICA, TENSOR), P(TENSOR, None), P(), P())
    return jax.shard_map(program, mesh=grid, in_specs=in_specs, out_specs=out_specs, check_vma=False)
```

time: 471 us -> 175 us (0.37)
  the two profiles are of different devices: /device:TPU:16 before, /device:TPU:1 now
where the time goes in v1:
time: 175 us; the launch traced here: 174 us
  starting transfers between devices  89.7 us (51%)
  Pallas kernels  23.7 us (14%)
  blocking collectives  16.2 us (9%)
  local copies, waits for them, and re-layouts  15.5 us (9%)
  waiting for transfers between devices  14.9 us (9%)
  other arithmetic  11.3 us (6%)
    ppermute x7, starting transfers between devices, swap(): return lax.ppermute(value, 'core', [(0, 1), (1, 0)])  33.9 us
    all_to_all x5, starting transfers between devices, exchange(): return lax.all_to_all(value, axes, 0, 0)  31.6 us
    ppermute x8, starting transfers between devices, shift(): return lax.ppermute(value, TENSOR, hops)  24.2 us
    psum x1, blocking collectives, program(): slope = lax.psum(slope, 'y')  16.2 us
    all_to_all x5, waiting for transfers between devices, exchange(): return lax.all_to_all(value, axes, 0, 0)  11.3 us
    pallas_call x1, Pallas kernels, backward(): pl.pallas_call(backward_kernel, out_shape=(jax.ShapeDtypeStruct((tokens,...  9.01 us
    pallas_call x1, Pallas kernels, forward(): pl.pallas_call(forward_kernel, out_shape=tuple((jax.ShapeDtypeStruct((r,...  6.17 us
    pallas_call x1, Pallas kernels, merge(): pl.pallas_call(merge_kernel, out_shape=(jax.ShapeDtypeStruct((rows, cols)...  4.74 us
  transfers between devices with their start and end apart: 20, of which 7 were waited for; matrix products, arithmetic and copies ran while one was open for 11% of the time, Pallas kernels for 11%

profile of v1, /device:TPU:1, one launch (start us, length us, event | category | flops | bytes accessed | tf_op | source)
XLA Modules:
  0.0 173.9 jit_solution(1055911905289639498)
XLA Ops:
  0.6 0.9 reduce-precision_convert_fusion
  1.5 0.8 copy.17.wide_ref
  2.3 1.2 fusion
  3.4 0.7 slice_add_fusion.1.zt
  4.1 0.6 pad_maximum_fusion.8.pick_ref
  4.8 4.7 %merge.1 = (bf16[256,4096]{1,0:T(8,128)(2,1)}, f32[16,24,128]{2,1,0:T(8,128)}) custom-call(bf16[256,4096]{1,0:T(8,128)(2,1)} %base_ref.1, bf16[256,256]{1,0:T(8,128)(2,1)} %copy.17.wide_ref, bf16[16,256]{1,0:T(8,128)(2,1)} %pad_maximum_fusion.8.pick_ref, f32[64,4096]{1,0:T(8,128)} %a_ref.3, f32[64,512]{1,0:T(8,128)} %slice_add_fusion.1.zt), custom_call_target="tpu_custom_call" | custom-call | flops 1400000000 | bytes 7000000 | tf_op jit(solution)/shard_map/merge/pallas_call | solution.py:54
  9.5 8.9 %collective-permute-start.1 = (bf16[256,4096]{1,0:T(8,128)(2,1)}, bf16[256,4096]{1,0:T(8,128)(2,1)S(1)}, u32[]{:S(2)}, u32[]{:S(2)}) collective-permute-start(bf16[256,4096]{1,0:T(8,128)(2,1)} %get-tuple-element.19.wa_ref.wo_ref), channel_id=1, source_target_pairs={{0,1},{1,0},{2,3},{3,2},{4,5},{5,4},{6,7},{7,6},{8,9},{9,8},{10,11... | collective-permute-start | bytes 6291464 | tf_op jit(solution)/shard_map/ppermute | solution.py:263
  18.4 3.4 %all-to-all-start = ((f32[16,24,128]{2,1,0:T(8,128)}), f32[16,24,128]{2,1,0:T(8,128)S(1)}, u32[]{:S(2)}, u32[]{:S(2)}) async-start(f32[16,24,128]{2,1,0:T(8,128)} %get-tuple-element.25), calls=%async_computation | async-start | bytes 393216 | tf_op jit(solution)/shard_map/all_to_all | solution.py:269
  21.8 2.0 %collective-permute-start.7 = (bf16[32,4096]{1,0:T(8,128)(2,1)S(1)}, bf16[32,4096]{1,0:T(8,128)(2,1)S(1)}, u32[]{:S(2)}, u32[]{:S(2)}) collective-permute-start(bf16[32,4096]{1,0:T(8,128)(2,1)S(1)} %copy-done.9), channel_id=1, source_target_pairs={{0,1},{1,0},{2,3},{3,2},{4,5},{5,4},{6,7},{7,6},{8,9},{9,8},{10,11... | collective-permute-start | bytes 786440 | tf_op jit(solution)/shard_map/ppermute | solution.py:263
  23.9 0.7 constant_dynamic-update-slice_fusion.1
  24.6 0.7 collective-permute-done.7
  25.3 0.7 constant_dynamic-update-slice_fusion.block_ref
  26.0 4.6 %collective-permute-start.8 = (bf16[64,4096]{1,0:T(8,128)(2,1)}, bf16[64,4096]{1,0:T(8,128)(2,1)}, u32[]{:S(2)}, u32[]{:S(2)}) collective-permute-start(bf16[64,4096]{1,0:T(8,128)(2,1)} %constant_dynamic-update-slice_fusion.block_ref), channel_id=1, source_target_pairs={{0,2},{2,4},{4,6},{6,8},{8,10},{10,12},{12,14},{14,0},{1,15},{3,1}... | collective-permute-start | bytes 1572872 | tf_op jit(solution)/shard_map/ppermute | solution.py:266
  30.6 1.4 all-to-all-done
  32.0 0.7 broadcast_in_dim.13
  32.7 3.8 %all-to-all-start.1 = ((f32[16,24,128]{2,1,0:T(8,128)}), f32[16,24,128]{2,1,0:T(8,128)S(1)}, u32[]{:S(2)}, u32[]{:S(2)}) async-start(f32[16,24,128]{2,1,0:T(8,128)} %broadcast_in_dim.13), calls=%async_computation.1 | async-start | bytes 393216 | tf_op jit(solution)/shard_map/all_to_all | solution.py:269
  36.5 0.5 collective-permute-done.8.hop1_ref
  37.0 5.0 %collective-permute-start.9 = (bf16[64,4096]{1,0:T(8,128)(2,1)}, bf16[64,4096]{1,0:T(8,128)(2,1)}, u32[]{:S(2)}, u32[]{:S(2)}) collective-permute-start(bf16[64,4096]{1,0:T(8,128)(2,1)} %collective-permute-done.8.hop1_ref), channel_id=1, source_target_pairs={{0,2},{2,4},{4,6},{6,8},{8,10},{10,12},{12,14},{14,0},{1,15},{3,1}... | collective-permute-start | bytes 1572872 | tf_op jit(solution)/shard_map/ppermute | solution.py:266
  42.0 0.1 copy.16
  42.2 1.9 %collective-permute-start = (bf16[512,256]{0,1:T(8,128)(2,1)S(1)}, bf16[512,256]{0,1:T(8,128)(2,1)S(1)}, u32[]{:S(2)}, u32[]{:S(2)}) collective-permute-start(bf16[512,256]{0,1:T(8,128)(2,1)S(1)} %copy.16), channel_id=1, source_target_pairs={{0,1},{1,0},{2,3},{3,2},{4,5},{5,4},{6,7},{7,6},{8,9},{9,8},{10,11... | collective-permute-start | bytes 786440 | tf_op jit(solution)/shard_map/ppermute | solution.py:263
  44.1 2.2 %all-to-all-done.1.second_ref = f32[16,24,128]{2,1,0:T(8,128)S(1)} async-done(((f32[16,24,128]{2,1,0:T(8,128)}), f32[16,24,128]{2,1,0:T(8,128)S(1)}, u32[]{:S(2)}, u32[]{:S(2)}) %all-to-all-start.1) | async-done | bytes 196640 | tf_op jit(solution)/shard_map/all_to_all | solution.py:269
  46.4 0.7 broadcast_in_dim.14
  47.1 11.4 %all-to-all-start.2 = ((bf16[32,32,128]{2,1,0:T(8,128)(2,1)}), bf16[32,32,128]{2,1,0:T(8,128)(2,1)S(1)}, u32[]{:S(2)}, u32[]{:S(2)}) async-start(bf16[32,32,128]{2,1,0:T(8,128)(2,1)} %broadcast_in_dim.14), calls=%async_computation.2 | async-start | bytes 524288 | tf_op jit(solution)/shard_map/all_to_all | solution.py:269
  58.5 0.6 stack.85.at_ref
  59.2 0.8 copy.18.b_ref
  60.1 0.6 div.11
  60.7 1.9 %collective-permute-start.10 = (bf16[64,4096]{1,0:T(8,128)(2,1)}, bf16[64,4096]{1,0:T(8,128)(2,1)}, u32[]{:S(2)}, u32[]{:S(2)}) collective-permute-start(bf16[64,4096]{1,0:T(8,128)(2,1)} %collective-permute-done.9.hop2_ref), channel_id=1, source_target_pairs={{0,2},{2,4},{4,6},{6,8},{8,10},{10,12},{12,14},{14,0},{1,15},{3,1}... | collective-permute-start | bytes 1572872 | tf_op jit(solution)/shard_map/ppermute | solution.py:266
  62.6 1.0 constant_dynamic-slice_fusion.2
  63.6 7.7 %all-to-all-done.2 = bf16[32,32,128]{2,1,0:T(8,128)(2,1)S(1)} async-done(((bf16[32,32,128]{2,1,0:T(8,128)(2,1)}), bf16[32,32,128]{2,1,0:T(8,128)(2,1)S(1)}, u32[]{:S(2)}, u32[]{:S(2)}) %all-to-all-start.2) | async-done | bytes 262176 | tf_op jit(solution)/shard_map/all_to_all | solution.py:269
  71.3 0.1 reshape.102
  71.5 1.0 constant_dynamic-slice_fusion.1
  72.5 1.3 copy-done
  73.8 6.2 %forward.1 = (bf16[32,4096]{1,0:T(8,128)(2,1)}, f32[64,4096]{1,0:T(8,128)}, f32[64,4096]{1,0:T(8,128)}, f32[64,4096]{1,0:T(8,128)}, f32[32,4096]{1,0:T(8,128)}) custom-call(s32[25]{0:T(128)} %stack.85.at_ref, bf16[512,256]{1,0:T(8,128)(2,1)} %a_ref.2, bf16[512,256]{1,0:T(8,128)(2,1)} %copy.18.b_ref, bf16[256,4096]{1,0:T(8,128)(2,1)} %get-tuple-element.19.wa_ref.wo_ref, ...), custom_call_target="tpu_custom_call" | custom-call | flops 1073741824 | bytes 5000000 | tf_op jit(solution)/shard_map/forward/pallas_call | solution.py:103
  80.0 2.0 %collective-permute-start.2 = (bf16[32,4096]{1,0:T(8,128)(2,1)}, bf16[32,4096]{1,0:T(8,128)(2,1)S(1)}, u32[]{:S(2)}, u32[]{:S(2)}) collective-permute-start(bf16[32,4096]{1,0:T(8,128)(2,1)} %get-tuple-element.24), channel_id=1, source_target_pairs={{0,2},{2,4},{4,6},{6,8},{8,10},{10,12},{12,14},{14,0},{1,15},{3,1}... | collective-permute-start | bytes 786440 | tf_op jit(solution)/shard_map/ppermute | solution.py:266
  82.0 1.1 constant_dynamic-slice_fusion
  83.1 2.4 %collective-permute-start.11 = (bf16[64,2048]{1,0:T(8,128)(2,1)S(1)}, bf16[64,2048]{1,0:T(8,128)(2,1)S(1)}, u32[]{:S(2)}, u32[]{:S(2)}) collective-permute-start(bf16[64,2048]{1,0:T(8,128)(2,1)S(1)} %get-tuple-element.48), channel_id=1, source_target_pairs={{0,2},{2,4},{4,6},{6,8},{8,10},{10,12},{12,14},{14,0},{1,15},{3,1}... | collective-permute-start | bytes 786440 | tf_op jit(solution)/shard_map/ppermute | solution.py:266
  85.6 4.2 %collective-permute-start.12 = (bf16[192,2048]{1,0:T(8,128)(2,1)S(1)}, bf16[192,2048]{1,0:T(8,128)(2,1)S(1)}, u32[]{:S(2)}, u32[]{:S(2)}) collective-permute-start(bf16[192,2048]{1,0:T(8,128)(2,1)S(1)} %pad_maximum_fusion), channel_id=1, source_target_pairs={{0,1},{1,0},{2,3},{3,2},{4,5},{5,4},{6,7},{7,6},{8,9},{9,8},{10,11... | collective-permute-start | bytes 2359304 | tf_op jit(solution)/shard_map/ppermute | solution.py:263
  89.9 3.8 %collective-permute-start.3 = (bf16[64,4096]{1,0:T(8,128)(2,1)S(1)}, bf16[64,4096]{1,0:T(8,128)(2,1)S(1)}, u32[]{:S(2)}, u32[]{:S(2)}) collective-permute-start(bf16[64,4096]{1,0:T(8,128)(2,1)S(1)} %pad_maximum_fusion.2), channel_id=1, source_target_pairs={{0,2},{2,4},{4,6},{6,8},{8,10},{10,12},{12,14},{14,0},{1,15},{3,1}... | collective-permute-start | bytes 1572872 | tf_op jit(solution)/shard_map/ppermute | solution.py:266
  93.8 0.9 copy-done.17
  94.7 9.0 %backward.1 = (f32[512,256]{1,0:T(8,128)}, bf16[512,256]{1,0:T(8,128)(2,1)}, bf16[512,64]{1,0:T(8,128)(2,1)}, f32[1,2048]{1,0:T(1,128)}, bf16[64,2048]{1,0:T(8,128)(2,1)}) custom-call(s32[25]{0:T(128)} %stack.85.at_ref, bf16[64,4096]{1,0:T(8,128)(2,1)} %constant_dynamic-update-slice_fusion.block_ref, bf16[64,4096]{1,0:T(8,128)(2,1)} %collective-permute-done.8.hop1_ref, ...), custom_call_target="tpu_custom_call" | custom-call | flops 5000000000 | bytes 8000000 | tf_op jit(solution)/shard_map/backward/pallas_call | solution.py:177
  103.8 1.1 reshape.96
  104.9 1.1 reshape.95
  106.0 0.8 pad_maximum_fusion.3
  106.7 3.9 %all-to-all-start.3 = ((bf16[32,40,128]{2,1,0:T(8,128)(2,1)}), bf16[32,40,128]{2,1,0:T(8,128)(2,1)S(1)}, u32[]{:S(2)}, u32[]{:S(2)}) async-start(bf16[32,40,128]{2,1,0:T(8,128)(2,1)} %pad_maximum_fusion.3), calls=%async_computation.3 | async-start | bytes 655360 | tf_op jit(solution)/shard_map/all_to_all | solution.py:269
  110.6 0.9 add_convert_fusion.1
  111.5 2.4 %collective-permute-start.4 = (bf16[64,4096]{1,0:T(8,128)(2,1)}, bf16[64,4096]{1,0:T(8,128)(2,1)}, u32[]{:S(2)}, u32[]{:S(2)}) collective-permute-start(bf16[64,4096]{1,0:T(8,128)(2,1)} %add_convert_fusion.1), channel_id=1, source_target_pairs={{0,2},{2,4},{4,6},{6,8},{8,10},{10,12},{12,14},{14,0},{1,15},{3,1}... | collective-permute-start | bytes 1572872 | tf_op jit(solution)/shard_map/ppermute | solution.py:266
  114.0 16.2 %psum.7 = f32[1,2048]{1,0:T(1,128)S(1)} all-reduce(f32[1,2048]{1,0:T(1,128)S(1)} %copy-done.16), channel_id=1, replica_groups=mesh['z'=8,'x'=4,'y'=8,'core'=2] {'y'}, use_global_device_ids=true, to_apply=%region_2.0 | all-reduce | flops 2048 | bytes 16384 | tf_op jit(solution)/shard_map/psum | solution.py:338
  130.3 0.9 broadcast_in_dim.15
  131.2 9.2 %all-to-all-start.4 = ((bf16[32,72,128]{2,1,0:T(8,128)(2,1)}), bf16[32,72,128]{2,1,0:T(8,128)(2,1)S(1)}, u32[]{:S(2)}, u32[]{:S(2)}) async-start(bf16[32,72,128]{2,1,0:T(8,128)(2,1)} %broadcast_in_dim.15), calls=%async_computation.4 | async-start | bytes 1179648 | tf_op jit(solution)/shard_map/all_to_all | solution.py:269
  140.4 1.9 %add_convert_fusion = bf16[64,4096]{1,0:T(8,128)(2,1)} fusion(f32[64,4096]{1,0:T(8,128)S(1)} %copy-done.2, bf16[64,4096]{1,0:T(8,128)(2,1)} %collective-permute-done.4), kind=kLoop, calls=%fused_computation.1 | loop fusion | flops 786432 | bytes 2097152 | tf_op jit(solution)/shard_map/convert_element_type | solution.py:327
  142.3 2.0 %collective-permute-start.5 = (bf16[64,4096]{1,0:T(8,128)(2,1)}, bf16[64,4096]{1,0:T(8,128)(2,1)S(1)}, u32[]{:S(2)}, u32[]{:S(2)}) collective-permute-start(bf16[64,4096]{1,0:T(8,128)(2,1)} %add_convert_fusion), channel_id=1, source_target_pairs={{0,2},{2,4},{4,6},{6,8},{8,10},{10,12},{12,14},{14,0},{1,15},{3,1}... | collective-permute-start | bytes 1572872 | tf_op jit(solution)/shard_map/ppermute | solution.py:266
  144.3 8.6 %collective-permute-start.13 = (bf16[512,256]{1,0:T(8,128)(2,1)S(1)}, bf16[512,256]{1,0:T(8,128)(2,1)S(1)}, u32[]{:S(2)}, u32[]{:S(2)}) collective-permute-start(bf16[512,256]{1,0:T(8,128)(2,1)S(1)} %copy-done.18), channel_id=1, source_target_pairs={{0,1},{1,0},{2,3},{3,2},{4,5},{5,4},{6,7},{7,6},{8,9},{9,8},{10,11... | collective-permute-start | bytes 786440 | tf_op jit(solution)/shard_map/ppermute | solution.py:263
  152.9 1.1 collective-permute-done.13
  154.1 0.8 add_convert_fusion.2
  154.9 6.4 %collective-permute-start.6 = (bf16[32,4096]{1,0:T(8,128)(2,1)S(1)}, bf16[32,4096]{1,0:T(8,128)(2,1)S(1)}, u32[]{:S(2)}, u32[]{:S(2)}) collective-permute-start(bf16[32,4096]{1,0:T(8,128)(2,1)S(1)} %slice.74), channel_id=1, source_target_pairs={{0,1},{1,0},{2,3},{3,2},{4,5},{5,4},{6,7},{7,6},{8,9},{9,8},{10,11... | collective-permute-start | bytes 786440 | tf_op jit(solution)/shard_map/ppermute | solution.py:263
  161.6 0.5 copy-done.13
  162.1 3.8 %finish.1 = f32[512,64]{1,0:T(8,128)} custom-call(s32[25]{0:T(128)} %stack.85.at_ref, bf16[256,4096]{1,0:T(8,128)(2,1)} %get-tuple-element.19.wa_ref.wo_ref, bf16[256,4096]{1,0:T(8,128)(2,1)} %copy-done, f32[64,4096]{1,0:T(8,128)} %a_ref.3, f32[1,2048]{1,0:T(1,128)} %copy-done.13), custom_call_target="tpu_custom_call" | custom-call | flops 600000000 | bytes 3000000 | tf_op jit(solution)/shard_map/finish/pallas_call | solution.py:233
  166.0 1.0 add.227
  167.3 1.9 %collective-permute-start.14 = (f32[73,2048]{1,0:T(8,128)S(1)}, f32[73,2048]{1,0:T(8,128)S(1)}, u32[]{:S(2)}, u32[]{:S(2)}) collective-permute-start(f32[73,2048]{1,0:T(8,128)S(1)} %pad_maximum_fusion.1), channel_id=1, source_target_pairs={{0,1},{1,0},{2,3},{3,2},{4,5},{5,4},{6,7},{7,6},{8,9},{9,8},{10,11... | collective-permute-start | bytes 1794056 | tf_op jit(solution)/shard_map/ppermute | solution.py:263
  169.2 0.8 multiply_convert_fusion
  170.0 1.2 collective-permute-done.14
  171.4 0.7 copy.21
  172.1 1.1 maximum_select_fusion
  173.2 0.6 maximum_select_fusion.1
  (84 shorter events, 1.2 us)
Async XLA Ops:
  4.8 17.1 %copy-start.9 = (bf16[32,4096]{1,0:T(8,128)(2,1)S(1)}, bf16[32,4096]{1,0:T(8,128)(2,1)}, u32[]{:S(2)}) copy-start(bf16[32,4096]{1,0:T(8,128)(2,1)} %param.11) | copy-start | bytes 786436
  9.5 32.5 %copy-start.1 = (bf16[512,256]{1,0:T(8,128)(2,1)S(1)}, bf16[512,256]{1,0:T(8,128)(2,1)}, u32[]{:S(2)}) copy-start(bf16[512,256]{1,0:T(8,128)(2,1)} %a_ref.2) | copy-start | bytes 786436
  9.5 62.9 %collective-permute-start.1 = (bf16[256,4096]{1,0:T(8,128)(2,1)}, bf16[256,4096]{1,0:T(8,128)(2,1)S(1)}, u32[]{:S(2)}, u32[]{:S(2)}) collective-permute-start(bf16[256,4096]{1,0:T(8,128)(2,1)} %get-tuple-element.19.wa_ref.wo_ref), channel_id=1, source_target_pairs={{0,1},{1,0},{2,3},{3,2},{4,5},{5,4},{6,7},{7,6},{8,9},{9,8},{10,11... | collective-permute-start | bytes 6291464 | tf_op jit(solution)/shard_map/ppermute | solution.py:263
  18.4 13.6 %all-to-all-start = ((f32[16,24,128]{2,1,0:T(8,128)}), f32[16,24,128]{2,1,0:T(8,128)S(1)}, u32[]{:S(2)}, u32[]{:S(2)}) async-start(f32[16,24,128]{2,1,0:T(8,128)} %get-tuple-element.25), calls=%async_computation | async-start | bytes 393216 | tf_op jit(solution)/shard_map/all_to_all | solution.py:269
  21.8 3.4 %collective-permute-start.7 = (bf16[32,4096]{1,0:T(8,128)(2,1)S(1)}, bf16[32,4096]{1,0:T(8,128)(2,1)S(1)}, u32[]{:S(2)}, u32[]{:S(2)}) collective-permute-start(bf16[32,4096]{1,0:T(8,128)(2,1)S(1)} %copy-done.9), channel_id=1, source_target_pairs={{0,1},{1,0},{2,3},{3,2},{4,5},{5,4},{6,7},{7,6},{8,9},{9,8},{10,11... | collective-permute-start | bytes 786440 | tf_op jit(solution)/shard_map/ppermute | solution.py:263
  26.0 34.1 %copy-start.15 = (f32[4096]{0:T(1024)S(1)}, f32[4096]{0:T(1024)}, u32[]{:S(2)}) copy-start(f32[4096]{0:T(1024)} %param.10) | copy-start | bytes 49156
  26.0 11.0 %collective-permute-start.8 = (bf16[64,4096]{1,0:T(8,128)(2,1)}, bf16[64,4096]{1,0:T(8,128)(2,1)}, u32[]{:S(2)}, u32[]{:S(2)}) collective-permute-start(bf16[64,4096]{1,0:T(8,128)(2,1)} %constant_dynamic-update-slice_fusion.block_ref), channel_id=1, source_target_pairs={{0,2},{2,4},{4,6},{6,8},{8,10},{10,12},{12,14},{14,0},{1,15},{3,1}... | collective-permute-start | bytes 1572872 | tf_op jit(solution)/shard_map/ppermute | solution.py:266
  32.7 13.6 %all-to-all-start.1 = ((f32[16,24,128]{2,1,0:T(8,128)}), f32[16,24,128]{2,1,0:T(8,128)S(1)}, u32[]{:S(2)}, u32[]{:S(2)}) async-start(f32[16,24,128]{2,1,0:T(8,128)} %broadcast_in_dim.13), calls=%async_computation.1 | async-start | bytes 393216 | tf_op jit(solution)/shard_map/all_to_all | solution.py:269
  37.0 23.7 %collective-permute-start.9 = (bf16[64,4096]{1,0:T(8,128)(2,1)}, bf16[64,4096]{1,0:T(8,128)(2,1)}, u32[]{:S(2)}, u32[]{:S(2)}) collective-permute-start(bf16[64,4096]{1,0:T(8,128)(2,1)} %collective-permute-done.8.hop1_ref), channel_id=1, source_target_pairs={{0,2},{2,4},{4,6},{6,8},{8,10},{10,12},{12,14},{14,0},{1,15},{3,1}... | collective-permute-start | bytes 1572872 | tf_op jit(solution)/shard_map/ppermute | solution.py:266
  42.2 21.4 %copy-start.10 = (bf16[512,256]{0,1:T(8,128)(2,1)}, bf16[512,256]{0,1:T(8,128)(2,1)S(1)}, u32[]{:S(2)}) copy-start(bf16[512,256]{0,1:T(8,128)(2,1)S(1)} %copy.16) | copy-start | bytes 786436
  42.2 17.0 %collective-permute-start = (bf16[512,256]{0,1:T(8,128)(2,1)S(1)}, bf16[512,256]{0,1:T(8,128)(2,1)S(1)}, u32[]{:S(2)}, u32[]{:S(2)}) collective-permute-start(bf16[512,256]{0,1:T(8,128)(2,1)S(1)} %copy.16), channel_id=1, source_target_pairs={{0,1},{1,0},{2,3},{3,2},{4,5},{5,4},{6,7},{7,6},{8,9},{9,8},{10,11... | collective-permute-start | bytes 786440 | tf_op jit(solution)/shard_map/ppermute | solution.py:263
  46.3 14.4 %copy-start.12 = (f32[16,24,128]{2,1,0:T(8,128)}, f32[16,24,128]{2,1,0:T(8,128)S(1)}, u32[]{:S(2)}) copy-start(f32[16,24,128]{2,1,0:T(8,128)S(1)} %all-to-all-done.1.second_ref) | copy-start | bytes 589828
  47.1 24.2 %all-to-all-start.2 = ((bf16[32,32,128]{2,1,0:T(8,128)(2,1)}), bf16[32,32,128]{2,1,0:T(8,128)(2,1)S(1)}, u32[]{:S(2)}, u32[]{:S(2)}) async-start(bf16[32,32,128]{2,1,0:T(8,128)(2,1)} %broadcast_in_dim.14), calls=%async_computation.2 | async-start | bytes 524288 | tf_op jit(solution)/shard_map/all_to_all | solution.py:269
  59.2 4.4 %copy-start.11 = (bf16[512,256]{0,1:T(8,128)(2,1)}, bf16[512,256]{0,1:T(8,128)(2,1)S(1)}, u32[]{:S(2)}) copy-start(bf16[512,256]{0,1:T(8,128)(2,1)S(1)} %collective-permute-done) | copy-start | bytes 786436
  60.7 21.3 %collective-permute-start.10 = (bf16[64,4096]{1,0:T(8,128)(2,1)}, bf16[64,4096]{1,0:T(8,128)(2,1)}, u32[]{:S(2)}, u32[]{:S(2)}) collective-permute-start(bf16[64,4096]{1,0:T(8,128)(2,1)} %collective-permute-done.9.hop2_ref), channel_id=1, source_target_pairs={{0,2},{2,4},{4,6},{6,8},{8,10},{10,12},{12,14},{14,0},{1,15},{3,1}... | collective-permute-start | bytes 1572872 | tf_op jit(solution)/shard_map/ppermute | solution.py:266
  72.4 1.3 copy-start
  80.0 9.8 %copy-start.4 = (f32[64,4096]{1,0:T(8,128)S(1)}, f32[64,4096]{1,0:T(8,128)}, u32[]{:S(2)}) copy-start(f32[64,4096]{1,0:T(8,128)} %get-tuple-element.23) | copy-start | bytes 3145732
  80.0 9.9 %collective-permute-start.2 = (bf16[32,4096]{1,0:T(8,128)(2,1)}, bf16[32,4096]{1,0:T(8,128)(2,1)S(1)}, u32[]{:S(2)}, u32[]{:S(2)}) collective-permute-start(bf16[32,4096]{1,0:T(8,128)(2,1)} %get-tuple-element.24), channel_id=1, source_target_pairs={{0,2},{2,4},{4,6},{6,8},{8,10},{10,12},{12,14},{14,0},{1,15},{3,1}... | collective-permute-start | bytes 786440 | tf_op jit(solution)/shard_map/ppermute | solution.py:266
  83.1 10.7 %collective-permute-start.11 = (bf16[64,2048]{1,0:T(8,128)(2,1)S(1)}, bf16[64,2048]{1,0:T(8,128)(2,1)S(1)}, u32[]{:S(2)}, u32[]{:S(2)}) collective-permute-start(bf16[64,2048]{1,0:T(8,128)(2,1)S(1)} %get-tuple-element.48), channel_id=1, source_target_pairs={{0,2},{2,4},{4,6},{6,8},{8,10},{10,12},{12,14},{14,0},{1,15},{3,1}... | collective-permute-start | bytes 786440 | tf_op jit(solution)/shard_map/ppermute | solution.py:266
  85.6 8.2 %collective-permute-start.12 = (bf16[192,2048]{1,0:T(8,128)(2,1)S(1)}, bf16[192,2048]{1,0:T(8,128)(2,1)S(1)}, u32[]{:S(2)}, u32[]{:S(2)}) collective-permute-start(bf16[192,2048]{1,0:T(8,128)(2,1)S(1)} %pad_maximum_fusion), channel_id=1, source_target_pairs={{0,1},{1,0},{2,3},{3,2},{4,5},{5,4},{6,7},{7,6},{8,9},{9,8},{10,11... | collective-permute-start | bytes 2359304 | tf_op jit(solution)/shard_map/ppermute | solution.py:263
  89.9 20.7 %collective-permute-start.3 = (bf16[64,4096]{1,0:T(8,128)(2,1)S(1)}, bf16[64,4096]{1,0:T(8,128)(2,1)S(1)}, u32[]{:S(2)}, u32[]{:S(2)}) collective-permute-start(bf16[64,4096]{1,0:T(8,128)(2,1)S(1)} %pad_maximum_fusion.2), channel_id=1, source_target_pairs={{0,2},{2,4},{4,6},{6,8},{8,10},{10,12},{12,14},{14,0},{1,15},{3,1}... | collective-permute-start | bytes 1572872 | tf_op jit(solution)/shard_map/ppermute | solution.py:266
  93.8 1.0 copy-start.19
  93.8 0.9 copy-start.17
  103.8 6.9 %copy-start.3 = (f32[64,4096]{1,0:T(8,128)S(1)}, f32[64,4096]{1,0:T(8,128)}, u32[]{:S(2)}) copy-start(f32[64,4096]{1,0:T(8,128)} %get-tuple-element.22) | copy-start | bytes 3145732
  106.0 8.0 %copy-start.16 = (f32[1,2048]{1,0:T(1,128)S(1)}, f32[1,2048]{1,0:T(1,128)}, u32[]{:S(2)}) copy-start(f32[1,2048]{1,0:T(1,128)} %get-tuple-element.31) | copy-start | bytes 24580
  106.7 23.5 %all-to-all-start.3 = ((bf16[32,40,128]{2,1,0:T(8,128)(2,1)}), bf16[32,40,128]{2,1,0:T(8,128)(2,1)S(1)}, u32[]{:S(2)}, u32[]{:S(2)}) async-start(bf16[32,40,128]{2,1,0:T(8,128)(2,1)} %pad_maximum_fusion.3), calls=%async_computation.3 | async-start | bytes 655360 | tf_op jit(solution)/shard_map/all_to_all | solution.py:269
  111.5 28.8 %copy-start.2 = (f32[64,4096]{1,0:T(8,128)S(1)}, f32[64,4096]{1,0:T(8,128)}, u32[]{:S(2)}) copy-start(f32[64,4096]{1,0:T(8,128)} %get-tuple-element.21) | copy-start | bytes 3145732
  111.5 28.8 %collective-permute-start.4 = (bf16[64,4096]{1,0:T(8,128)(2,1)}, bf16[64,4096]{1,0:T(8,128)(2,1)}, u32[]{:S(2)}, u32[]{:S(2)}) collective-permute-start(bf16[64,4096]{1,0:T(8,128)(2,1)} %add_convert_fusion.1), channel_id=1, source_target_pairs={{0,2},{2,4},{4,6},{6,8},{8,10},{10,12},{12,14},{14,0},{1,15},{3,1}... | collective-permute-start | bytes 1572872 | tf_op jit(solution)/shard_map/ppermute | solution.py:266
  131.2 13.1 %copy-start.18 = (bf16[512,256]{1,0:T(8,128)(2,1)S(1)}, bf16[512,256]{1,0:T(8,128)(2,1)}, u32[]{:S(2)}) copy-start(bf16[512,256]{1,0:T(8,128)(2,1)} %get-tuple-element.27) | copy-start | bytes 786436
  131.2 22.9 %copy-start.5 = (f32[512,256]{1,0:T(8,128)S(1)}, f32[512,256]{1,0:T(8,128)}, u32[]{:S(2)}) copy-start(f32[512,256]{1,0:T(8,128)} %get-tuple-element.26) | copy-start | bytes 1572868
  131.2 30.0 %all-to-all-start.4 = ((bf16[32,72,128]{2,1,0:T(8,128)(2,1)}), bf16[32,72,128]{2,1,0:T(8,128)(2,1)S(1)}, u32[]{:S(2)}, u32[]{:S(2)}) async-start(bf16[32,72,128]{2,1,0:T(8,128)(2,1)} %broadcast_in_dim.15), calls=%async_computation.4 | async-start | bytes 1179648 | tf_op jit(solution)/shard_map/all_to_all | solution.py:269
  142.3 12.5 %collective-permute-start.5 = (bf16[64,4096]{1,0:T(8,128)(2,1)}, bf16[64,4096]{1,0:T(8,128)(2,1)S(1)}, u32[]{:S(2)}, u32[]{:S(2)}) collective-permute-start(bf16[64,4096]{1,0:T(8,128)(2,1)} %add_convert_fusion), channel_id=1, source_target_pairs={{0,2},{2,4},{4,6},{6,8},{8,10},{10,12},{12,14},{14,0},{1,15},{3,1}... | collective-permute-start | bytes 1572872 | tf_op jit(solution)/shard_map/ppermute | solution.py:266
  144.3 9.8 %collective-permute-start.13 = (bf16[512,256]{1,0:T(8,128)(2,1)S(1)}, bf16[512,256]{1,0:T(8,128)(2,1)S(1)}, u32[]{:S(2)}, u32[]{:S(2)}) collective-permute-start(bf16[512,256]{1,0:T(8,128)(2,1)S(1)} %copy-done.18), channel_id=1, source_target_pairs={{0,1},{1,0},{2,3},{3,2},{4,5},{5,4},{6,7},{7,6},{8,9},{9,8},{10,11... | collective-permute-start | bytes 786440 | tf_op jit(solution)/shard_map/ppermute | solution.py:263
  154.8 6.6 %dynamic-slice-start = ((f32[4096]{0:T(1024)}, s32[]{:T(128)}), f32[2048]{0:T(1024)S(1)}, s32[]{:S(2)}) async-start(f32[4096]{0:T(1024)} %param.10, s32[]{:T(128)} %select_n.40), calls=%async_computation.5 | async-start | bytes 16896 | tf_op jit(solution)/shard_map/dynamic-slice
  154.8 6.4 %copy-start.6 = (bf16[64,4096]{1,0:T(8,128)(2,1)}, bf16[64,4096]{1,0:T(8,128)(2,1)S(1)}, u32[]{:S(2)}) copy-start(bf16[64,4096]{1,0:T(8,128)(2,1)S(1)} %collective-permute-done.5) | copy-start | bytes 1572868
  154.9 14.3 %collective-permute-start.6 = (bf16[32,4096]{1,0:T(8,128)(2,1)S(1)}, bf16[32,4096]{1,0:T(8,128)(2,1)S(1)}, u32[]{:S(2)}, u32[]{:S(2)}) collective-permute-start(bf16[32,4096]{1,0:T(8,128)(2,1)S(1)} %slice.74), channel_id=1, source_target_pairs={{0,1},{1,0},{2,3},{3,2},{4,5},{5,4},{6,7},{7,6},{8,9},{9,8},{10,11... | collective-permute-start | bytes 786440 | tf_op jit(solution)/shard_map/ppermute | solution.py:263
  161.5 0.6 copy-start.13
  165.9 3.3 %copy-start.7 = (bf16[64,4096]{1,0:T(8,128)(2,1)S(1)}, bf16[64,4096]{1,0:T(8,128)(2,1)}, u32[]{:S(2)}) copy-start(bf16[64,4096]{1,0:T(8,128)(2,1)} %copy-done.6) | copy-start | bytes 1572868
  165.9 3.3 %copy-start.8 = (f32[32,4096]{1,0:T(8,128)S(1)}, f32[32,4096]{1,0:T(8,128)}, u32[]{:S(2)}) copy-start(f32[32,4096]{1,0:T(8,128)} %get-tuple-element.20) | copy-start | bytes 1572868
  165.9 3.3 %copy-start.14 = (f32[4096]{0:T(1024)S(1)}, f32[4096]{0:T(1024)}, u32[]{:S(2)}) copy-start(f32[4096]{0:T(1024)} %div.11) | copy-start | bytes 49156
  167.3 4.0 %collective-permute-start.14 = (f32[73,2048]{1,0:T(8,128)S(1)}, f32[73,2048]{1,0:T(8,128)S(1)}, u32[]{:S(2)}, u32[]{:S(2)}) collective-permute-start(f32[73,2048]{1,0:T(8,128)S(1)} %pad_maximum_fusion.1), channel_id=1, source_target_pairs={{0,1},{1,0},{2,3},{3,2},{4,5},{5,4},{6,7},{7,6},{8,9},{9,8},{10,11... | collective-permute-start | bytes 1794056 | tf_op jit(solution)/shard_map/ppermute | solution.py:263

commit v2 on v1

v2 whole, which is shorter than its diff:
```python
import jax
import jax.numpy as jnp
from jax import lax
from jax.experimental import pallas as pl
from jax.experimental.pallas import tpu as pltpu
from jax.sharding import Mesh, PartitionSpec as P


epsilon = 1e-06
F32, BF16 = jnp.float32, jnp.bfloat16
REPLICA = ("z", "x")
TENSOR = ("y", "core")
TILE = 512


def split(value):
    high = value.astype(BF16)
    return high, (value - high.astype(F32)).astype(BF16)


def contract(left, right, dims):
    return lax.dot_general(left, right, ((dims[:1], dims[1:]), ((), ())), preferred_element_type=F32)


def merge_kernel(at_ref, base_ref, wide_ref, pick_ref, out_ref, zt_ref, low_ref, first_ref):
    step = pl.program_id(0)
    ah, al = split(out_ref[...])
    low = contract(wide_ref[...], jnp.concatenate([ah, al, ah, al], 0), (1, 0))
    merged = base_ref[...].astype(F32) + low
    squares = jnp.sum(merged * merged, axis=0, keepdims=True)
    low_ref[...] = merged.astype(BF16)
    ranks = zt_ref[pl.ds(pl.multiple_of(step * 16, 16), 16), :]
    for k in range(4):
        member = 4 * step + k
        for q in range(4):
            first_ref[member, 4 * q : 4 * q + 4, :] = ranks[4 * k : 4 * k + 4, 128 * q : 128 * q + 128]
        for r in range(2):
            first_ref[member, 16 + r : 17 + r, :] = squares[:, 256 * k + 128 * r : 256 * k + 128 * r + 128]
        first_ref[member, 22:24, :] = jnp.zeros((2, 128), F32)

    @pl.when(lax.rem(step, 2) == at_ref[0])
    def _():
        span = pl.ds(pl.multiple_of(at_ref[1] * 128, 128), 128)
        both = contract(pick_ref[...], low_ref[:, span], (1, 0))
        block = both[:32] + both[32:]
        for k in range(8):
            first_ref[2 * k + step // 2, 18:22, :] = block[4 * k : 4 * k + 4]


def merge(at, base, wide, pick, adapter_out, zt):
    rows, cols = base.shape
    tokens = zt.shape[1]
    steps = cols // 1024
    tile = lambda i, c: (0, i)
    whole = lambda i, c: (0, 0)
    return pl.pallas_call(
        merge_kernel,
        out_shape=(jax.ShapeDtypeStruct((rows, cols), BF16), jax.ShapeDtypeStruct((16, 24, 128), F32)),
        grid_spec=pltpu.PrefetchScalarGridSpec(
            num_scalar_prefetch=1,
            grid=(steps,),
            in_specs=[
                pl.BlockSpec((rows, 1024), tile),
                pl.BlockSpec((rows, 256), whole),
                pl.BlockSpec((64, rows), whole),
                pl.BlockSpec((64, 1024), tile),
                pl.BlockSpec((64, tokens), whole),
            ],
            out_specs=(
                pl.BlockSpec((rows, 1024), tile),
                pl.BlockSpec((16, 24, 128), lambda i, c: (0, 0, 0)),
            ),
        ),
        cost_estimate=pl.CostEstimate(flops=1400000000, bytes_accessed=7000000, transcendentals=0),
        name="merge",
    )(at, base, wide, pick, adapter_out, zt)


def forward_kernel(at_ref, a_ref, b_ref, wa_ref, wb_ref, r4_ref, r3_ref, r2_ref, r1_ref, r0_ref, acts):
    @pl.when(pl.program_id(0) == 0)
    def _():
        for k in range(8):
            rows = pl.ds(pl.multiple_of(at_ref[17 + k] * 32, 32), 32)
            acts[32 * k : 32 * k + 32, :256] = a_ref[rows, :]
            acts[32 * k : 32 * k + 32, 256:] = b_ref[rows, :]

    part = contract(acts[...], jnp.concatenate([wa_ref[...], wb_ref[...]], 0), (1, 0))
    r4_ref[...] = part[0:32].astype(BF16)
    r3_ref[...] = part[32:96]
    r2_ref[...] = part[96:160]
    r1_ref[...] = part[160:224]
    r0_ref[...] = part[224:256]


def forward(at, act_own, act_peer, w_own, w_peer):
    tokens, feats = act_own.shape
    cols = w_own.shape[1]
    whole = pl.BlockSpec((tokens, feats), lambda i, c: (0, 0))
    tile = lambda rows: pl.BlockSpec((rows, 1024), lambda i, c: (0, i))
    rows = (32, 64, 64, 64, 32)
    kinds = (BF16, F32, F32, F32, F32)
    return pl.pallas_call(
        forward_kernel,
        out_shape=tuple(jax.ShapeDtypeStruct((r, cols), k) for r, k in zip(rows, kinds)),
        grid_spec=pltpu.PrefetchScalarGridSpec(
            num_scalar_prefetch=1,
            grid=(cols // 1024,),
            in_specs=[whole, whole, tile(feats), tile(feats)],
            out_specs=tuple(tile(r) for r in rows),
            scratch_shapes=[pltpu.VMEM((256, 512), BF16)],
        ),
        cost_estimate=pl.CostEstimate(flops=2 * tokens * feats * cols, bytes_accessed=5000000, transcendentals=0),
        name="forward",
    )(at, act_own, act_peer, w_own, w_peer)


def slope_kernel(
    at_ref, block_ref, hop1_ref, hop2_ref, hop3_ref, hop4_ref, cross_ref, scale_ref, wo_ref, wp_ref, ato_ref, atp_ref,
    scaled_ref, slope_ref, cots,
):
    parts = [block_ref, hop1_ref, hop2_ref, hop3_ref, hop4_ref]
    parts = [(part, r) for part in parts for r in (0, 32)] + [(cross_ref, r) for r in range(0, 192, 32)]
    for k, (part, r) in enumerate(parts):
        cots[pl.ds(pl.multiple_of(at_ref[1 + k] * 32, 32), 32), :] = part[r : r + 32, :]
    cot = cots[...]
    slope = jnp.sum(contract(ato_ref[...], cot, (1, 0)) * wo_ref[...].astype(F32), axis=0, keepdims=True)
    slope = slope + jnp.sum(contract(atp_ref[...], cot, (1, 0)) * wp_ref[...].astype(F32), axis=0, keepdims=True)
    scaled_ref[...] = (cot.astype(F32) * scale_ref[...]).astype(BF16)
    for q in range(8):
        row = slope[:, 128 * q : 128 * q + 128]
        for k in range(8):
            slope_ref[k, q : q + 1, :] = row


def slopes(at, block, hops, hop4, crossed, scale, w_own, w_peer, at_own, at_peer):
    cols = hop4.shape[1]
    feats, tokens = at_own.shape
    steps = cols // 1024
    whole = lambda i, c: (0, 0)
    tile = lambda i, c: (0, i)
    side = lambda i, c: (0, c[0] * steps + i)
    return pl.pallas_call(
        slope_kernel,
        out_shape=(jax.ShapeDtypeStruct((tokens, cols), BF16), jax.ShapeDtypeStruct((8, 16, 128), F32)),
        grid_spec=pltpu.PrefetchScalarGridSpec(
            num_scalar_prefetch=1,
            grid=(steps,),
            in_specs=[pl.BlockSpec((64, 1024), side)] * 4
            + [
                pl.BlockSpec((64, 1024), tile),
                pl.BlockSpec((192, 1024), tile),
                pl.BlockSpec((1, 1024), side),
                pl.BlockSpec((feats, 1024), side),
                pl.BlockSpec((feats, 1024), side),
                pl.BlockSpec((feats, tokens), whole),
                pl.BlockSpec((feats, tokens), whole),
            ],
            out_specs=(pl.BlockSpec((tokens, 1024), tile), pl.BlockSpec((8, 8, 128), lambda i, c: (0, i, 0))),
            scratch_shapes=[pltpu.VMEM((tokens, 1024), BF16)],
        ),
        cost_estimate=pl.CostEstimate(flops=2200000000, bytes_accessed=8000000, transcendentals=0),
        name="slopes",
    )(at, block, *hops, hop4, crossed, scale, w_own, w_peer, at_own, at_peer)


def backward_kernel(
    at_ref, scaled_ref, wo_ref, wp_ref, ato_ref, atp_ref, second_ref, out_ref,
    gao_ref, gap_ref, low_ref, sum_own, sum_peer, sum_y, zt,
):
    step = pl.program_id(0)

    @pl.when(step == 0)
    def _():
        for m in range(16):
            for q in range(4):
                zt[4 * m : 4 * m + 4, 128 * q : 128 * q + 128] = second_ref[m, 4 * q : 4 * q + 4, :]

    scaled = scaled_ref[...]
    both = contract(jnp.concatenate(split(zt[...]), 0), scaled, (1, 0))
    p = (both[:64] + both[64:]).astype(BF16)
    for q in range(4):
        for r in range(2):
            low_ref[8 * step + 2 * q + r, 0:32, :] = p[32 * r : 32 * r + 32, 128 * q : 128 * q + 128]
    own = contract(scaled, wo_ref[...], (1, 1))
    peer = contract(scaled, wp_ref[...], (1, 1))
    y = contract(scaled, jnp.concatenate(split(out_ref[...]), 0), (1, 1))

    @pl.when(step == 0)
    def _():
        sum_own[...] = own
        sum_peer[...] = peer
        sum_y[...] = y

    @pl.when(step > 0)
    def _():
        sum_own[...] += own
        sum_peer[...] += peer
        sum_y[...] += y

    @pl.when(step == pl.num_programs(0) - 1)
    def _():
        gao_ref[...] = sum_own[...]
        gap_ref[...] = sum_peer[...].astype(BF16)
        pair = jnp.concatenate(split(sum_y[...]), 0)
        for k, ref in enumerate((ato_ref, atp_ref)):
            both = contract(jnp.concatenate([ref[...], ref[...]], 1), pair, (1, 0)).T
            both = (both[:64] + both[64:]).astype(BF16)
            for a in range(8):
                for q in range(2):
                    low_ref[4 * a + 2 * k + q, 32:40, :] = both[8 * a : 8 * a + 8, 128 * q : 128 * q + 128]


def backward(at, scaled, w_own, w_peer, at_own, at_peer, second, adapter_out):
    tokens, cols = scaled.shape
    feats = at_own.shape[0]
    steps = cols // TILE
    whole = lambda i, c: (0, 0)
    tile = lambda i, c: (0, i)
    side = lambda i, c: (0, c[0] * steps + i)
    return pl.pallas_call(
        backward_kernel,
        out_shape=(
            jax.ShapeDtypeStruct((tokens, feats), F32),
            jax.ShapeDtypeStruct((tokens, feats), BF16),
            jax.ShapeDtypeStruct((32, 40, 128), BF16),
        ),
        grid_spec=pltpu.PrefetchScalarGridSpec(
            num_scalar_prefetch=1,
            grid=(steps,),
            in_specs=[
                pl.BlockSpec((tokens, TILE), tile),
                pl.BlockSpec((feats, TILE), side),
                pl.BlockSpec((feats, TILE), side),
                pl.BlockSpec((feats, tokens), whole),
                pl.BlockSpec((feats, tokens), whole),
                pl.BlockSpec((16, 24, 128), lambda i, c: (0, 0, 0)),
                pl.BlockSpec((64, TILE), side),
            ],
            out_specs=(
                pl.BlockSpec((tokens, feats), whole),
                pl.BlockSpec((tokens, feats), whole),
                pl.BlockSpec((32, 40, 128), lambda i, c: (0, 0, 0)),
            ),
            scratch_shapes=[
                pltpu.VMEM((tokens, feats), F32),
                pltpu.VMEM((tokens, feats), F32),
                pltpu.VMEM((tokens, 128), F32),
                pltpu.VMEM((64, tokens), F32),
            ],
        ),
        cost_estimate=pl.CostEstimate(flops=3000000000, bytes_accessed=6000000, transcendentals=0),
        name="backward",
    )(at, scaled, w_own, w_peer, at_own, at_peer, second, adapter_out)


def combine_kernel(at_ref, got_ref, second_ref, norm_ref, size_ref, o_ref):
    total = jnp.sum(got_ref[...].astype(F32), axis=0)
    norm = norm_ref[...]
    mag = (total[40:41] + total[41:42]) / norm
    coeff = -mag * size_ref[...] / (norm * norm)
    q = jnp.concatenate([second_ref[2 * k + at_ref[0], 18:22, :] for k in range(8)], 0)
    high, low = split(mag)
    out = (total[0:32] + q * coeff).astype(BF16)
    o_ref[...] = jnp.broadcast_to(jnp.concatenate([out, total[32:40].astype(BF16), high, low], 0), o_ref.shape)


def combine(at, got, second, norm, size):
    column = pl.BlockSpec((1, 128), lambda i, c: (0, c[0] * 16 + c[1]))
    block = pl.BlockSpec(got.shape, lambda i, c: (0, 0, 0))
    return pl.pallas_call(
        combine_kernel,
        out_shape=jax.ShapeDtypeStruct(got.shape, BF16),
        grid_spec=pltpu.PrefetchScalarGridSpec(
            num_scalar_prefetch=1,
            grid=(1,),
            in_specs=[block, pl.BlockSpec((16, 24, 128), lambda i, c: (0, 0, 0)), column, column],
            out_specs=block,
        ),
        cost_estimate=pl.CostEstimate(flops=2000000, bytes_accessed=700000, transcendentals=0),
        name="combine",
    )(at, got, second, norm, size)


def finish_kernel(at_ref, got_ref, wo_ref, wp_ref, a_ref, norm_ref, size_ref, last_ref, own_ref, sum_own, sum_peer):
    step = pl.program_id(0)
    mags = []
    for q in range(8):
        j = 16 * step + 2 * q
        mags.append(got_ref[j, 40:41, :].astype(F32) + got_ref[j, 41:42, :].astype(F32))
        span = pl.ds(pl.multiple_of(step * 1024 + 128 * q, 128), 128)
        for r in range(2):
            last_ref[32 * r : 32 * r + 32, span] = got_ref[j + r, 0:32, :].astype(F32)
    mag = jnp.concatenate(mags, 1)
    last_ref[64:72, pl.ds(pl.multiple_of(step * 1024, 1024), 1024)] = jnp.broadcast_to(mag, (8, 1024))
    norm = norm_ref[...]
    coeff = -mag * size_ref[...] / (norm * norm)
    pair = jnp.concatenate(split(a_ref[...] * coeff), 0)
    own = contract(wo_ref[...], pair, (1, 1))
    peer = contract(wp_ref[...], pair, (1, 1))

    @pl.when(step == 0)
    def _():
        sum_own[...] = own
        sum_peer[...] = peer

    @pl.when(step > 0)
    def _():
        own_total, peer_total = (sum_own[...] + own).T, (sum_peer[...] + peer).T
        own_ref[...] = own_total[:64] + own_total[64:]
        last_ref[0:64, 2048:2304] = peer_total[:64] + peer_total[64:]
        last_ref[64:72, 2048:2304] = jnp.zeros((8, 256), F32)
        for a in range(8):
            rows = slice(8 * a, 8 * a + 8)
            for q in range(2):
                span = slice(128 * q, 128 * q + 128)
                own_ref[rows, span] += got_ref[4 * a + q, 32:40, :].astype(F32)
                last_ref[rows, 2048 + 128 * q : 2176 + 128 * q] += got_ref[4 * a + 2 + q, 32:40, :].astype(F32)


def finish(at, got, w_own, w_peer, adapter_out, norm, size):
    side = lambda i, c: (0, c[0] * 2 + i)
    whole = lambda i, c: (0, 0)
    return pl.pallas_call(
        finish_kernel,
        out_shape=(jax.ShapeDtypeStruct((72, 2304), F32), jax.ShapeDtypeStruct((64, 256), F32)),
        grid_spec=pltpu.PrefetchScalarGridSpec(
            num_scalar_prefetch=1,
            grid=(2,),
            in_specs=[
                pl.BlockSpec(got.shape, lambda i, c: (0, 0, 0)),
                pl.BlockSpec((256, 1024), side),
                pl.BlockSpec((256, 1024), side),
                pl.BlockSpec((64, 1024), side),
                pl.BlockSpec((1, 1024), side),
                pl.BlockSpec((1, 1024), side),
            ],
            out_specs=(pl.BlockSpec((72, 2304), whole), pl.BlockSpec((64, 256), whole)),
            scratch_shapes=[pltpu.VMEM((256, 128), F32), pltpu.VMEM((256, 128), F32)],
        ),
        cost_estimate=pl.CostEstimate(flops=600000000, bytes_accessed=3000000, transcendentals=0),
        name="finish",
    )(at, got, w_own, w_peer, adapter_out, norm, size)


def program(activations, base_weight, adapter_in, adapter_out, magnitude, cotangent):
    core = lax.axis_index("core")
    y = lax.axis_index("y")
    replica = lax.axis_index(REPLICA)
    sides = lax.axis_size("y")
    replicas = lax.axis_size(REPLICA)
    half = adapter_out.shape[1] // 2
    hops = [(2 * s, 2 * ((s + 1) % sides)) for s in range(sides)]
    hops += [(2 * s + 1, 2 * ((s - 1) % sides) + 1) for s in range(sides)]

    def swap(value):
        return lax.ppermute(value, "core", [(0, 1), (1, 0)])

    def shift(value):
        return lax.ppermute(value, TENSOR, hops)

    def exchange(value, axes):
        return lax.all_to_all(value, axes, 0, 0)

    def spread(value, axes):
        return exchange(jnp.broadcast_to(value, (lax.axis_size(axes),) + value.shape), axes)

    mine = lambda value: lax.dynamic_slice_in_dim(value, core * half, half, 1)
    other = lambda value: lax.dynamic_slice_in_dim(value, (1 - core) * half, half, 1)

    block = jnp.concatenate([cotangent, swap(cotangent)], 0)
    hop1 = shift(block)
    hop2 = shift(hop1)
    hop3 = shift(hop2)
    sign = 1 - 2 * core
    near, far = [], []
    for k in range(5):
        chip = lax.rem(y - sign * k + sides, sides) * 2
        near += [chip + core, chip + 1 - core]
    for k in range(1, 4):
        chip = lax.rem(y + sign * k + sides, sides) * 2
        far += [chip + 1 - core, chip + core]
    rows = [lax.rem(y + sign * 4 + sides, sides) * 2 + core]
    for k in (3, 2, 1):
        chip = lax.rem(y + sign * k + sides, sides) * 2
        rows += [chip + core, chip + 1 - core]
    rows += [2 * y + core]
    at = jnp.stack([core] + near + far + rows).astype(jnp.int32)

    act_peer = swap(activations)
    high = lax.reduce_precision(adapter_in, 8, 7)
    rest = (adapter_in - high).astype(BF16)
    high = high.astype(BF16)
    wide = jnp.concatenate([high, high, rest, rest], 1)
    pair = jnp.concatenate([high.T, rest.T], 0)
    window, part = replica // 2, lax.rem(replica, 2)
    pick = jnp.concatenate([lax.dynamic_slice_in_dim(pair, 64 * k + part * 32, 32, 0) for k in range(2)], 0)
    at_own = activations.T
    z = contract(pair, at_own, (1, 0))
    place = jnp.stack([window // 8, lax.rem(window, 8)]).astype(jnp.int32)
    w_own, first = merge(place, base_weight, wide, pick, adapter_out, z[:64] + z[64:])
    w_peer = swap(w_own)
    first = jnp.sum(exchange(first, TENSOR), axis=0)
    second = spread(first, TENSOR)
    hop4 = shift(mine(hop3))
    crossed = swap(jnp.concatenate([other(hop1), other(hop2), other(hop3)], 0))

    square_sum = second[:, 16:18].reshape(1, 2 * half)
    col_norm = jnp.sqrt(square_sum + epsilon)
    magnitude = magnitude.reshape(1, 2 * half)
    col_scale = magnitude / col_norm
    r4, r3, r2, r1, r0 = forward(at, activations, act_peer, w_own, w_peer)
    got = shift(r4).astype(F32)
    got = shift(jnp.concatenate([r3[:32] + got, r3[32:]], 0).astype(BF16)).astype(F32)
    got = shift((r2 + got).astype(BF16)).astype(F32)
    got = shift((r1 + got).astype(BF16))
    summed = r0 + got[:32].astype(F32) + swap(got[32:]).astype(F32)
    output = (summed * col_scale).astype(BF16)

    at_peer = act_peer.T
    scaled, slope = slopes(at, block, (hop1, hop2, hop3), hop4, crossed, col_scale, w_own, w_peer, at_own, at_peer)
    slope = jnp.sum(exchange(slope, "y"), axis=0)
    high = lax.reduce_precision(slope, 8, 7)
    slope = jnp.stack([high, slope - high], 1).astype(BF16)
    slope = jnp.broadcast_to(slope[:, None], (16, 2, 2, 128)).reshape(replicas, 2, 128)
    act_own, act_send, low = backward(at, scaled, w_own, w_peer, at_own, at_peer, second, adapter_out)
    low = exchange(jnp.concatenate([low, slope], 1), REPLICA)
    place = jnp.stack([core, window]).astype(jnp.int32)
    low = exchange(combine(place, low, second, col_norm, magnitude), REPLICA)
    act_add = swap(act_send)
    payload, in_own = finish(at, low, w_own, w_peer, adapter_out, col_norm, magnitude)
    last = swap(payload)
    grad_in = (in_own + last[:64, half:]).T
    join = lambda a, b: jnp.where(core == 0, jnp.concatenate([a, b], 1), jnp.concatenate([b, a], 1))
    grad_out = join(payload[:64, :half], last[:64, :half])
    grad_mag = join(payload[64:65, :half], last[64:65, :half]).reshape(2 * half)
    grad_act = (act_own + act_add.astype(F32)).astype(BF16)
    return (output, grad_act, grad_in, grad_out, grad_mag)


def solution(mesh):
    grid = Mesh(mesh.devices.reshape(8, 4, 8, 2), ("z", "x", "y", "core"))
    every = ("z", "x", "y", "core")
    in_specs = (P(REPLICA, TENSOR), P(TENSOR, None), P(TENSOR, None), P(), P(), P(every, None))
    out_specs = (P(every, None), P(REPLICA, TENSOR), P(TENSOR, None), P(), P())
    return jax.shard_map(program, mesh=grid, in_specs=in_specs, out_specs=out_specs, check_vma=False)
```

time: 175 us -> 180 us (1.029)
  waiting for transfers between devices: 14.9 us -> 32.3 us
  blocking collectives: 16.2 us -> 0 us
  Pallas kernels: 23.7 us -> 31.8 us
  local copies, waits for them, and re-layouts: 15.5 us -> 11.6 us
    psum x1 -> x0, blocking collectives: 16.2 us -> none  [program(): slope = lax.psum(slope, 'y')]
    ppermute x8, waiting for transfers between devices: 0.53 us -> 15.5 us  [shift(): return lax.ppermute(value, TENSOR, hops)]
    pallas_call x1 -> x3, Pallas kernels: 3.83 us -> 12.2 us  [the longest x1 5.34 us: slopes(): pl.pallas_call(slope_kernel, out_shape=(jax.ShapeDtypeStruct((tokens, col...]
    all_to_all x5, starting transfers between devices: 31.6 us -> 29 us  [exchange(): return lax.all_to_all(value, axes, 0, 0)]
    all_to_all x5, waiting for transfers between devices: 11.3 us -> 13.7 us  [exchange(): return lax.all_to_all(value, axes, 0, 0)]
    reshape x4 -> x0, local copies, waits for them, and re-layouts: 2.37 us -> none  [the longest x1 1.11 us: program(): in_part.reshape(replicas, 8, 128)]
    ppermute x8, starting transfers between devices: 24.2 us -> 26.4 us  [shift(): return lax.ppermute(value, TENSOR, hops)]
    slice x4, local copies, waits for them, and re-layouts: 0.06 us -> 1.96 us  [the longest x2 1.11 us: program(): grad_out = join(payload[:64, :half], last[:64, :half])]
  transfers between devices with their start and end apart: 20 -> 20, of which waited for: 7 -> 8; matrix products, arithmetic and copies ran while one was open for 11% -> 7% of each run, Pallas kernels for 11% -> 15%
where the time goes in v2:
time: 180 us; the launch traced here: 178 us
  starting transfers between devices  89.2 us (50%)
  waiting for transfers between devices  32.3 us (18%)
  Pallas kernels  31.8 us (18%)
  local copies, waits for them, and re-layouts  11.6 us (6%)
  other arithmetic  10.8 us (6%)
    ppermute x7, starting transfers between devices, swap(): return lax.ppermute(value, 'core', [(0, 1), (1, 0)])  33.9 us
    all_to_all x5, starting transfers between devices, exchange(): return lax.all_to_all(value, axes, 0, 0)  29 us
    ppermute x8, starting transfers between devices, shift(): return lax.ppermute(value, TENSOR, hops)  26.4 us
    ppermute x8, waiting for transfers between devices, shift(): return lax.ppermute(value, TENSOR, hops)  15.5 us
    all_to_all x5, waiting for transfers between devices, exchange(): return lax.all_to_all(value, axes, 0, 0)  13.7 us
    pallas_call x1, Pallas kernels, backward(): pl.pallas_call(backward_kernel, out_shape=(jax.ShapeDtypeStruct((tokens,...  7.73 us
    pallas_call x1, Pallas kernels, forward(): pl.pallas_call(forward_kernel, out_shape=tuple((jax.ShapeDtypeStruct((r,...  6.18 us
    pallas_call x1, Pallas kernels, merge(): pl.pallas_call(merge_kernel, out_shape=(jax.ShapeDtypeStruct((rows, cols)...  5.67 us
  transfers between devices with their start and end apart: 20, of which 8 were waited for; matrix products, arithmetic and copies ran while one was open for 7% of the time, Pallas kernels for 15%

profile of v2, /device:TPU:1, one launch (start us, length us, event | category | flops | bytes accessed | tf_op | source)
XLA Modules:
  0.0 178.2 jit_solution(7736531040267222662)
XLA Ops:
  0.7 0.9 reduce-precision_convert_fusion
  1.5 1.2 fusion
  2.7 0.7 slice_add_fusion.zt_ref
  3.4 0.8 copy.16.wide_ref
  4.2 0.6 pad_add_fusion.at_ref
  4.8 0.6 pad_maximum_fusion.6.pick_ref
  5.4 5.7 %merge.1 = (bf16[256,4096]{1,0:T(8,128)(2,1)}, f32[16,24,128]{2,1,0:T(8,128)}) custom-call(s32[2]{0:T(128)} %pad_add_fusion.at_ref, bf16[256,4096]{1,0:T(8,128)(2,1)} %base_ref.1, bf16[256,256]{1,0:T(8,128)(2,1)} %copy.16.wide_ref, bf16[64,256]{1,0:T(8,128)(2,1)} %pad_maximum_fusion.6.pick_ref, f32[64,4096]{1,0:T(8,128)} %a_ref.3, ...), custom_call_target="tpu_custom_call" | custom-call | flops 1400000000 | bytes 7000000 | tf_op jit(solution)/shard_map/merge/pallas_call | solution.py:56
  11.1 8.9 %collective-permute-start.1 = (bf16[256,4096]{1,0:T(8,128)(2,1)}, bf16[256,4096]{1,0:T(8,128)(2,1)S(1)}, u32[]{:S(2)}, u32[]{:S(2)}) collective-permute-start(bf16[256,4096]{1,0:T(8,128)(2,1)} %get-tuple-element.19.wa_ref.wo_ref), channel_id=1, source_target_pairs={{0,1},{1,0},{2,3},{3,2},{4,5},{5,4},{6,7},{7,6},{8,9},{9,8},{10,11... | collective-permute-start | bytes 6291464 | tf_op jit(solution)/shard_map/ppermute | solution.py:356
  20.0 1.9 %collective-permute-start.7 = (bf16[32,4096]{1,0:T(8,128)(2,1)S(1)}, bf16[32,4096]{1,0:T(8,128)(2,1)S(1)}, u32[]{:S(2)}, u32[]{:S(2)}) collective-permute-start(bf16[32,4096]{1,0:T(8,128)(2,1)S(1)} %copy-done.11), channel_id=1, source_target_pairs={{0,1},{1,0},{2,3},{3,2},{4,5},{5,4},{6,7},{7,6},{8,9},{9,8},{10,11... | collective-permute-start | bytes 786440 | tf_op jit(solution)/shard_map/ppermute | solution.py:356
  22.0 2.4 %collective-permute-done.7 = bf16[32,4096]{1,0:T(8,128)(2,1)S(1)} collective-permute-done((bf16[32,4096]{1,0:T(8,128)(2,1)S(1)}, bf16[32,4096]{1,0:T(8,128)(2,1)S(1)}, u32[]{:S(2)}, u32[]{:S(2)}) %collective-permute-start.7) | collective-permute-done | bytes 262176 | tf_op jit(solution)/shard_map/ppermute | solution.py:356
  24.4 1.9 %collective-permute-start.8 = (bf16[64,4096]{1,0:T(8,128)(2,1)S(1)}, bf16[64,4096]{1,0:T(8,128)(2,1)S(1)}, u32[]{:S(2)}, u32[]{:S(2)}) collective-permute-start(bf16[64,4096]{1,0:T(8,128)(2,1)S(1)} %constant_dynamic-update-slice_fusion.block_ref), channel_id=1, source_target_pairs={{0,2},{2,4},{4,6},{6,8},{8,10},{10,12},{12,14},{14,0},{1,15},{3,1}... | collective-permute-start | bytes 1572872 | tf_op jit(solution)/shard_map/ppermute | solution.py:359
  26.3 8.3 %collective-permute-done.8.hop1_ref = bf16[64,4096]{1,0:T(8,128)(2,1)S(1)} collective-permute-done((bf16[64,4096]{1,0:T(8,128)(2,1)S(1)}, bf16[64,4096]{1,0:T(8,128)(2,1)S(1)}, u32[]{:S(2)}, u32[]{:S(2)}) %collective-permute-start.8) | collective-permute-done | bytes 524320 | tf_op jit(solution)/shard_map/ppermute | solution.py:359
  34.6 2.8 %collective-permute-start.9 = (bf16[64,4096]{1,0:T(8,128)(2,1)S(1)}, bf16[64,4096]{1,0:T(8,128)(2,1)}, u32[]{:S(2)}, u32[]{:S(2)}) collective-permute-start(bf16[64,4096]{1,0:T(8,128)(2,1)S(1)} %collective-permute-done.8.hop1_ref), channel_id=1, source_target_pairs={{0,2},{2,4},{4,6},{6,8},{8,10},{10,12},{12,14},{14,0},{1,15},{3,1}... | collective-permute-start | bytes 1572872 | tf_op jit(solution)/shard_map/ppermute | solution.py:359
  37.5 6.0 %all-to-all-start = ((f32[16,24,128]{2,1,0:T(8,128)}), f32[16,24,128]{2,1,0:T(8,128)S(1)}, u32[]{:S(2)}, u32[]{:S(2)}) async-start(f32[16,24,128]{2,1,0:T(8,128)} %get-tuple-element.25), calls=%async_computation | async-start | bytes 393216 | tf_op jit(solution)/shard_map/all_to_all | solution.py:362
  43.5 0.1 copy.15
  43.7 2.0 %collective-permute-start = (bf16[512,256]{0,1:T(8,128)(2,1)S(1)}, bf16[512,256]{0,1:T(8,128)(2,1)S(1)}, u32[]{:S(2)}, u32[]{:S(2)}) collective-permute-start(bf16[512,256]{0,1:T(8,128)(2,1)S(1)} %copy.15), channel_id=1, source_target_pairs={{0,1},{1,0},{2,3},{3,2},{4,5},{5,4},{6,7},{7,6},{8,9},{9,8},{10,11... | collective-permute-start | bytes 786440 | tf_op jit(solution)/shard_map/ppermute | solution.py:356
  45.7 0.7 stack.106.at_ref
  46.4 0.7 collective-permute-done
  47.1 0.8 copy.17.b_ref
  47.9 5.5 %all-to-all-done = f32[16,24,128]{2,1,0:T(8,128)S(1)} async-done(((f32[16,24,128]{2,1,0:T(8,128)}), f32[16,24,128]{2,1,0:T(8,128)S(1)}, u32[]{:S(2)}, u32[]{:S(2)}) %all-to-all-start) | async-done | bytes 196640 | tf_op jit(solution)/shard_map/all_to_all | solution.py:362
  53.5 0.7 broadcast_in_dim.4
  54.2 3.4 %all-to-all-start.1 = ((f32[16,24,128]{2,1,0:T(8,128)}), f32[16,24,128]{2,1,0:T(8,128)S(1)}, u32[]{:S(2)}, u32[]{:S(2)}) async-start(f32[16,24,128]{2,1,0:T(8,128)} %broadcast_in_dim.4), calls=%async_computation.1 | async-start | bytes 393216 | tf_op jit(solution)/shard_map/all_to_all | solution.py:362
  57.7 4.5 %collective-permute-start.10 = (bf16[64,4096]{1,0:T(8,128)(2,1)}, bf16[64,4096]{1,0:T(8,128)(2,1)S(1)}, u32[]{:S(2)}, u32[]{:S(2)}) collective-permute-start(bf16[64,4096]{1,0:T(8,128)(2,1)} %collective-permute-done.9.hop2_ref), channel_id=1, source_target_pairs={{0,2},{2,4},{4,6},{6,8},{8,10},{10,12},{12,14},{14,0},{1,15},{3,1}... | collective-permute-start | bytes 1572872 | tf_op jit(solution)/shard_map/ppermute | solution.py:359
  62.1 1.0 constant_dynamic-slice_fusion.2
  63.1 1.0 constant_dynamic-slice_fusion.1
  64.1 1.3 copy-done
  65.4 6.2 %forward.1 = (bf16[32,4096]{1,0:T(8,128)(2,1)}, f32[64,4096]{1,0:T(8,128)}, f32[64,4096]{1,0:T(8,128)}, f32[64,4096]{1,0:T(8,128)}, f32[32,4096]{1,0:T(8,128)}) custom-call(s32[25]{0:T(128)} %stack.106.at_ref, bf16[512,256]{1,0:T(8,128)(2,1)} %a_ref.2, bf16[512,256]{1,0:T(8,128)(2,1)} %copy.17.b_ref, bf16[256,4096]{1,0:T(8,128)(2,1)} %get-tuple-element.19.wa_ref.wo_ref, ...), custom_call_target="tpu_custom_call" | custom-call | flops 1073741824 | bytes 5000000 | tf_op jit(solution)/shard_map/forward/pallas_call | solution.py:102
  71.6 3.2 %collective-permute-start.2 = (bf16[32,4096]{1,0:T(8,128)(2,1)}, bf16[32,4096]{1,0:T(8,128)(2,1)S(1)}, u32[]{:S(2)}, u32[]{:S(2)}) collective-permute-start(bf16[32,4096]{1,0:T(8,128)(2,1)} %get-tuple-element.24), channel_id=1, source_target_pairs={{0,2},{2,4},{4,6},{6,8},{8,10},{10,12},{12,14},{14,0},{1,15},{3,1}... | collective-permute-start | bytes 786440 | tf_op jit(solution)/shard_map/ppermute | solution.py:359
  74.9 0.8 constant_dynamic-slice_fusion
  75.8 1.9 %collective-permute-start.12 = (bf16[192,2048]{1,0:T(8,128)(2,1)S(1)}, bf16[192,2048]{1,0:T(8,128)(2,1)}, u32[]{:S(2)}, u32[]{:S(2)}) collective-permute-start(bf16[192,2048]{1,0:T(8,128)(2,1)S(1)} %pad_maximum_fusion), channel_id=1, source_target_pairs={{0,1},{1,0},{2,3},{3,2},{4,5},{5,4},{6,7},{7,6},{8,9},{9,8},{10,11... | collective-permute-start | bytes 2359304 | tf_op jit(solution)/shard_map/ppermute | solution.py:356
  77.8 1.6 collective-permute-done.2
  79.5 4.0 %collective-permute-start.3 = (bf16[64,4096]{1,0:T(8,128)(2,1)S(1)}, bf16[64,4096]{1,0:T(8,128)(2,1)S(1)}, u32[]{:S(2)}, u32[]{:S(2)}) collective-permute-start(bf16[64,4096]{1,0:T(8,128)(2,1)S(1)} %pad_maximum_fusion.1), channel_id=1, source_target_pairs={{0,2},{2,4},{4,6},{6,8},{8,10},{10,12},{12,14},{14,0},{1,15},{3,1}... | collective-permute-start | bytes 1572872 | tf_op jit(solution)/shard_map/ppermute | solution.py:359
  83.5 2.2 %collective-permute-start.11 = (bf16[64,2048]{1,0:T(8,128)(2,1)}, bf16[64,2048]{1,0:T(8,128)(2,1)S(1)}, u32[]{:S(2)}, u32[]{:S(2)}) collective-permute-start(bf16[64,2048]{1,0:T(8,128)(2,1)} %get-tuple-element.34), channel_id=1, source_target_pairs={{0,2},{2,4},{4,6},{6,8},{8,10},{10,12},{12,14},{14,0},{1,15},{3,1}... | collective-permute-start | bytes 786440 | tf_op jit(solution)/shard_map/ppermute | solution.py:359
  85.7 0.7 fusion.5
  86.3 0.6 div.26
  86.9 5.6 %collective-permute-done.11.hop4_ref = bf16[64,2048]{1,0:T(8,128)(2,1)S(1)} collective-permute-done((bf16[64,2048]{1,0:T(8,128)(2,1)}, bf16[64,2048]{1,0:T(8,128)(2,1)S(1)}, u32[]{:S(2)}, u32[]{:S(2)}) %collective-permute-start.11) | collective-permute-done | bytes 262176 | tf_op jit(solution)/shard_map/ppermute | solution.py:359
  92.5 0.7 copy-done.20
  93.2 5.3 %slopes.1 = (bf16[512,2048]{1,0:T(8,128)(2,1)}, f32[8,16,128]{2,1,0:T(8,128)}) custom-call(s32[25]{0:T(128)} %stack.106.at_ref, bf16[64,4096]{1,0:T(8,128)(2,1)} %copy-done.16, bf16[64,4096]{1,0:T(8,128)(2,1)} %copy-done.15, bf16[64,4096]{1,0:T(8,128)(2,1)} %collective-permute-done.9.hop2_ref, bf16[64,4096]{1,0:T(8,128)(2,1)} %copy-done.8, ...), custom_call_target="tpu_custom_call" | custom-call | flops 2200000000 | bytes 8000000 | tf_op jit(solution)/shard_map/slopes/pallas_call | solution.py:142
  98.5 4.3 %all-to-all-start.2 = ((f32[8,16,128]{2,1,0:T(8,128)}), f32[8,16,128]{2,1,0:T(8,128)S(1)}, u32[]{:S(2)}, u32[]{:S(2)}) async-start(f32[8,16,128]{2,1,0:T(8,128)} %get-tuple-element.30), calls=%async_computation.2 | async-start | bytes 131072 | tf_op jit(solution)/shard_map/all_to_all | solution.py:362
  102.9 0.1 add_convert_fusion.1
  103.0 4.6 %collective-permute-start.4 = (bf16[64,4096]{1,0:T(8,128)(2,1)S(1)}, bf16[64,4096]{1,0:T(8,128)(2,1)S(1)}, u32[]{:S(2)}, u32[]{:S(2)}) collective-permute-start(bf16[64,4096]{1,0:T(8,128)(2,1)S(1)} %add_convert_fusion.1), channel_id=1, source_target_pairs={{0,2},{2,4},{4,6},{6,8},{8,10},{10,12},{12,14},{14,0},{1,15},{3,1}... | collective-permute-start | bytes 1572872 | tf_op jit(solution)/shard_map/ppermute | solution.py:359
  107.5 7.7 %backward.1 = (f32[512,256]{1,0:T(8,128)}, bf16[512,256]{1,0:T(8,128)(2,1)}, bf16[32,40,128]{2,1,0:T(8,128)(2,1)}) custom-call(s32[25]{0:T(128)} %stack.106.at_ref, bf16[512,2048]{1,0:T(8,128)(2,1)} %get-tuple-element.26.scaled_ref, bf16[256,4096]{1,0:T(8,128)(2,1)} %get-tuple-element.19.wa_ref.wo_ref, bf16[256,4096]{1,0:T(8,128)(2,1)} %copy-done, ...), custom_call_target="tpu_custom_call" | custom-call | flops 3000000000 | bytes 6000000 | tf_op jit(solution)/shard_map/backward/pallas_call | solution.py:220
  115.4 1.8 %pad_maximum_fusion.2 = bf16[32,42,128]{2,1,0:T(8,128)(2,1)} fusion(bf16[32,2,128]{2,1,0:T(2,128)(2,1)S(1)} %bitcast.52, bf16[32,40,128]{2,1,0:T(8,128)(2,1)} %get-tuple-element.29), kind=kLoop, calls=%fused_computation.9 | loop fusion | flops 688128 | bytes 688128 | tf_op jit(solution)/shard_map/concatenate | solution.py:426
  117.2 11.3 %all-to-all-start.3 = ((bf16[32,42,128]{2,1,0:T(8,128)(2,1)}), bf16[32,42,128]{2,1,0:T(8,128)(2,1)S(1)}, u32[]{:S(2)}, u32[]{:S(2)}) async-start(bf16[32,42,128]{2,1,0:T(8,128)(2,1)} %pad_maximum_fusion.2), calls=%async_computation.3 | async-start | bytes 786432 | tf_op jit(solution)/shard_map/all_to_all | solution.py:362
  128.5 0.1 add_convert_fusion
  128.7 3.2 %collective-permute-start.5 = (bf16[64,4096]{1,0:T(8,128)(2,1)S(1)}, bf16[64,4096]{1,0:T(8,128)(2,1)S(1)}, u32[]{:S(2)}, u32[]{:S(2)}) collective-permute-start(bf16[64,4096]{1,0:T(8,128)(2,1)S(1)} %add_convert_fusion), channel_id=1, source_target_pairs={{0,2},{2,4},{4,6},{6,8},{8,10},{10,12},{12,14},{14,0},{1,15},{3,1}... | collective-permute-start | bytes 1572872 | tf_op jit(solution)/shard_map/ppermute | solution.py:359
  131.9 0.6 pad_add_fusion.1.at_ref
  132.5 7.5 %all-to-all-done.3.got_ref = bf16[32,42,128]{2,1,0:T(8,128)(2,1)S(1)} async-done(((bf16[32,42,128]{2,1,0:T(8,128)(2,1)}), bf16[32,42,128]{2,1,0:T(8,128)(2,1)S(1)}, u32[]{:S(2)}, u32[]{:S(2)}) %all-to-all-start.3) | async-done | bytes 344096 | tf_op jit(solution)/shard_map/all_to_all | solution.py:362
  140.0 0.8 copy-done.3
  140.8 2.6 %combine.1 = bf16[32,42,128]{2,1,0:T(8,128)(2,1)} custom-call(s32[2]{0:T(128)} %pad_add_fusion.1.at_ref, bf16[32,42,128]{2,1,0:T(8,128)(2,1)} %copy-done.3, f32[16,24,128]{2,1,0:T(8,128)} %copy-done.6, f32[1,4096]{1,0:T(1,128)} %bitcast.49, f32[1,4096]{1,0:T(1,128)} %bitcast.47), custom_call_target="tpu_custom_call" | custom-call | flops 2000000 | bytes 700000 | tf_op jit(solution)/shard_map/combine/pallas_call | solution.py:270
  143.4 3.9 %all-to-all-start.4 = ((bf16[32,42,128]{2,1,0:T(8,128)(2,1)}), bf16[32,42,128]{2,1,0:T(8,128)(2,1)S(1)}, u32[]{:S(2)}, u32[]{:S(2)}) async-start(bf16[32,42,128]{2,1,0:T(8,128)(2,1)} %combine.1), calls=%async_computation.4 | async-start | bytes 786432 | tf_op jit(solution)/shard_map/all_to_all | solution.py:362
  147.3 8.0 %collective-permute-start.13 = (bf16[512,256]{1,0:T(8,128)(2,1)S(1)}, bf16[512,256]{1,0:T(8,128)(2,1)S(1)}, u32[]{:S(2)}, u32[]{:S(2)}) collective-permute-start(bf16[512,256]{1,0:T(8,128)(2,1)S(1)} %copy-done.19), channel_id=1, source_target_pairs={{0,1},{1,0},{2,3},{3,2},{4,5},{5,4},{6,7},{7,6},{8,9},{9,8},{10,11... | collective-permute-start | bytes 786440 | tf_op jit(solution)/shard_map/ppermute | solution.py:356
  155.4 1.9 %collective-permute-start.6 = (bf16[32,4096]{1,0:T(8,128)(2,1)S(1)}, bf16[32,4096]{1,0:T(8,128)(2,1)S(1)}, u32[]{:S(2)}, u32[]{:S(2)}) collective-permute-start(bf16[32,4096]{1,0:T(8,128)(2,1)S(1)} %slice.53), channel_id=1, source_target_pairs={{0,1},{1,0},{2,3},{3,2},{4,5},{5,4},{6,7},{7,6},{8,9},{9,8},{10,11... | collective-permute-start | bytes 786440 | tf_op jit(solution)/shard_map/ppermute | solution.py:356
  157.3 0.8 add_convert_fusion.2
  158.1 0.7 all-to-all-done.4.got_ref
  158.8 0.7 copy-done.2
  159.5 4.3 %finish.1 = (f32[72,2304]{1,0:T(8,128)}, f32[64,256]{1,0:T(8,128)}) custom-call(s32[25]{0:T(128)} %stack.106.at_ref, bf16[32,42,128]{2,1,0:T(8,128)(2,1)} %copy-done.2, bf16[256,4096]{1,0:T(8,128)(2,1)} %get-tuple-element.19.wa_ref.wo_ref, bf16[256,4096]{1,0:T(8,128)(2,1)} %copy-done, f32[64,4096]{1,0:T(8,128)} %a_ref.3, f32[1,4096]{1,0:T(1,128)} %bitcast.50, ...), custom_call_target="tpu_custom_call" | custom-call | flops 600000000 | bytes 3000000 | tf_op jit(solution)/shard_map/finish/pallas_call | solution.py:323
  163.8 9.2 %collective-permute-start.14 = (f32[72,2304]{1,0:T(8,128)}, f32[72,2304]{1,0:T(8,128)S(1)}, u32[]{:S(2)}, u32[]{:S(2)}) collective-permute-start(f32[72,2304]{1,0:T(8,128)} %get-tuple-element.32), channel_id=1, source_target_pairs={{0,1},{1,0},{2,3},{3,2},{4,5},{5,4},{6,7},{7,6},{8,9},{9,8},{10,11... | collective-permute-start | bytes 1990664 | tf_op jit(solution)/shard_map/ppermute | solution.py:356
  173.0 0.8 slice.47
  173.9 1.1 slice.45
  175.0 0.8 multiply_convert_fusion
  175.8 0.6 maximum_select_fusion.1
  176.4 1.1 maximum_select_fusion
  177.5 0.6 fusion.2
  (67 shorter events, 0.5 us)
Async XLA Ops:
  5.4 14.6 %copy-start.11 = (bf16[32,4096]{1,0:T(8,128)(2,1)S(1)}, bf16[32,4096]{1,0:T(8,128)(2,1)}, u32[]{:S(2)}) copy-start(bf16[32,4096]{1,0:T(8,128)(2,1)} %param.11) | copy-start | bytes 786436
  11.1 32.4 %copy-start.1 = (bf16[512,256]{1,0:T(8,128)(2,1)S(1)}, bf16[512,256]{1,0:T(8,128)(2,1)}, u32[]{:S(2)}) copy-start(bf16[512,256]{1,0:T(8,128)(2,1)} %a_ref.2) | copy-start | bytes 786436
  11.1 53.0 %collective-permute-start.1 = (bf16[256,4096]{1,0:T(8,128)(2,1)}, bf16[256,4096]{1,0:T(8,128)(2,1)S(1)}, u32[]{:S(2)}, u32[]{:S(2)}) collective-permute-start(bf16[256,4096]{1,0:T(8,128)(2,1)} %get-tuple-element.19.wa_ref.wo_ref), channel_id=1, source_target_pairs={{0,1},{1,0},{2,3},{3,2},{4,5},{5,4},{6,7},{7,6},{8,9},{9,8},{10,11... | collective-permute-start | bytes 6291464 | tf_op jit(solution)/shard_map/ppermute | solution.py:356
  20.0 4.3 %collective-permute-start.7 = (bf16[32,4096]{1,0:T(8,128)(2,1)S(1)}, bf16[32,4096]{1,0:T(8,128)(2,1)S(1)}, u32[]{:S(2)}, u32[]{:S(2)}) collective-permute-start(bf16[32,4096]{1,0:T(8,128)(2,1)S(1)} %copy-done.11), channel_id=1, source_target_pairs={{0,1},{1,0},{2,3},{3,2},{4,5},{5,4},{6,7},{7,6},{8,9},{9,8},{10,11... | collective-permute-start | bytes 786440 | tf_op jit(solution)/shard_map/ppermute | solution.py:356
  24.4 10.2 %copy-start.16 = (bf16[64,4096]{1,0:T(8,128)(2,1)}, bf16[64,4096]{1,0:T(8,128)(2,1)S(1)}, u32[]{:S(2)}) copy-start(bf16[64,4096]{1,0:T(8,128)(2,1)S(1)} %constant_dynamic-update-slice_fusion.block_ref) | copy-start | bytes 1572868
  24.4 10.2 %collective-permute-start.8 = (bf16[64,4096]{1,0:T(8,128)(2,1)S(1)}, bf16[64,4096]{1,0:T(8,128)(2,1)S(1)}, u32[]{:S(2)}, u32[]{:S(2)}) collective-permute-start(bf16[64,4096]{1,0:T(8,128)(2,1)S(1)} %constant_dynamic-update-slice_fusion.block_ref), channel_id=1, source_target_pairs={{0,2},{2,4},{4,6},{6,8},{8,10},{10,12},{12,14},{14,0},{1,15},{3,1}... | collective-permute-start | bytes 1572872 | tf_op jit(solution)/shard_map/ppermute | solution.py:359
  34.6 23.0 %copy-start.15 = (bf16[64,4096]{1,0:T(8,128)(2,1)}, bf16[64,4096]{1,0:T(8,128)(2,1)S(1)}, u32[]{:S(2)}) copy-start(bf16[64,4096]{1,0:T(8,128)(2,1)S(1)} %collective-permute-done.8.hop1_ref) | copy-start | bytes 1572868
  34.6 23.0 %collective-permute-start.9 = (bf16[64,4096]{1,0:T(8,128)(2,1)S(1)}, bf16[64,4096]{1,0:T(8,128)(2,1)}, u32[]{:S(2)}, u32[]{:S(2)}) collective-permute-start(bf16[64,4096]{1,0:T(8,128)(2,1)S(1)} %collective-permute-done.8.hop1_ref), channel_id=1, source_target_pairs={{0,2},{2,4},{4,6},{6,8},{8,10},{10,12},{12,14},{14,0},{1,15},{3,1}... | collective-permute-start | bytes 1572872 | tf_op jit(solution)/shard_map/ppermute | solution.py:359
  37.5 16.0 %all-to-all-start = ((f32[16,24,128]{2,1,0:T(8,128)}), f32[16,24,128]{2,1,0:T(8,128)S(1)}, u32[]{:S(2)}, u32[]{:S(2)}) async-start(f32[16,24,128]{2,1,0:T(8,128)} %get-tuple-element.25), calls=%async_computation | async-start | bytes 393216 | tf_op jit(solution)/shard_map/all_to_all | solution.py:362
  43.7 10.6 %copy-start.12 = (bf16[512,256]{0,1:T(8,128)(2,1)}, bf16[512,256]{0,1:T(8,128)(2,1)S(1)}, u32[]{:S(2)}) copy-start(bf16[512,256]{0,1:T(8,128)(2,1)S(1)} %copy.15) | copy-start | bytes 786436
  43.7 3.4 %collective-permute-start = (bf16[512,256]{0,1:T(8,128)(2,1)S(1)}, bf16[512,256]{0,1:T(8,128)(2,1)S(1)}, u32[]{:S(2)}, u32[]{:S(2)}) collective-permute-start(bf16[512,256]{0,1:T(8,128)(2,1)S(1)} %copy.15), channel_id=1, source_target_pairs={{0,1},{1,0},{2,3},{3,2},{4,5},{5,4},{6,7},{7,6},{8,9},{9,8},{10,11... | collective-permute-start | bytes 786440 | tf_op jit(solution)/shard_map/ppermute | solution.py:356
  47.1 10.6 %copy-start.13 = (bf16[512,256]{0,1:T(8,128)(2,1)}, bf16[512,256]{0,1:T(8,128)(2,1)S(1)}, u32[]{:S(2)}) copy-start(bf16[512,256]{0,1:T(8,128)(2,1)S(1)} %collective-permute-done) | copy-start | bytes 786436
  54.2 31.4 %all-to-all-start.1 = ((f32[16,24,128]{2,1,0:T(8,128)}), f32[16,24,128]{2,1,0:T(8,128)S(1)}, u32[]{:S(2)}, u32[]{:S(2)}) async-start(f32[16,24,128]{2,1,0:T(8,128)} %broadcast_in_dim.4), calls=%async_computation.1 | async-start | bytes 393216 | tf_op jit(solution)/shard_map/all_to_all | solution.py:362
  57.7 17.2 %collective-permute-start.10 = (bf16[64,4096]{1,0:T(8,128)(2,1)}, bf16[64,4096]{1,0:T(8,128)(2,1)S(1)}, u32[]{:S(2)}, u32[]{:S(2)}) collective-permute-start(bf16[64,4096]{1,0:T(8,128)(2,1)} %collective-permute-done.9.hop2_ref), channel_id=1, source_target_pairs={{0,2},{2,4},{4,6},{6,8},{8,10},{10,12},{12,14},{14,0},{1,15},{3,1}... | collective-permute-start | bytes 1572872 | tf_op jit(solution)/shard_map/ppermute | solution.py:359
  64.1 1.3 copy-start
  71.6 6.1 %copy-start.7 = (f32[64,4096]{1,0:T(8,128)S(1)}, f32[64,4096]{1,0:T(8,128)}, u32[]{:S(2)}) copy-start(f32[64,4096]{1,0:T(8,128)} %get-tuple-element.23) | copy-start | bytes 3145732
  71.6 7.7 %collective-permute-start.2 = (bf16[32,4096]{1,0:T(8,128)(2,1)}, bf16[32,4096]{1,0:T(8,128)(2,1)S(1)}, u32[]{:S(2)}, u32[]{:S(2)}) collective-permute-start(bf16[32,4096]{1,0:T(8,128)(2,1)} %get-tuple-element.24), channel_id=1, source_target_pairs={{0,2},{2,4},{4,6},{6,8},{8,10},{10,12},{12,14},{14,0},{1,15},{3,1}... | collective-permute-start | bytes 786440 | tf_op jit(solution)/shard_map/ppermute | solution.py:359
  74.8 2.9 %copy-start.8 = (bf16[64,4096]{1,0:T(8,128)(2,1)}, bf16[64,4096]{1,0:T(8,128)(2,1)S(1)}, u32[]{:S(2)}) copy-start(bf16[64,4096]{1,0:T(8,128)(2,1)S(1)} %collective-permute-done.10.hop3_ref) | copy-start | bytes 1572868
  75.8 10.6 %copy-start.14 = (f32[4096]{0:T(1024)S(1)}, f32[4096]{0:T(1024)}, u32[]{:S(2)}) copy-start(f32[4096]{0:T(1024)} %param.10) | copy-start | bytes 49156
  75.8 16.7 %collective-permute-start.12 = (bf16[192,2048]{1,0:T(8,128)(2,1)S(1)}, bf16[192,2048]{1,0:T(8,128)(2,1)}, u32[]{:S(2)}, u32[]{:S(2)}) collective-permute-start(bf16[192,2048]{1,0:T(8,128)(2,1)S(1)} %pad_maximum_fusion), channel_id=1, source_target_pairs={{0,1},{1,0},{2,3},{3,2},{4,5},{5,4},{6,7},{7,6},{8,9},{9,8},{10,11... | collective-permute-start | bytes 2359304 | tf_op jit(solution)/shard_map/ppermute | solution.py:356
  79.5 23.4 %collective-permute-start.3 = (bf16[64,4096]{1,0:T(8,128)(2,1)S(1)}, bf16[64,4096]{1,0:T(8,128)(2,1)S(1)}, u32[]{:S(2)}, u32[]{:S(2)}) collective-permute-start(bf16[64,4096]{1,0:T(8,128)(2,1)S(1)} %pad_maximum_fusion.1), channel_id=1, source_target_pairs={{0,2},{2,4},{4,6},{6,8},{8,10},{10,12},{12,14},{14,0},{1,15},{3,1}... | collective-permute-start | bytes 1572872 | tf_op jit(solution)/shard_map/ppermute | solution.py:359
  83.5 9.0 %collective-permute-start.11 = (bf16[64,2048]{1,0:T(8,128)(2,1)}, bf16[64,2048]{1,0:T(8,128)(2,1)S(1)}, u32[]{:S(2)}, u32[]{:S(2)}) collective-permute-start(bf16[64,2048]{1,0:T(8,128)(2,1)} %get-tuple-element.34), channel_id=1, source_target_pairs={{0,2},{2,4},{4,6},{6,8},{8,10},{10,12},{12,14},{14,0},{1,15},{3,1}... | collective-permute-start | bytes 786440 | tf_op jit(solution)/shard_map/ppermute | solution.py:359
  85.6 12.9 %copy-start.6 = (f32[16,24,128]{2,1,0:T(8,128)}, f32[16,24,128]{2,1,0:T(8,128)S(1)}, u32[]{:S(2)}) copy-start(f32[16,24,128]{2,1,0:T(8,128)S(1)} %all-to-all-done.1.second_ref) | copy-start | bytes 589828
  92.5 0.7 copy-start.20
  93.2 9.6 %copy-start.5 = (f32[64,4096]{1,0:T(8,128)S(1)}, f32[64,4096]{1,0:T(8,128)}, u32[]{:S(2)}) copy-start(f32[64,4096]{1,0:T(8,128)} %get-tuple-element.22) | copy-start | bytes 3145732
  98.5 16.7 %all-to-all-start.2 = ((f32[8,16,128]{2,1,0:T(8,128)}), f32[8,16,128]{2,1,0:T(8,128)S(1)}, u32[]{:S(2)}, u32[]{:S(2)}) async-start(f32[8,16,128]{2,1,0:T(8,128)} %get-tuple-element.30), calls=%async_computation.2 | async-start | bytes 131072 | tf_op jit(solution)/shard_map/all_to_all | solution.py:362
  103.0 25.6 %collective-permute-start.4 = (bf16[64,4096]{1,0:T(8,128)(2,1)S(1)}, bf16[64,4096]{1,0:T(8,128)(2,1)S(1)}, u32[]{:S(2)}, u32[]{:S(2)}) collective-permute-start(bf16[64,4096]{1,0:T(8,128)(2,1)S(1)} %add_convert_fusion.1), channel_id=1, source_target_pairs={{0,2},{2,4},{4,6},{6,8},{8,10},{10,12},{12,14},{14,0},{1,15},{3,1}... | collective-permute-start | bytes 1572872 | tf_op jit(solution)/shard_map/ppermute | solution.py:359
  115.3 13.3 %copy-start.4 = (f32[64,4096]{1,0:T(8,128)S(1)}, f32[64,4096]{1,0:T(8,128)}, u32[]{:S(2)}) copy-start(f32[64,4096]{1,0:T(8,128)} %get-tuple-element.21) | copy-start | bytes 3145732
  117.2 22.8 %all-to-all-start.3 = ((bf16[32,42,128]{2,1,0:T(8,128)(2,1)}), bf16[32,42,128]{2,1,0:T(8,128)(2,1)S(1)}, u32[]{:S(2)}, u32[]{:S(2)}) async-start(bf16[32,42,128]{2,1,0:T(8,128)(2,1)} %pad_maximum_fusion.2), calls=%async_computation.3 | async-start | bytes 786432 | tf_op jit(solution)/shard_map/all_to_all | solution.py:362
  128.5 18.8 %copy-start.19 = (bf16[512,256]{1,0:T(8,128)(2,1)S(1)}, bf16[512,256]{1,0:T(8,128)(2,1)}, u32[]{:S(2)}) copy-start(bf16[512,256]{1,0:T(8,128)(2,1)} %get-tuple-element.28) | copy-start | bytes 786436
  128.6 28.7 %copy-start.9 = (f32[512,256]{1,0:T(8,128)S(1)}, f32[512,256]{1,0:T(8,128)}, u32[]{:S(2)}) copy-start(f32[512,256]{1,0:T(8,128)} %get-tuple-element.27) | copy-start | bytes 1572868
  128.7 26.7 %collective-permute-start.5 = (bf16[64,4096]{1,0:T(8,128)(2,1)S(1)}, bf16[64,4096]{1,0:T(8,128)(2,1)S(1)}, u32[]{:S(2)}, u32[]{:S(2)}) collective-permute-start(bf16[64,4096]{1,0:T(8,128)(2,1)S(1)} %add_convert_fusion), channel_id=1, source_target_pairs={{0,2},{2,4},{4,6},{6,8},{8,10},{10,12},{12,14},{14,0},{1,15},{3,1}... | collective-permute-start | bytes 1572872 | tf_op jit(solution)/shard_map/ppermute | solution.py:359
  140.0 0.8 copy-start.3
  143.4 15.4 %all-to-all-start.4 = ((bf16[32,42,128]{2,1,0:T(8,128)(2,1)}), bf16[32,42,128]{2,1,0:T(8,128)(2,1)S(1)}, u32[]{:S(2)}, u32[]{:S(2)}) async-start(bf16[32,42,128]{2,1,0:T(8,128)(2,1)} %combine.1), calls=%async_computation.4 | async-start | bytes 786432 | tf_op jit(solution)/shard_map/all_to_all | solution.py:362
  147.3 10.0 %collective-permute-start.13 = (bf16[512,256]{1,0:T(8,128)(2,1)S(1)}, bf16[512,256]{1,0:T(8,128)(2,1)S(1)}, u32[]{:S(2)}, u32[]{:S(2)}) collective-permute-start(bf16[512,256]{1,0:T(8,128)(2,1)S(1)} %copy-done.19), channel_id=1, source_target_pairs={{0,1},{1,0},{2,3},{3,2},{4,5},{5,4},{6,7},{7,6},{8,9},{9,8},{10,11... | collective-permute-start | bytes 786440 | tf_op jit(solution)/shard_map/ppermute | solution.py:356
  155.4 19.6 %collective-permute-start.6 = (bf16[32,4096]{1,0:T(8,128)(2,1)S(1)}, bf16[32,4096]{1,0:T(8,128)(2,1)S(1)}, u32[]{:S(2)}, u32[]{:S(2)}) collective-permute-start(bf16[32,4096]{1,0:T(8,128)(2,1)S(1)} %slice.53), channel_id=1, source_target_pairs={{0,1},{1,0},{2,3},{3,2},{4,5},{5,4},{6,7},{7,6},{8,9},{9,8},{10,11... | collective-permute-start | bytes 786440 | tf_op jit(solution)/shard_map/ppermute | solution.py:356
  158.1 16.9 %copy-start.10 = (f32[32,4096]{1,0:T(8,128)S(1)}, f32[32,4096]{1,0:T(8,128)}, u32[]{:S(2)}) copy-start(f32[32,4096]{1,0:T(8,128)} %get-tuple-element.20) | copy-start | bytes 1572868
  158.1 16.9 %copy-start.18 = (f32[4096]{0:T(1024)S(1)}, f32[4096]{0:T(1024)}, u32[]{:S(2)}) copy-start(f32[4096]{0:T(1024)} %div.26) | copy-start | bytes 49156
  158.8 0.8 copy-start.2
  163.8 12.0 %collective-permute-start.14 = (f32[72,2304]{1,0:T(8,128)}, f32[72,2304]{1,0:T(8,128)S(1)}, u32[]{:S(2)}, u32[]{:S(2)}) collective-permute-start(f32[72,2304]{1,0:T(8,128)} %get-tuple-element.32), channel_id=1, source_target_pairs={{0,1},{1,0},{2,3},{3,2},{4,5},{5,4},{6,7},{7,6},{8,9},{9,8},{10,11... | collective-permute-start | bytes 1990664 | tf_op jit(solution)/shard_map/ppermute | solution.py:356
  176.4 1.2 copy-start.17

commit v3 on v2

--- a/solution.py
+++ b/solution.py
@@ -22,14 +22,14 @@
     return lax.dot_general(left, right, ((dims[:1], dims[1:]), ((), ())), preferred_element_type=F32)
 
 
-def merge_kernel(at_ref, base_ref, wide_ref, pick_ref, out_ref, zt_ref, low_ref, first_ref):
+def merge_kernel(at_ref, base_ref, wide_ref, pair_ref, out_ref, z_ref, low_ref, first_ref):
     step = pl.program_id(0)
     ah, al = split(out_ref[...])
     low = contract(wide_ref[...], jnp.concatenate([ah, al, ah, al], 0), (1, 0))
     merged = base_ref[...].astype(F32) + low
     squares = jnp.sum(merged * merged, axis=0, keepdims=True)
     low_ref[...] = merged.astype(BF16)
-    ranks = zt_ref[pl.ds(pl.multiple_of(step * 16, 16), 16), :]
+    ranks = z_ref[pl.ds(pl.multiple_of(step * 16, 16), 16), :] + z_ref[pl.ds(pl.multiple_of(64 + step * 16, 16), 16), :]
     for k in range(4):
         member = 4 * step + k
         for q in range(4):
@@ -38,18 +38,19 @@
             first_ref[member, 16 + r : 17 + r, :] = squares[:, 256 * k + 128 * r : 256 * k + 128 * r + 128]
         first_ref[member, 22:24, :] = jnp.zeros((2, 128), F32)
 
-    @pl.when(lax.rem(step, 2) == at_ref[0])
-    def _():
-        span = pl.ds(pl.multiple_of(at_ref[1] * 128, 128), 128)
-        both = contract(pick_ref[...], low_ref[:, span], (1, 0))
+    @pl.when(lax.rem(step, 2) == at_ref[25])
+    def _():
+        span = pl.ds(pl.multiple_of(at_ref[26] * 128, 128), 128)
+        rows = [pair_ref[pl.ds(pl.multiple_of(64 * k + at_ref[28] * 32, 32), 32), :] for k in range(2)]
+        both = contract(jnp.concatenate(rows, 0), low_ref[:, span], (1, 0))
         block = both[:32] + both[32:]
         for k in range(8):
             first_ref[2 * k + step // 2, 18:22, :] = block[4 * k : 4 * k + 4]
 
 
-def merge(at, base, wide, pick, adapter_out, zt):
+def merge(at, base, wide, pair, adapter_out, z):
     rows, cols = base.shape
-    tokens = zt.shape[1]
+    tokens = z.shape[1]
     steps = cols // 1024
     tile = lambda i, c: (0, i)
     whole = lambda i, c: (0, 0)
@@ -62,9 +63,9 @@
             in_specs=[
                 pl.BlockSpec((rows, 1024), tile),
                 pl.BlockSpec((rows, 256), whole),
-                pl.BlockSpec((64, rows), whole),
+                pl.BlockSpec((128, rows), whole),
                 pl.BlockSpec((64, 1024), tile),
-                pl.BlockSpec((64, tokens), whole),
+                pl.BlockSpec((128, tokens), whole),
             ],
             out_specs=(
                 pl.BlockSpec((rows, 1024), tile),
@@ -73,7 +74,7 @@
         ),
         cost_estimate=pl.CostEstimate(flops=1400000000, bytes_accessed=7000000, transcendentals=0),
         name="merge",
-    )(at, base, wide, pick, adapter_out, zt)
+    )(at, base, wide, pair, adapter_out, z)
 
 
 def forward_kernel(at_ref, a_ref, b_ref, wa_ref, wb_ref, r4_ref, r3_ref, r2_ref, r1_ref, r0_ref, acts):
@@ -201,6 +202,7 @@
     def _():
         gao_ref[...] = sum_own[...]
         gap_ref[...] = sum_peer[...].astype(BF16)
+        low_ref[:, 40:48, :] = jnp.zeros((32, 8, 128), BF16)
         pair = jnp.concatenate(split(sum_y[...]), 0)
         for k, ref in enumerate((ato_ref, atp_ref)):
             both = contract(jnp.concatenate([ref[...], ref[...]], 1), pair, (1, 0)).T
@@ -222,7 +224,7 @@
         out_shape=(
             jax.ShapeDtypeStruct((tokens, feats), F32),
             jax.ShapeDtypeStruct((tokens, feats), BF16),
-            jax.ShapeDtypeStruct((32, 40, 128), BF16),
+            jax.ShapeDtypeStruct((32, 48, 128), BF16),
         ),
         grid_spec=pltpu.PrefetchScalarGridSpec(
             num_scalar_prefetch=1,
@@ -239,7 +241,7 @@
             out_specs=(
                 pl.BlockSpec((tokens, feats), whole),
                 pl.BlockSpec((tokens, feats), whole),
-                pl.BlockSpec((32, 40, 128), lambda i, c: (0, 0, 0)),
+                pl.BlockSpec((32, 48, 128), lambda i, c: (0, 0, 0)),
             ),
             scratch_shapes=[
                 pltpu.VMEM((tokens, feats), F32),
@@ -251,6 +253,30 @@
         cost_estimate=pl.CostEstimate(flops=3000000000, bytes_accessed=6000000, transcendentals=0),
         name="backward",
     )(at, scaled, w_own, w_peer, at_own, at_peer, second, adapter_out)
+
+
+def pack_kernel(got_ref, low_ref, o_ref):
+    slope = jnp.sum(got_ref[...], axis=0)
+    high, low = split(slope)
+    high, low = high.astype(F32), low.astype(F32)
+    none = jnp.zeros((6, 128), F32)
+    for k in range(16):
+        rows = jnp.concatenate([high[k : k + 1], low[k : k + 1], none], 0).astype(BF16)
+        o_ref[2 * k] = rows
+        o_ref[2 * k + 1] = rows
+
+
+def pack(got, low):
+    return pl.pallas_call(
+        pack_kernel,
+        out_shape=jax.ShapeDtypeStruct(low.shape, BF16),
+        grid=(1,),
+        in_specs=[pl.BlockSpec(got.shape, lambda i: (0, 0, 0)), pl.BlockSpec(memory_space=pl.ANY)],
+        out_specs=pl.BlockSpec((32, 8, 128), lambda i: (0, 5, 0)),
+        input_output_aliases={1: 0},
+        cost_estimate=pl.CostEstimate(flops=20000, bytes_accessed=130000, transcendentals=0),
+        name="pack",
+    )(got, low)
 
 
 def combine_kernel(at_ref, got_ref, second_ref, norm_ref, size_ref, o_ref):
@@ -261,11 +287,11 @@
     q = jnp.concatenate([second_ref[2 * k + at_ref[0], 18:22, :] for k in range(8)], 0)
     high, low = split(mag)
     out = (total[0:32] + q * coeff).astype(BF16)
-    o_ref[...] = jnp.broadcast_to(jnp.concatenate([out, total[32:40].astype(BF16), high, low], 0), o_ref.shape)
+    o_ref[...] = jnp.broadcast_to(jnp.concatenate([out, total[32:40].astype(BF16), high, low, jnp.zeros((6, 128), BF16)], 0), o_ref.shape)
 
 
 def combine(at, got, second, norm, size):
-    column = pl.BlockSpec((1, 128), lambda i, c: (0, c[0] * 16 + c[1]))
+    column = pl.BlockSpec((1, 128), lambda i, c: (0, c[0] * 16 + c[27]))
     block = pl.BlockSpec(got.shape, lambda i, c: (0, 0, 0))
     return pl.pallas_call(
         combine_kernel,
@@ -342,12 +368,35 @@
     )(at, got, w_own, w_peer, adapter_out, norm, size)
 
 
+def join_kernel(at_ref, mine_ref, other_ref, out_ref, mag_ref):
+    cols = out_ref.shape[1] // 2
+    for ref, side in ((mine_ref, at_ref[0]), (other_ref, 1 - at_ref[0])):
+        span = pl.ds(pl.multiple_of(side * cols, cols), cols)
+        out_ref[:, span] = ref[0:64, 0:cols]
+        mag_ref[:, span] = ref[64:72, 0:cols]
+
+
+def join(at, mine, other):
+    block = pl.BlockSpec(mine.shape, lambda i, c: (0, 0))
+    return pl.pallas_call(
+        join_kernel,
+        out_shape=(jax.ShapeDtypeStruct((64, 4096), F32), jax.ShapeDtypeStruct((8, 4096), F32)),
+        grid_spec=pltpu.PrefetchScalarGridSpec(
+            num_scalar_prefetch=1,
+            grid=(1,),
+            in_specs=[block, block],
+            out_specs=(pl.BlockSpec((64, 4096), lambda i, c: (0, 0)), pl.BlockSpec((8, 4096), lambda i, c: (0, 0))),
+        ),
+        cost_estimate=pl.CostEstimate(flops=100000, bytes_accessed=2500000, transcendentals=0),
+        name="join",
+    )(at, mine, other)
+
+
 def program(activations, base_weight, adapter_in, adapter_out, magnitude, cotangent):
     core = lax.axis_index("core")
     y = lax.axis_index("y")
     replica = lax.axis_index(REPLICA)
     sides = lax.axis_size("y")
-    replicas = lax.axis_size(REPLICA)
     half = adapter_out.shape[1] // 2
     hops = [(2 * s, 2 * ((s + 1) % sides)) for s in range(sides)]
     hops += [(2 * s + 1, 2 * ((s - 1) % sides) + 1) for s in range(sides)]
@@ -384,7 +433,9 @@
         chip = lax.rem(y + sign * k + sides, sides) * 2
         rows += [chip + core, chip + 1 - core]
     rows += [2 * y + core]
-    at = jnp.stack([core] + near + far + rows).astype(jnp.int32)
+    window, part = replica // 2, lax.rem(replica, 2)
+    at = [core] + near + far + rows + [window // 8, lax.rem(window, 8), window, part]
+    at = jnp.stack(at).astype(jnp.int32)
 
     act_peer = swap(activations)
     high = lax.reduce_precision(adapter_in, 8, 7)
@@ -392,12 +443,9 @@
     high = high.astype(BF16)
     wide = jnp.concatenate([high, high, rest, rest], 1)
     pair = jnp.concatenate([high.T, rest.T], 0)
-    window, part = replica // 2, lax.rem(replica, 2)
-    pick = jnp.concatenate([lax.dynamic_slice_in_dim(pair, 64 * k + part * 32, 32, 0) for k in range(2)], 0)
     at_own = activations.T
     z = contract(pair, at_own, (1, 0))
-    place = jnp.stack([window // 8, lax.rem(window, 8)]).astype(jnp.int32)
-    w_own, first = merge(place, base_weight, wide, pick, adapter_out, z[:64] + z[64:])
+    w_own, first = merge(at, base_weight, wide, pair, adapter_out, z)
     w_peer = swap(w_own)
     first = jnp.sum(exchange(first, TENSOR), axis=0)
     second = spread(first, TENSOR)
@@ -418,21 +466,16 @@
 
     at_peer = act_peer.T
     scaled, slope = slopes(at, block, (hop1, hop2, hop3), hop4, crossed, col_scale, w_own, w_peer, at_own, at_peer)
-    slope = jnp.sum(exchange(slope, "y"), axis=0)
-    high = lax.reduce_precision(slope, 8, 7)
-    slope = jnp.stack([high, slope - high], 1).astype(BF16)
-    slope = jnp.broadcast_to(slope[:, None], (16, 2, 2, 128)).reshape(replicas, 2, 128)
+    slope = exchange(slope, "y")
     act_own, act_send, low = backward(at, scaled, w_own, w_peer, at_own, at_peer, second, adapter_out)
-    low = exchange(jnp.concatenate([low, slope], 1), REPLICA)
-    place = jnp.stack([core, window]).astype(jnp.int32)
-    low = exchange(combine(place, low, second, col_norm, magnitude), REPLICA)
+    low = exchange(pack(slope, low), REPLICA)
+    low = exchange(combine(at, low, second, col_norm, magnitude), REPLICA)
     act_add = swap(act_send)
     payload, in_own = finish(at, low, w_own, w_peer, adapter_out, col_norm, magnitude)
     last = swap(payload)
     grad_in = (in_own + last[:64, half:]).T
-    join = lambda a, b: jnp.where(core == 0, jnp.concatenate([a, b], 1), jnp.concatenate([b, a], 1))
-    grad_out = join(payload[:64, :half], last[:64, :half])
-    grad_mag = join(payload[64:65, :half], last[64:65, :half]).reshape(2 * half)
+    grad_out, grad_mag = join(at, payload, last)
+    grad_mag = grad_mag[0]
     grad_act = (act_own + act_add.astype(F32)).astype(BF16)
     return (output, grad_act, grad_in, grad_out, grad_mag)
 

time: 180 us -> 167 us (0.928)
  waiting for transfers between devices: 32.3 us -> 17 us
  other arithmetic: 10.8 us -> 6.16 us
  Pallas kernels: 31.8 us -> 36.3 us
  local copies, waits for them, and re-layouts: 11.6 us -> 13.6 us
    ppermute x8, waiting for transfers between devices: 15.5 us -> 4.11 us  [shift(): return lax.ppermute(value, TENSOR, hops)]
    pallas_call x0 -> x2, Pallas kernels: none -> 4.53 us  [the longest x1 3.02 us: join(): pl.pallas_call(join_kernel, out_shape=(jax.ShapeDtypeStruct((64, 4096), F...]
    all_to_all x5, waiting for transfers between devices: 13.7 us -> 10.1 us  [exchange(): return lax.all_to_all(value, axes, 0, 0)]
    ppermute x7, starting transfers between devices: 33.9 us -> 30.9 us  [swap(): return lax.ppermute(value, 'core', [(0, 1), (1, 0)])]
    all_to_all x5, starting transfers between devices: 29 us -> 31.5 us  [exchange(): return lax.all_to_all(value, axes, 0, 0)]
    concatenate x2 -> x0, other arithmetic: 2.46 us -> none  [the longest x1 1.84 us: program(): low = exchange(jnp.concatenate([low, slope], 1), REPLICA)]
    unnamed x44 -> x48, local copies, waits for them, and re-layouts: 3.79 us -> 6.23 us
  transfers between devices with their start and end apart: 20 -> 20, of which waited for: 8 -> 6; matrix products, arithmetic and copies ran while one was open for 7% -> 5% of each run, Pallas kernels for 15% -> 17%
where the time goes in v3:
time: 167 us; the launch traced here: 165 us
  starting transfers between devices  89.3 us (53%)
  Pallas kernels  36.3 us (22%)
  waiting for transfers between devices  17 us (10%)
  local copies, waits for them, and re-layouts  13.6 us (8%)
  other arithmetic  6.16 us (4%)
  matrix products  1.88 us (1%)
    all_to_all x5, starting transfers between devices, exchange(): return lax.all_to_all(value, axes, 0, 0)  31.5 us
    ppermute x7, starting transfers between devices, swap(): return lax.ppermute(value, 'core', [(0, 1), (1, 0)])  30.9 us
    ppermute x8, starting transfers between devices, shift(): return lax.ppermute(value, TENSOR, hops)  26.9 us
    all_to_all x5, waiting for transfers between devices, exchange(): return lax.all_to_all(value, axes, 0, 0)  10.1 us
    pallas_call x1, Pallas kernels, backward(): pl.pallas_call(backward_kernel, out_shape=(jax.ShapeDtypeStruct((tokens,...  7.72 us
    unnamed x48, local copies, waits for them, and re-layouts  6.23 us
    pallas_call x1, Pallas kernels, forward(): pl.pallas_call(forward_kernel, out_shape=tuple((jax.ShapeDtypeStruct((r,...  6.17 us
    pallas_call x1, Pallas kernels, merge(): pl.pallas_call(merge_kernel, out_shape=(jax.ShapeDtypeStruct((rows, cols)...  5.79 us
  transfers between devices with their start and end apart: 20, of which 6 were waited for; matrix products, arithmetic and copies ran while one was open for 5% of the time, Pallas kernels for 17%

profile of v3, /device:TPU:1, one launch (start us, length us, event | category | flops | bytes accessed | tf_op | source)
XLA Modules:
  0.0 165.5 jit_solution(17713718286281824681)
XLA Ops:
  0.7 0.9 reduce-precision_convert_fusion
  1.6 0.6 pad_maximum_fusion.3.pair_ref
  2.2 1.9 %fusion.4.z_ref = f32[128,512]{1,0:T(8,128)} fusion(bf16[512,256]{1,0:T(8,128)(2,1)} %a_ref.2, bf16[64,256]{1,0:T(8,128)(2,1)S(1)} %bitcast.38, bf16[64,256]{1,0:T(8,128)(2,1)S(1)} %bitcast.36), kind=kOutput, calls=%fused_computation.24 | convolution fusion | flops 33685504 | bytes 589824 | tf_op jit(solution)/shard_map/dot_general | solution.py:22
  4.1 0.8 copy.13.wide_ref
  4.9 0.7 stack.101.at_ref
  5.6 5.8 %merge.1 = (bf16[256,4096]{1,0:T(8,128)(2,1)}, f32[16,24,128]{2,1,0:T(8,128)}) custom-call(s32[29]{0:T(128)} %stack.101.at_ref, bf16[256,4096]{1,0:T(8,128)(2,1)} %base_ref.1, bf16[256,256]{1,0:T(8,128)(2,1)} %copy.13.wide_ref, bf16[128,256]{1,0:T(8,128)(2,1)} %pad_maximum_fusion.3.pair_ref, f32[64,4096]{1,0:T(8,128)} %a_ref.3, f32[128,512]{1,0:T(8,128)} %fusion.4.z_ref), custom_call_target="tpu_custom_call" | custom-call | flops 1400000000 | bytes 7000000 | tf_op jit(solution)/shard_map/merge/pallas_call | solution.py:57
  11.4 8.7 %collective-permute-start.1 = (bf16[256,4096]{1,0:T(8,128)(2,1)}, bf16[256,4096]{1,0:T(8,128)(2,1)S(1)}, u32[]{:S(2)}, u32[]{:S(2)}) collective-permute-start(bf16[256,4096]{1,0:T(8,128)(2,1)} %get-tuple-element.21.wa_ref.wo_ref), channel_id=1, source_target_pairs={{0,1},{1,0},{2,3},{3,2},{4,5},{5,4},{6,7},{7,6},{8,9},{9,8},{10,11... | collective-permute-start | bytes 6291464 | tf_op jit(solution)/shard_map/ppermute | solution.py:405
  20.1 1.9 %collective-permute-start.7 = (bf16[32,4096]{1,0:T(8,128)(2,1)S(1)}, bf16[32,4096]{1,0:T(8,128)(2,1)S(1)}, u32[]{:S(2)}, u32[]{:S(2)}) collective-permute-start(bf16[32,4096]{1,0:T(8,128)(2,1)S(1)} %copy-done.12), channel_id=1, source_target_pairs={{0,1},{1,0},{2,3},{3,2},{4,5},{5,4},{6,7},{7,6},{8,9},{9,8},{10,11... | collective-permute-start | bytes 786440 | tf_op jit(solution)/shard_map/ppermute | solution.py:405
  22.0 0.7 constant_dynamic-update-slice_fusion.1
  22.8 1.7 %collective-permute-done.7 = bf16[32,4096]{1,0:T(8,128)(2,1)S(1)} collective-permute-done((bf16[32,4096]{1,0:T(8,128)(2,1)S(1)}, bf16[32,4096]{1,0:T(8,128)(2,1)S(1)}, u32[]{:S(2)}, u32[]{:S(2)}) %collective-permute-start.7) | collective-permute-done | bytes 262176 | tf_op jit(solution)/shard_map/ppermute | solution.py:405
  24.5 0.7 constant_dynamic-update-slice_fusion.block_ref
  25.2 1.9 %collective-permute-start.8 = (bf16[64,4096]{1,0:T(8,128)(2,1)}, bf16[64,4096]{1,0:T(8,128)(2,1)S(1)}, u32[]{:S(2)}, u32[]{:S(2)}) collective-permute-start(bf16[64,4096]{1,0:T(8,128)(2,1)} %constant_dynamic-update-slice_fusion.block_ref), channel_id=1, source_target_pairs={{0,2},{2,4},{4,6},{6,8},{8,10},{10,12},{12,14},{14,0},{1,15},{3,1}... | collective-permute-start | bytes 1572872 | tf_op jit(solution)/shard_map/ppermute | solution.py:408
  27.1 0.1 copy.12
  27.3 2.3 %collective-permute-start = (bf16[512,256]{0,1:T(8,128)(2,1)S(1)}, bf16[512,256]{0,1:T(8,128)(2,1)S(1)}, u32[]{:S(2)}, u32[]{:S(2)}) collective-permute-start(bf16[512,256]{0,1:T(8,128)(2,1)S(1)} %copy.12), channel_id=1, source_target_pairs={{0,1},{1,0},{2,3},{3,2},{4,5},{5,4},{6,7},{7,6},{8,9},{9,8},{10,11... | collective-permute-start | bytes 786440 | tf_op jit(solution)/shard_map/ppermute | solution.py:405
  29.5 4.6 %all-to-all-start = ((f32[16,24,128]{2,1,0:T(8,128)}), f32[16,24,128]{2,1,0:T(8,128)S(1)}, u32[]{:S(2)}, u32[]{:S(2)}) async-start(f32[16,24,128]{2,1,0:T(8,128)} %get-tuple-element.27), calls=%async_computation | async-start | bytes 393216 | tf_op jit(solution)/shard_map/all_to_all | solution.py:411
  34.2 1.4 collective-permute-done.8.hop1_ref
  35.6 3.1 %collective-permute-start.9 = (bf16[64,4096]{1,0:T(8,128)(2,1)S(1)}, bf16[64,4096]{1,0:T(8,128)(2,1)}, u32[]{:S(2)}, u32[]{:S(2)}) collective-permute-start(bf16[64,4096]{1,0:T(8,128)(2,1)S(1)} %collective-permute-done.8.hop1_ref), channel_id=1, source_target_pairs={{0,2},{2,4},{4,6},{6,8},{8,10},{10,12},{12,14},{14,0},{1,15},{3,1}... | collective-permute-start | bytes 1572872 | tf_op jit(solution)/shard_map/ppermute | solution.py:408
  38.7 0.8 copy.14.b_ref
  39.6 1.4 copy-done
  40.9 6.2 %forward.1 = (bf16[32,4096]{1,0:T(8,128)(2,1)}, f32[64,4096]{1,0:T(8,128)}, f32[64,4096]{1,0:T(8,128)}, f32[64,4096]{1,0:T(8,128)}, f32[32,4096]{1,0:T(8,128)}) custom-call(s32[29]{0:T(128)} %stack.101.at_ref, bf16[512,256]{1,0:T(8,128)(2,1)} %a_ref.2, bf16[512,256]{1,0:T(8,128)(2,1)} %copy.14.b_ref, bf16[256,4096]{1,0:T(8,128)(2,1)} %get-tuple-element.21.wa_ref.wo_ref, ...), custom_call_target="tpu_custom_call" | custom-call | flops 1073741824 | bytes 5000000 | tf_op jit(solution)/shard_map/forward/pallas_call | solution.py:103
  47.1 0.0 copy-start.8
  47.1 3.2 %collective-permute-start.2 = (bf16[32,4096]{1,0:T(8,128)(2,1)}, bf16[32,4096]{1,0:T(8,128)(2,1)S(1)}, u32[]{:S(2)}, u32[]{:S(2)}) collective-permute-start(bf16[32,4096]{1,0:T(8,128)(2,1)} %get-tuple-element.26), channel_id=1, source_target_pairs={{0,2},{2,4},{4,6},{6,8},{8,10},{10,12},{12,14},{14,0},{1,15},{3,1}... | collective-permute-start | bytes 786440 | tf_op jit(solution)/shard_map/ppermute | solution.py:408
  50.4 0.7 broadcast_in_dim.3
  51.1 6.1 %all-to-all-start.1 = ((f32[16,24,128]{2,1,0:T(8,128)}), f32[16,24,128]{2,1,0:T(8,128)S(1)}, u32[]{:S(2)}, u32[]{:S(2)}) async-start(f32[16,24,128]{2,1,0:T(8,128)} %broadcast_in_dim.3), calls=%async_computation.1 | async-start | bytes 393216 | tf_op jit(solution)/shard_map/all_to_all | solution.py:411
  57.2 4.5 %collective-permute-start.10 = (bf16[64,4096]{1,0:T(8,128)(2,1)}, bf16[64,4096]{1,0:T(8,128)(2,1)S(1)}, u32[]{:S(2)}, u32[]{:S(2)}) collective-permute-start(bf16[64,4096]{1,0:T(8,128)(2,1)} %collective-permute-done.9.hop2_ref), channel_id=1, source_target_pairs={{0,2},{2,4},{4,6},{6,8},{8,10},{10,12},{12,14},{14,0},{1,15},{3,1}... | collective-permute-start | bytes 1572872 | tf_op jit(solution)/shard_map/ppermute | solution.py:408
  61.7 1.1 slice.45
  62.9 3.2 %collective-permute-start.3 = (bf16[64,4096]{1,0:T(8,128)(2,1)S(1)}, bf16[64,4096]{1,0:T(8,128)(2,1)S(1)}, u32[]{:S(2)}, u32[]{:S(2)}) collective-permute-start(bf16[64,4096]{1,0:T(8,128)(2,1)S(1)} %pad_maximum_fusion.1), channel_id=1, source_target_pairs={{0,2},{2,4},{4,6},{6,8},{8,10},{10,12},{12,14},{14,0},{1,15},{3,1}... | collective-permute-start | bytes 1572872 | tf_op jit(solution)/shard_map/ppermute | solution.py:408
  66.1 1.0 constant_dynamic-slice_fusion.1
  67.1 2.7 %collective-permute-done.10.hop3_ref = bf16[64,4096]{1,0:T(8,128)(2,1)S(1)} collective-permute-done((bf16[64,4096]{1,0:T(8,128)(2,1)}, bf16[64,4096]{1,0:T(8,128)(2,1)S(1)}, u32[]{:S(2)}, u32[]{:S(2)}) %collective-permute-start.10) | collective-permute-done | bytes 524320 | tf_op jit(solution)/shard_map/ppermute | solution.py:408
  69.8 0.1 pad_maximum_fusion
  69.9 3.5 %collective-permute-start.12 = (bf16[192,2048]{1,0:T(8,128)(2,1)S(1)}, bf16[192,2048]{1,0:T(8,128)(2,1)S(1)}, u32[]{:S(2)}, u32[]{:S(2)}) collective-permute-start(bf16[192,2048]{1,0:T(8,128)(2,1)S(1)} %pad_maximum_fusion), channel_id=1, source_target_pairs={{0,1},{1,0},{2,3},{3,2},{4,5},{5,4},{6,7},{7,6},{8,9},{9,8},{10,11... | collective-permute-start | bytes 2359304 | tf_op jit(solution)/shard_map/ppermute | solution.py:405
  73.4 3.1 %collective-permute-start.11 = (bf16[64,2048]{1,0:T(8,128)(2,1)S(1)}, bf16[64,2048]{1,0:T(8,128)(2,1)S(1)}, u32[]{:S(2)}, u32[]{:S(2)}) collective-permute-start(bf16[64,2048]{1,0:T(8,128)(2,1)S(1)} %get-tuple-element.38), channel_id=1, source_target_pairs={{0,2},{2,4},{4,6},{6,8},{8,10},{10,12},{12,14},{14,0},{1,15},{3,1}... | collective-permute-start | bytes 786440 | tf_op jit(solution)/shard_map/ppermute | solution.py:408
  76.6 0.1 add_convert_fusion.1
  76.7 3.2 %collective-permute-start.4 = (bf16[64,4096]{1,0:T(8,128)(2,1)S(1)}, bf16[64,4096]{1,0:T(8,128)(2,1)S(1)}, u32[]{:S(2)}, u32[]{:S(2)}) collective-permute-start(bf16[64,4096]{1,0:T(8,128)(2,1)S(1)} %add_convert_fusion.1), channel_id=1, source_target_pairs={{0,2},{2,4},{4,6},{6,8},{8,10},{10,12},{12,14},{14,0},{1,15},{3,1}... | collective-permute-start | bytes 1572872 | tf_op jit(solution)/shard_map/ppermute | solution.py:408
  79.9 0.7 fusion.2
  80.6 0.6 div.26
  81.2 0.7 copy-done.22
  81.9 0.3 copy-done.20
  82.1 5.2 %slopes.1 = (bf16[512,2048]{1,0:T(8,128)(2,1)}, f32[8,16,128]{2,1,0:T(8,128)}) custom-call(s32[29]{0:T(128)} %stack.101.at_ref, bf16[64,4096]{1,0:T(8,128)(2,1)} %constant_dynamic-update-slice_fusion.block_ref, bf16[64,4096]{1,0:T(8,128)(2,1)} %copy-done.17, bf16[64,4096]{1,0:T(8,128)(2,1)} %collective-permute-done.9.hop2_ref, bf16[64,4096]{1,0:T(8,128)(2,1)} %copy-done.9, ...), custom_call_target="tpu_custom_call" | custom-call | flops 2200000000 | bytes 8000000 | tf_op jit(solution)/shard_map/slopes/pallas_call | solution.py:143
  87.4 5.1 %all-to-all-start.2 = ((f32[8,16,128]{2,1,0:T(8,128)}), f32[8,16,128]{2,1,0:T(8,128)S(1)}, u32[]{:S(2)}, u32[]{:S(2)}) async-start(f32[8,16,128]{2,1,0:T(8,128)} %get-tuple-element.31), calls=%async_computation.2 | async-start | bytes 131072 | tf_op jit(solution)/shard_map/all_to_all | solution.py:411
  92.5 7.7 %backward.1 = (f32[512,256]{1,0:T(8,128)}, bf16[512,256]{1,0:T(8,128)(2,1)}, bf16[32,48,128]{2,1,0:T(8,128)(2,1)}) custom-call(s32[29]{0:T(128)} %stack.101.at_ref, bf16[512,2048]{1,0:T(8,128)(2,1)} %get-tuple-element.28.scaled_ref, bf16[256,4096]{1,0:T(8,128)(2,1)} %get-tuple-element.21.wa_ref.wo_ref, bf16[256,4096]{1,0:T(8,128)(2,1)} %copy-done, ...), custom_call_target="tpu_custom_call" | custom-call | flops 3000000000 | bytes 6000000 | tf_op jit(solution)/shard_map/backward/pallas_call | solution.py:222
  100.2 0.0 copy-start.15
  100.2 0.6 copy-done.15
  100.8 1.5 pack.1
  102.3 9.8 %all-to-all-start.3 = ((bf16[32,48,128]{2,1,0:T(8,128)(2,1)}), bf16[32,48,128]{2,1,0:T(8,128)(2,1)S(1)}, u32[]{:S(2)}, u32[]{:S(2)}) async-start(bf16[32,48,128]{2,1,0:T(8,128)(2,1)} %pack.1), calls=%async_computation.3 | async-start | bytes 786432 | tf_op jit(solution)/shard_map/all_to_all | solution.py:411
  112.2 0.1 add_convert_fusion
  112.3 4.7 %collective-permute-start.5 = (bf16[64,4096]{1,0:T(8,128)(2,1)S(1)}, bf16[64,4096]{1,0:T(8,128)(2,1)S(1)}, u32[]{:S(2)}, u32[]{:S(2)}) collective-permute-start(bf16[64,4096]{1,0:T(8,128)(2,1)S(1)} %add_convert_fusion), channel_id=1, source_target_pairs={{0,2},{2,4},{4,6},{6,8},{8,10},{10,12},{12,14},{14,0},{1,15},{3,1}... | collective-permute-start | bytes 1572872 | tf_op jit(solution)/shard_map/ppermute | solution.py:408
  117.0 6.6 %all-to-all-done.3.got_ref = bf16[32,48,128]{2,1,0:T(8,128)(2,1)S(1)} async-done(((bf16[32,48,128]{2,1,0:T(8,128)(2,1)}), bf16[32,48,128]{2,1,0:T(8,128)(2,1)S(1)}, u32[]{:S(2)}, u32[]{:S(2)}) %all-to-all-start.3) | async-done | bytes 393248 | tf_op jit(solution)/shard_map/all_to_all | solution.py:411
  123.6 0.8 copy-done.3
  124.4 2.6 %combine.1 = bf16[32,48,128]{2,1,0:T(8,128)(2,1)} custom-call(s32[29]{0:T(128)} %stack.101.at_ref, bf16[32,48,128]{2,1,0:T(8,128)(2,1)} %copy-done.3, f32[16,24,128]{2,1,0:T(8,128)} %copy-done.6, f32[1,4096]{1,0:T(1,128)} %bitcast.45, f32[1,4096]{1,0:T(1,128)} %bitcast.43), custom_call_target="tpu_custom_call" | custom-call | flops 2000000 | bytes 700000 | tf_op jit(solution)/shard_map/combine/pallas_call | solution.py:296
  127.0 5.8 %all-to-all-start.4 = ((bf16[32,48,128]{2,1,0:T(8,128)(2,1)}), bf16[32,48,128]{2,1,0:T(8,128)(2,1)S(1)}, u32[]{:S(2)}, u32[]{:S(2)}) async-start(bf16[32,48,128]{2,1,0:T(8,128)(2,1)} %combine.1), calls=%async_computation.4 | async-start | bytes 786432 | tf_op jit(solution)/shard_map/all_to_all | solution.py:411
  132.9 5.2 %collective-permute-start.13 = (bf16[512,256]{1,0:T(8,128)(2,1)S(1)}, bf16[512,256]{1,0:T(8,128)(2,1)S(1)}, u32[]{:S(2)}, u32[]{:S(2)}) collective-permute-start(bf16[512,256]{1,0:T(8,128)(2,1)S(1)} %copy-done.21), channel_id=1, source_target_pairs={{0,1},{1,0},{2,3},{3,2},{4,5},{5,4},{6,7},{7,6},{8,9},{9,8},{10,11... | collective-permute-start | bytes 786440 | tf_op jit(solution)/shard_map/ppermute | solution.py:405
  138.1 1.9 %collective-permute-start.6 = (bf16[32,4096]{1,0:T(8,128)(2,1)S(1)}, bf16[32,4096]{1,0:T(8,128)(2,1)S(1)}, u32[]{:S(2)}, u32[]{:S(2)}) collective-permute-start(bf16[32,4096]{1,0:T(8,128)(2,1)S(1)} %slice.31), channel_id=1, source_target_pairs={{0,1},{1,0},{2,3},{3,2},{4,5},{5,4},{6,7},{7,6},{8,9},{9,8},{10,11... | collective-permute-start | bytes 786440 | tf_op jit(solution)/shard_map/ppermute | solution.py:405
  140.1 0.8 add_convert_fusion.2
  140.9 3.4 %all-to-all-done.4.got_ref = bf16[32,48,128]{2,1,0:T(8,128)(2,1)S(1)} async-done(((bf16[32,48,128]{2,1,0:T(8,128)(2,1)}), bf16[32,48,128]{2,1,0:T(8,128)(2,1)S(1)}, u32[]{:S(2)}, u32[]{:S(2)}) %all-to-all-start.4) | async-done | bytes 393248 | tf_op jit(solution)/shard_map/all_to_all | solution.py:411
  144.3 0.7 copy-done.2
  145.0 4.3 %finish.1 = (f32[72,2304]{1,0:T(8,128)}, f32[64,256]{1,0:T(8,128)}) custom-call(s32[29]{0:T(128)} %stack.101.at_ref, bf16[32,48,128]{2,1,0:T(8,128)(2,1)} %copy-done.2, bf16[256,4096]{1,0:T(8,128)(2,1)} %get-tuple-element.21.wa_ref.wo_ref, bf16[256,4096]{1,0:T(8,128)(2,1)} %copy-done, f32[64,4096]{1,0:T(8,128)} %a_ref.3, f32[1,4096]{1,0:T(1,128)} %bitcast.46, ...), custom_call_target="tpu_custom_call" | custom-call | flops 600000000 | bytes 3000000 | tf_op jit(solution)/shard_map/finish/pallas_call | solution.py:349
  149.3 7.3 %collective-permute-start.14 = (f32[72,2304]{1,0:T(8,128)}, f32[72,2304]{1,0:T(8,128)S(1)}, u32[]{:S(2)}, u32[]{:S(2)}) collective-permute-start(f32[72,2304]{1,0:T(8,128)} %get-tuple-element.34.mine_ref), channel_id=1, source_target_pairs={{0,1},{1,0},{2,3},{3,2},{4,5},{5,4},{6,7},{7,6},{8,9},{9,8},{10,11... | collective-permute-start | bytes 1990664 | tf_op jit(solution)/shard_map/ppermute | solution.py:405
  156.7 0.8 multiply_convert_fusion
  157.5 1.1 collective-permute-done.14.other_ref
  158.6 0.8 copy-done.7
  159.4 3.0 %join.1 = (f32[64,4096]{1,0:T(8,128)}, f32[8,4096]{1,0:T(8,128)}) custom-call(s32[29]{0:T(128)} %stack.101.at_ref, f32[72,2304]{1,0:T(8,128)} %get-tuple-element.34.mine_ref, f32[72,2304]{1,0:T(8,128)} %copy-done.7), custom_call_target="tpu_custom_call" | custom-call | flops 100000 | bytes 2500000 | tf_op jit(solution)/shard_map/join/pallas_call | solution.py:381
  162.5 1.5 slice.28
  164.0 1.5 fusion.1
  (58 shorter events, 0.3 us)
Async XLA Ops:
  5.6 14.5 %copy-start.12 = (bf16[32,4096]{1,0:T(8,128)(2,1)S(1)}, bf16[32,4096]{1,0:T(8,128)(2,1)}, u32[]{:S(2)}) copy-start(bf16[32,4096]{1,0:T(8,128)(2,1)} %param.11) | copy-start | bytes 786436
  5.6 21.5 %copy-start.1 = (bf16[512,256]{1,0:T(8,128)(2,1)S(1)}, bf16[512,256]{1,0:T(8,128)(2,1)}, u32[]{:S(2)}) copy-start(bf16[512,256]{1,0:T(8,128)(2,1)} %a_ref.2) | copy-start | bytes 786436
  11.4 28.2 %collective-permute-start.1 = (bf16[256,4096]{1,0:T(8,128)(2,1)}, bf16[256,4096]{1,0:T(8,128)(2,1)S(1)}, u32[]{:S(2)}, u32[]{:S(2)}) collective-permute-start(bf16[256,4096]{1,0:T(8,128)(2,1)} %get-tuple-element.21.wa_ref.wo_ref), channel_id=1, source_target_pairs={{0,1},{1,0},{2,3},{3,2},{4,5},{5,4},{6,7},{7,6},{8,9},{9,8},{10,11... | collective-permute-start | bytes 6291464 | tf_op jit(solution)/shard_map/ppermute | solution.py:405
  20.1 4.3 %collective-permute-start.7 = (bf16[32,4096]{1,0:T(8,128)(2,1)S(1)}, bf16[32,4096]{1,0:T(8,128)(2,1)S(1)}, u32[]{:S(2)}, u32[]{:S(2)}) collective-permute-start(bf16[32,4096]{1,0:T(8,128)(2,1)S(1)} %copy-done.12), channel_id=1, source_target_pairs={{0,1},{1,0},{2,3},{3,2},{4,5},{5,4},{6,7},{7,6},{8,9},{9,8},{10,11... | collective-permute-start | bytes 786440 | tf_op jit(solution)/shard_map/ppermute | solution.py:405
  25.2 10.4 %collective-permute-start.8 = (bf16[64,4096]{1,0:T(8,128)(2,1)}, bf16[64,4096]{1,0:T(8,128)(2,1)S(1)}, u32[]{:S(2)}, u32[]{:S(2)}) collective-permute-start(bf16[64,4096]{1,0:T(8,128)(2,1)} %constant_dynamic-update-slice_fusion.block_ref), channel_id=1, source_target_pairs={{0,2},{2,4},{4,6},{6,8},{8,10},{10,12},{12,14},{14,0},{1,15},{3,1}... | collective-permute-start | bytes 1572872 | tf_op jit(solution)/shard_map/ppermute | solution.py:408
  27.2 19.8 %copy-start.13 = (bf16[512,256]{0,1:T(8,128)(2,1)}, bf16[512,256]{0,1:T(8,128)(2,1)S(1)}, u32[]{:S(2)}) copy-start(bf16[512,256]{0,1:T(8,128)(2,1)S(1)} %copy.12) | copy-start | bytes 786436
  27.3 11.4 %collective-permute-start = (bf16[512,256]{0,1:T(8,128)(2,1)S(1)}, bf16[512,256]{0,1:T(8,128)(2,1)S(1)}, u32[]{:S(2)}, u32[]{:S(2)}) collective-permute-start(bf16[512,256]{0,1:T(8,128)(2,1)S(1)} %copy.12), channel_id=1, source_target_pairs={{0,1},{1,0},{2,3},{3,2},{4,5},{5,4},{6,7},{7,6},{8,9},{9,8},{10,11... | collective-permute-start | bytes 786440 | tf_op jit(solution)/shard_map/ppermute | solution.py:405
  29.5 20.8 %all-to-all-start = ((f32[16,24,128]{2,1,0:T(8,128)}), f32[16,24,128]{2,1,0:T(8,128)S(1)}, u32[]{:S(2)}, u32[]{:S(2)}) async-start(f32[16,24,128]{2,1,0:T(8,128)} %get-tuple-element.27), calls=%async_computation | async-start | bytes 393216 | tf_op jit(solution)/shard_map/all_to_all | solution.py:411
  35.6 31.5 %copy-start.17 = (bf16[64,4096]{1,0:T(8,128)(2,1)}, bf16[64,4096]{1,0:T(8,128)(2,1)S(1)}, u32[]{:S(2)}) copy-start(bf16[64,4096]{1,0:T(8,128)(2,1)S(1)} %collective-permute-done.8.hop1_ref) | copy-start | bytes 1572868
  35.6 21.6 %collective-permute-start.9 = (bf16[64,4096]{1,0:T(8,128)(2,1)S(1)}, bf16[64,4096]{1,0:T(8,128)(2,1)}, u32[]{:S(2)}, u32[]{:S(2)}) collective-permute-start(bf16[64,4096]{1,0:T(8,128)(2,1)S(1)} %collective-permute-done.8.hop1_ref), channel_id=1, source_target_pairs={{0,2},{2,4},{4,6},{6,8},{8,10},{10,12},{12,14},{14,0},{1,15},{3,1}... | collective-permute-start | bytes 1572872 | tf_op jit(solution)/shard_map/ppermute | solution.py:408
  38.7 8.4 %copy-start.14 = (bf16[512,256]{0,1:T(8,128)(2,1)}, bf16[512,256]{0,1:T(8,128)(2,1)S(1)}, u32[]{:S(2)}) copy-start(bf16[512,256]{0,1:T(8,128)(2,1)S(1)} %collective-permute-done) | copy-start | bytes 786436
  39.6 1.4 copy-start
  47.1 15.6 %copy-start.8 = (f32[64,4096]{1,0:T(8,128)S(1)}, f32[64,4096]{1,0:T(8,128)}, u32[]{:S(2)}) copy-start(f32[64,4096]{1,0:T(8,128)} %get-tuple-element.25) | copy-start | bytes 3145732
  47.1 15.6 %collective-permute-start.2 = (bf16[32,4096]{1,0:T(8,128)(2,1)}, bf16[32,4096]{1,0:T(8,128)(2,1)S(1)}, u32[]{:S(2)}, u32[]{:S(2)}) collective-permute-start(bf16[32,4096]{1,0:T(8,128)(2,1)} %get-tuple-element.26), channel_id=1, source_target_pairs={{0,2},{2,4},{4,6},{6,8},{8,10},{10,12},{12,14},{14,0},{1,15},{3,1}... | collective-permute-start | bytes 786440 | tf_op jit(solution)/shard_map/ppermute | solution.py:408
  51.1 28.8 %all-to-all-start.1 = ((f32[16,24,128]{2,1,0:T(8,128)}), f32[16,24,128]{2,1,0:T(8,128)S(1)}, u32[]{:S(2)}, u32[]{:S(2)}) async-start(f32[16,24,128]{2,1,0:T(8,128)} %broadcast_in_dim.3), calls=%async_computation.1 | async-start | bytes 393216 | tf_op jit(solution)/shard_map/all_to_all | solution.py:411
  57.2 12.6 %collective-permute-start.10 = (bf16[64,4096]{1,0:T(8,128)(2,1)}, bf16[64,4096]{1,0:T(8,128)(2,1)S(1)}, u32[]{:S(2)}, u32[]{:S(2)}) collective-permute-start(bf16[64,4096]{1,0:T(8,128)(2,1)} %collective-permute-done.9.hop2_ref), channel_id=1, source_target_pairs={{0,2},{2,4},{4,6},{6,8},{8,10},{10,12},{12,14},{14,0},{1,15},{3,1}... | collective-permute-start | bytes 1572872 | tf_op jit(solution)/shard_map/ppermute | solution.py:408
  62.9 13.7 %copy-start.5 = (f32[64,4096]{1,0:T(8,128)S(1)}, f32[64,4096]{1,0:T(8,128)}, u32[]{:S(2)}) copy-start(f32[64,4096]{1,0:T(8,128)} %get-tuple-element.24) | copy-start | bytes 3145732
  62.9 13.7 %collective-permute-start.3 = (bf16[64,4096]{1,0:T(8,128)(2,1)S(1)}, bf16[64,4096]{1,0:T(8,128)(2,1)S(1)}, u32[]{:S(2)}, u32[]{:S(2)}) collective-permute-start(bf16[64,4096]{1,0:T(8,128)(2,1)S(1)} %pad_maximum_fusion.1), channel_id=1, source_target_pairs={{0,2},{2,4},{4,6},{6,8},{8,10},{10,12},{12,14},{14,0},{1,15},{3,1}... | collective-permute-start | bytes 1572872 | tf_op jit(solution)/shard_map/ppermute | solution.py:408
  69.8 6.9 %copy-start.9 = (bf16[64,4096]{1,0:T(8,128)(2,1)}, bf16[64,4096]{1,0:T(8,128)(2,1)S(1)}, u32[]{:S(2)}) copy-start(bf16[64,4096]{1,0:T(8,128)(2,1)S(1)} %collective-permute-done.10.hop3_ref) | copy-start | bytes 1572868
  69.8 10.8 %copy-start.16 = (f32[4096]{0:T(1024)S(1)}, f32[4096]{0:T(1024)}, u32[]{:S(2)}) copy-start(f32[4096]{0:T(1024)} %param.10) | copy-start | bytes 49156
  69.9 11.3 %collective-permute-start.12 = (bf16[192,2048]{1,0:T(8,128)(2,1)S(1)}, bf16[192,2048]{1,0:T(8,128)(2,1)S(1)}, u32[]{:S(2)}, u32[]{:S(2)}) collective-permute-start(bf16[192,2048]{1,0:T(8,128)(2,1)S(1)} %pad_maximum_fusion), channel_id=1, source_target_pairs={{0,1},{1,0},{2,3},{3,2},{4,5},{5,4},{6,7},{7,6},{8,9},{9,8},{10,11... | collective-permute-start | bytes 2359304 | tf_op jit(solution)/shard_map/ppermute | solution.py:405
  73.4 7.7 %collective-permute-start.11 = (bf16[64,2048]{1,0:T(8,128)(2,1)S(1)}, bf16[64,2048]{1,0:T(8,128)(2,1)S(1)}, u32[]{:S(2)}, u32[]{:S(2)}) collective-permute-start(bf16[64,2048]{1,0:T(8,128)(2,1)S(1)} %get-tuple-element.38), channel_id=1, source_target_pairs={{0,2},{2,4},{4,6},{6,8},{8,10},{10,12},{12,14},{14,0},{1,15},{3,1}... | collective-permute-start | bytes 786440 | tf_op jit(solution)/shard_map/ppermute | solution.py:408
  76.7 35.5 %collective-permute-start.4 = (bf16[64,4096]{1,0:T(8,128)(2,1)S(1)}, bf16[64,4096]{1,0:T(8,128)(2,1)S(1)}, u32[]{:S(2)}, u32[]{:S(2)}) collective-permute-start(bf16[64,4096]{1,0:T(8,128)(2,1)S(1)} %add_convert_fusion.1), channel_id=1, source_target_pairs={{0,2},{2,4},{4,6},{6,8},{8,10},{10,12},{12,14},{14,0},{1,15},{3,1}... | collective-permute-start | bytes 1572872 | tf_op jit(solution)/shard_map/ppermute | solution.py:408
  79.9 7.5 %copy-start.6 = (f32[16,24,128]{2,1,0:T(8,128)}, f32[16,24,128]{2,1,0:T(8,128)S(1)}, u32[]{:S(2)}) copy-start(f32[16,24,128]{2,1,0:T(8,128)S(1)} %all-to-all-done.1.second_ref) | copy-start | bytes 589828
  81.2 0.7 copy-start.22
  81.2 1.0 copy-start.20
  87.4 12.8 %all-to-all-start.2 = ((f32[8,16,128]{2,1,0:T(8,128)}), f32[8,16,128]{2,1,0:T(8,128)S(1)}, u32[]{:S(2)}, u32[]{:S(2)}) async-start(f32[8,16,128]{2,1,0:T(8,128)} %get-tuple-element.31), calls=%async_computation.2 | async-start | bytes 131072 | tf_op jit(solution)/shard_map/all_to_all | solution.py:411
  100.2 12.0 %copy-start.4 = (f32[64,4096]{1,0:T(8,128)S(1)}, f32[64,4096]{1,0:T(8,128)}, u32[]{:S(2)}) copy-start(f32[64,4096]{1,0:T(8,128)} %get-tuple-element.23) | copy-start | bytes 3145732
  100.2 0.6 copy-start.15
  102.3 21.3 %all-to-all-start.3 = ((bf16[32,48,128]{2,1,0:T(8,128)(2,1)}), bf16[32,48,128]{2,1,0:T(8,128)(2,1)S(1)}, u32[]{:S(2)}, u32[]{:S(2)}) async-start(bf16[32,48,128]{2,1,0:T(8,128)(2,1)} %pack.1), calls=%async_computation.3 | async-start | bytes 786432 | tf_op jit(solution)/shard_map/all_to_all | solution.py:411
  112.2 20.7 %copy-start.21 = (bf16[512,256]{1,0:T(8,128)(2,1)S(1)}, bf16[512,256]{1,0:T(8,128)(2,1)}, u32[]{:S(2)}) copy-start(bf16[512,256]{1,0:T(8,128)(2,1)} %get-tuple-element.30) | copy-start | bytes 786436
  112.3 27.8 %copy-start.10 = (f32[512,256]{1,0:T(8,128)S(1)}, f32[512,256]{1,0:T(8,128)}, u32[]{:S(2)}) copy-start(f32[512,256]{1,0:T(8,128)} %get-tuple-element.29) | copy-start | bytes 1572868
  112.3 25.8 %collective-permute-start.5 = (bf16[64,4096]{1,0:T(8,128)(2,1)S(1)}, bf16[64,4096]{1,0:T(8,128)(2,1)S(1)}, u32[]{:S(2)}, u32[]{:S(2)}) collective-permute-start(bf16[64,4096]{1,0:T(8,128)(2,1)S(1)} %add_convert_fusion), channel_id=1, source_target_pairs={{0,2},{2,4},{4,6},{6,8},{8,10},{10,12},{12,14},{14,0},{1,15},{3,1}... | collective-permute-start | bytes 1572872 | tf_op jit(solution)/shard_map/ppermute | solution.py:408
  123.6 0.8 copy-start.3
  127.0 17.3 %all-to-all-start.4 = ((bf16[32,48,128]{2,1,0:T(8,128)(2,1)}), bf16[32,48,128]{2,1,0:T(8,128)(2,1)S(1)}, u32[]{:S(2)}, u32[]{:S(2)}) async-start(bf16[32,48,128]{2,1,0:T(8,128)(2,1)} %combine.1), calls=%async_computation.4 | async-start | bytes 786432 | tf_op jit(solution)/shard_map/all_to_all | solution.py:411
  132.9 7.2 %collective-permute-start.13 = (bf16[512,256]{1,0:T(8,128)(2,1)S(1)}, bf16[512,256]{1,0:T(8,128)(2,1)S(1)}, u32[]{:S(2)}, u32[]{:S(2)}) collective-permute-start(bf16[512,256]{1,0:T(8,128)(2,1)S(1)} %copy-done.21), channel_id=1, source_target_pairs={{0,1},{1,0},{2,3},{3,2},{4,5},{5,4},{6,7},{7,6},{8,9},{9,8},{10,11... | collective-permute-start | bytes 786440 | tf_op jit(solution)/shard_map/ppermute | solution.py:405
  138.1 18.5 %collective-permute-start.6 = (bf16[32,4096]{1,0:T(8,128)(2,1)S(1)}, bf16[32,4096]{1,0:T(8,128)(2,1)S(1)}, u32[]{:S(2)}, u32[]{:S(2)}) collective-permute-start(bf16[32,4096]{1,0:T(8,128)(2,1)S(1)} %slice.31), channel_id=1, source_target_pairs={{0,1},{1,0},{2,3},{3,2},{4,5},{5,4},{6,7},{7,6},{8,9},{9,8},{10,11... | collective-permute-start | bytes 786440 | tf_op jit(solution)/shard_map/ppermute | solution.py:405
  140.8 15.8 %copy-start.11 = (f32[32,4096]{1,0:T(8,128)S(1)}, f32[32,4096]{1,0:T(8,128)}, u32[]{:S(2)}) copy-start(f32[32,4096]{1,0:T(8,128)} %get-tuple-element.22) | copy-start | bytes 1572868
  140.8 15.8 %copy-start.19 = (f32[4096]{0:T(1024)S(1)}, f32[4096]{0:T(1024)}, u32[]{:S(2)}) copy-start(f32[4096]{0:T(1024)} %div.26) | copy-start | bytes 49156
  144.3 0.7 copy-start.2
  149.3 14.7 %copy-start.18 = (f32[64,256]{1,0:T(8,128)S(1)}, f32[64,256]{1,0:T(8,128)}, u32[]{:S(2)}) copy-start(f32[64,256]{1,0:T(8,128)} %get-tuple-element.33) | copy-start | bytes 196612
  149.3 9.3 %collective-permute-start.14 = (f32[72,2304]{1,0:T(8,128)}, f32[72,2304]{1,0:T(8,128)S(1)}, u32[]{:S(2)}, u32[]{:S(2)}) collective-permute-start(f32[72,2304]{1,0:T(8,128)} %get-tuple-element.34.mine_ref), channel_id=1, source_target_pairs={{0,1},{1,0},{2,3},{3,2},{4,5},{5,4},{6,7},{7,6},{8,9},{9,8},{10,11... | collective-permute-start | bytes 1990664 | tf_op jit(solution)/shard_map/ppermute | solution.py:405
  158.6 0.9 copy-start.7

commit v4 on v3

--- a/solution.py
+++ b/solution.py
@@ -368,28 +368,30 @@
     )(at, got, w_own, w_peer, adapter_out, norm, size)
 
 
-def join_kernel(at_ref, mine_ref, other_ref, out_ref, mag_ref):
+def join_kernel(at_ref, mine_ref, other_ref, own_ref, out_ref, mag_ref, in_ref):
     cols = out_ref.shape[1] // 2
     for ref, side in ((mine_ref, at_ref[0]), (other_ref, 1 - at_ref[0])):
         span = pl.ds(pl.multiple_of(side * cols, cols), cols)
         out_ref[:, span] = ref[0:64, 0:cols]
-        mag_ref[:, span] = ref[64:72, 0:cols]
-
-
-def join(at, mine, other):
+        mag_ref[:, span] = ref[64:65, 0:cols]
+    in_ref[...] = (own_ref[...] + other_ref[0:64, cols:]).T
+
+
+def join(at, mine, other, own):
     block = pl.BlockSpec(mine.shape, lambda i, c: (0, 0))
+    shapes = ((64, 4096), (1, 4096), (256, 64))
     return pl.pallas_call(
         join_kernel,
-        out_shape=(jax.ShapeDtypeStruct((64, 4096), F32), jax.ShapeDtypeStruct((8, 4096), F32)),
+        out_shape=tuple(jax.ShapeDtypeStruct(s, F32) for s in shapes),
         grid_spec=pltpu.PrefetchScalarGridSpec(
             num_scalar_prefetch=1,
             grid=(1,),
-            in_specs=[block, block],
-            out_specs=(pl.BlockSpec((64, 4096), lambda i, c: (0, 0)), pl.BlockSpec((8, 4096), lambda i, c: (0, 0))),
+            in_specs=[block, block, pl.BlockSpec(own.shape, lambda i, c: (0, 0))],
+            out_specs=tuple(pl.BlockSpec(s, lambda i, c: (0, 0)) for s in shapes),
         ),
         cost_estimate=pl.CostEstimate(flops=100000, bytes_accessed=2500000, transcendentals=0),
         name="join",
-    )(at, mine, other)
+    )(at, mine, other, own)
 
 
 def program(activations, base_weight, adapter_in, adapter_out, magnitude, cotangent):
@@ -437,14 +439,14 @@
     at = [core] + near + far + rows + [window // 8, lax.rem(window, 8), window, part]
     at = jnp.stack(at).astype(jnp.int32)
 
-    act_peer = swap(activations)
+    at_own = activations.T
+    at_peer = swap(at_own)
     high = lax.reduce_precision(adapter_in, 8, 7)
     rest = (adapter_in - high).astype(BF16)
     high = high.astype(BF16)
     wide = jnp.concatenate([high, high, rest, rest], 1)
     pair = jnp.concatenate([high.T, rest.T], 0)
-    at_own = activations.T
-    z = contract(pair, at_own, (1, 0))
+    z = contract(pair, activations, (1, 1))
     w_own, first = merge(at, base_weight, wide, pair, adapter_out, z)
     w_peer = swap(w_own)
     first = jnp.sum(exchange(first, TENSOR), axis=0)
@@ -453,10 +455,11 @@
     crossed = swap(jnp.concatenate([other(hop1), other(hop2), other(hop3)], 0))
 
     square_sum = second[:, 16:18].reshape(1, 2 * half)
-    col_norm = jnp.sqrt(square_sum + epsilon)
     magnitude = magnitude.reshape(1, 2 * half)
-    col_scale = magnitude / col_norm
-    r4, r3, r2, r1, r0 = forward(at, activations, act_peer, w_own, w_peer)
+    col_scale = magnitude / jnp.sqrt(square_sum + epsilon)
+    scaled, slope = slopes(at, block, (hop1, hop2, hop3), hop4, crossed, col_scale, w_own, w_peer, at_own, at_peer)
+    turned, slope = lax.optimization_barrier((at_peer, slope))
+    r4, r3, r2, r1, r0 = forward(at, activations, turned.T, w_own, w_peer)
     got = shift(r4).astype(F32)
     got = shift(jnp.concatenate([r3[:32] + got, r3[32:]], 0).astype(BF16)).astype(F32)
     got = shift((r2 + got).astype(BF16)).astype(F32)
@@ -464,18 +467,17 @@
     summed = r0 + got[:32].astype(F32) + swap(got[32:]).astype(F32)
     output = (summed * col_scale).astype(BF16)
 
-    at_peer = act_peer.T
-    scaled, slope = slopes(at, block, (hop1, hop2, hop3), hop4, crossed, col_scale, w_own, w_peer, at_own, at_peer)
     slope = exchange(slope, "y")
+    square_sum, slope = lax.optimization_barrier((square_sum, slope))
+    col_norm = jnp.sqrt(square_sum + epsilon)
     act_own, act_send, low = backward(at, scaled, w_own, w_peer, at_own, at_peer, second, adapter_out)
     low = exchange(pack(slope, low), REPLICA)
     low = exchange(combine(at, low, second, col_norm, magnitude), REPLICA)
     act_add = swap(act_send)
     payload, in_own = finish(at, low, w_own, w_peer, adapter_out, col_norm, magnitude)
     last = swap(payload)
-    grad_in = (in_own + last[:64, half:]).T
-    grad_out, grad_mag = join(at, payload, last)
-    grad_mag = grad_mag[0]
+    grad_out, grad_mag, grad_in = join(at, payload, last, in_own)
+    grad_mag = grad_mag.reshape(2 * half)
     grad_act = (act_own + act_add.astype(F32)).astype(BF16)
     return (output, grad_act, grad_in, grad_out, grad_mag)
 

time: 167 us -> 190 us (1.14)
  waiting for transfers between devices: 17 us -> 28.4 us
  starting transfers between devices: 89.3 us -> 100 us
  local copies, waits for them, and re-layouts: 13.6 us -> 15.7 us
    ppermute x8, waiting for transfers between devices: 4.11 us -> 17.9 us  [shift(): return lax.ppermute(value, TENSOR, hops)]
    ppermute x7, starting transfers between devices: 30.9 us -> 39.1 us  [swap(): return lax.ppermute(value, 'core', [(0, 1), (1, 0)])]
    ppermute x8, starting transfers between devices: 26.9 us -> 34.2 us  [shift(): return lax.ppermute(value, TENSOR, hops)]
    all_to_all x5, starting transfers between devices: 31.5 us -> 27.1 us  [exchange(): return lax.all_to_all(value, axes, 0, 0)]
    unnamed x48 -> x37, local copies, waits for them, and re-layouts: 6.23 us -> 7.92 us
  transfers between devices with their start and end apart: 20 -> 20, of which waited for: 6 -> 10; matrix products, arithmetic and copies ran while one was open for 5% -> 7% of each run, Pallas kernels for 17% -> 12%
where the time goes in v4:
time: 190 us; the launch traced here: 188 us
  starting transfers between devices  100 us (53%)
  Pallas kernels  36.1 us (19%)
  waiting for transfers between devices  28.4 us (15%)
  local copies, waits for them, and re-layouts  15.7 us (8%)
  other arithmetic  5.77 us (3%)
    ppermute x7, starting transfers between devices, swap(): return lax.ppermute(value, 'core', [(0, 1), (1, 0)])  39.1 us
    ppermute x8, starting transfers between devices, shift(): return lax.ppermute(value, TENSOR, hops)  34.2 us
    all_to_all x5, starting transfers between devices, exchange(): return lax.all_to_all(value, axes, 0, 0)  27.1 us
    ppermute x8, waiting for transfers between devices, shift(): return lax.ppermute(value, TENSOR, hops)  17.9 us
    all_to_all x5, waiting for transfers between devices, exchange(): return lax.all_to_all(value, axes, 0, 0)  9.11 us
    unnamed x37, local copies, waits for them, and re-layouts  7.92 us
    pallas_call x1, Pallas kernels, backward(): pl.pallas_call(backward_kernel, out_shape=(jax.ShapeDtypeStruct((tokens,...  7.74 us
    pallas_call x1, Pallas kernels, forward(): pl.pallas_call(forward_kernel, out_shape=tuple((jax.ShapeDtypeStruct((r,...  6.18 us
  transfers between devices with their start and end apart: 20, of which 10 were waited for; matrix products, arithmetic and copies ran while one was open for 7% of the time, Pallas kernels for 12%

profile of v4, /device:TPU:1, one launch (start us, length us, event | category | flops | bytes accessed | tf_op | source)
XLA Modules:
  0.0 188.4 jit_solution(17290412596634653232)
XLA Ops:
  0.6 8.9 %collective-permute-start.1 = (bf16[32,4096]{1,0:T(8,128)(2,1)}, bf16[32,4096]{1,0:T(8,128)(2,1)S(1)}, u32[]{:S(2)}, u32[]{:S(2)}) collective-permute-start(bf16[32,4096]{1,0:T(8,128)(2,1)} %param.11), channel_id=1, source_target_pairs={{0,1},{1,0},{2,3},{3,2},{4,5},{5,4},{6,7},{7,6},{8,9},{9,8},{10,11... | collective-permute-start | bytes 786440 | tf_op jit(solution)/shard_map/ppermute | solution.py:407
  9.6 1.0 constant_dynamic-update-slice_fusion.1
  10.6 0.3 collective-permute-done.1
  10.9 1.9 %collective-permute-start.2 = (bf16[64,4096]{1,0:T(8,128)(2,1)S(1)}, bf16[64,4096]{1,0:T(8,128)(2,1)S(1)}, u32[]{:S(2)}, u32[]{:S(2)}) collective-permute-start(bf16[64,4096]{1,0:T(8,128)(2,1)S(1)} %constant_dynamic-update-slice_fusion.block_ref), channel_id=1, source_target_pairs={{0,2},{2,4},{4,6},{6,8},{8,10},{10,12},{12,14},{14,0},{1,15},{3,1}... | collective-permute-start | bytes 1572872 | tf_op jit(solution)/shard_map/ppermute | solution.py:410
  12.8 0.9 reduce-precision_convert_fusion
  13.7 0.7 copy.13.wide_ref
  14.5 0.6 stack.101.at_ref
  15.1 0.9 fusion.1.z_ref
  16.0 5.1 %collective-permute-done.2.hop1_ref = bf16[64,4096]{1,0:T(8,128)(2,1)S(1)} collective-permute-done((bf16[64,4096]{1,0:T(8,128)(2,1)S(1)}, bf16[64,4096]{1,0:T(8,128)(2,1)S(1)}, u32[]{:S(2)}, u32[]{:S(2)}) %collective-permute-start.2) | collective-permute-done | bytes 524320 | tf_op jit(solution)/shard_map/ppermute | solution.py:410
  21.1 2.8 %collective-permute-start.3 = (bf16[64,4096]{1,0:T(8,128)(2,1)S(1)}, bf16[64,4096]{1,0:T(8,128)(2,1)}, u32[]{:S(2)}, u32[]{:S(2)}) collective-permute-start(bf16[64,4096]{1,0:T(8,128)(2,1)S(1)} %collective-permute-done.2.hop1_ref), channel_id=1, source_target_pairs={{0,2},{2,4},{4,6},{6,8},{8,10},{10,12},{12,14},{14,0},{1,15},{3,1}... | collective-permute-start | bytes 1572872 | tf_op jit(solution)/shard_map/ppermute | solution.py:410
  24.0 0.6 pad_maximum_fusion.3.pair_ref
  24.6 5.6 %merge.1 = (bf16[256,4096]{1,0:T(8,128)(2,1)}, f32[16,24,128]{2,1,0:T(8,128)}) custom-call(s32[29]{0:T(128)} %stack.101.at_ref, bf16[256,4096]{1,0:T(8,128)(2,1)} %base_ref.1, bf16[256,256]{1,0:T(8,128)(2,1)} %copy.13.wide_ref, bf16[128,256]{1,0:T(8,128)(2,1)} %pad_maximum_fusion.3.pair_ref, f32[64,4096]{1,0:T(8,128)} %a_ref.3, f32[128,512]{1,0:T(8,128)} %fusion.1.z_ref), custom_call_target="tpu_custom_call" | custom-call | flops 1400000000 | bytes 7000000 | tf_op jit(solution)/shard_map/merge/pallas_call | solution.py:57
  30.2 3.4 %collective-permute-start.7 = (bf16[256,4096]{1,0:T(8,128)(2,1)}, bf16[256,4096]{1,0:T(8,128)(2,1)S(1)}, u32[]{:S(2)}, u32[]{:S(2)}) collective-permute-start(bf16[256,4096]{1,0:T(8,128)(2,1)} %get-tuple-element.27.wo_ref.wa_ref), channel_id=1, source_target_pairs={{0,1},{1,0},{2,3},{3,2},{4,5},{5,4},{6,7},{7,6},{8,9},{9,8},{10,11... | collective-permute-start | bytes 6291464 | tf_op jit(solution)/shard_map/ppermute | solution.py:407
  33.7 4.9 %collective-permute-start.4 = (bf16[64,4096]{1,0:T(8,128)(2,1)}, bf16[64,4096]{1,0:T(8,128)(2,1)S(1)}, u32[]{:S(2)}, u32[]{:S(2)}) collective-permute-start(bf16[64,4096]{1,0:T(8,128)(2,1)} %collective-permute-done.3.hop2_ref), channel_id=1, source_target_pairs={{0,2},{2,4},{4,6},{6,8},{8,10},{10,12},{12,14},{14,0},{1,15},{3,1}... | collective-permute-start | bytes 1572872 | tf_op jit(solution)/shard_map/ppermute | solution.py:410
  38.5 3.9 %all-to-all-start = ((f32[16,24,128]{2,1,0:T(8,128)}), f32[16,24,128]{2,1,0:T(8,128)S(1)}, u32[]{:S(2)}, u32[]{:S(2)}) async-start(f32[16,24,128]{2,1,0:T(8,128)} %get-tuple-element.26), calls=%async_computation | async-start | bytes 393216 | tf_op jit(solution)/shard_map/all_to_all | solution.py:413
  42.4 1.0 constant_dynamic-slice_fusion.2
  43.4 1.0 constant_dynamic-slice_fusion.1
  44.3 3.7 %collective-permute-done.4.hop3_ref = bf16[64,4096]{1,0:T(8,128)(2,1)S(1)} collective-permute-done((bf16[64,4096]{1,0:T(8,128)(2,1)}, bf16[64,4096]{1,0:T(8,128)(2,1)S(1)}, u32[]{:S(2)}, u32[]{:S(2)}) %collective-permute-start.4) | collective-permute-done | bytes 524320 | tf_op jit(solution)/shard_map/ppermute | solution.py:410
  48.1 0.8 constant_dynamic-slice_fusion
  48.9 0.1 copy-done.8
  49.1 5.4 %collective-permute-start.6 = (bf16[192,2048]{1,0:T(8,128)(2,1)S(1)}, bf16[192,2048]{1,0:T(8,128)(2,1)}, u32[]{:S(2)}, u32[]{:S(2)}) collective-permute-start(bf16[192,2048]{1,0:T(8,128)(2,1)S(1)} %pad_maximum_fusion), channel_id=1, source_target_pairs={{0,1},{1,0},{2,3},{3,2},{4,5},{5,4},{6,7},{7,6},{8,9},{9,8},{10,11... | collective-permute-start | bytes 2359304 | tf_op jit(solution)/shard_map/ppermute | solution.py:407
  54.6 0.7 broadcast_in_dim.3
  55.3 3.4 %all-to-all-start.1 = ((f32[16,24,128]{2,1,0:T(8,128)}), f32[16,24,128]{2,1,0:T(8,128)S(1)}, u32[]{:S(2)}, u32[]{:S(2)}) async-start(f32[16,24,128]{2,1,0:T(8,128)} %broadcast_in_dim.3), calls=%async_computation.1 | async-start | bytes 393216 | tf_op jit(solution)/shard_map/all_to_all | solution.py:413
  58.7 0.8 copy.12
  59.6 2.0 %collective-permute-start = (bf16[256,512]{1,0:T(8,128)(2,1)}, bf16[256,512]{1,0:T(8,128)(2,1)S(1)}, u32[]{:S(2)}, u32[]{:S(2)}) collective-permute-start(bf16[256,512]{1,0:T(8,128)(2,1)} %bitcast.37), channel_id=1, source_target_pairs={{0,1},{1,0},{2,3},{3,2},{4,5},{5,4},{6,7},{7,6},{8,9},{9,8},{10,11... | collective-permute-start | bytes 786440 | tf_op jit(solution)/shard_map/ppermute | solution.py:407
  61.6 4.7 %collective-permute-start.5 = (bf16[64,2048]{1,0:T(8,128)(2,1)}, bf16[64,2048]{1,0:T(8,128)(2,1)}, u32[]{:S(2)}, u32[]{:S(2)}) collective-permute-start(bf16[64,2048]{1,0:T(8,128)(2,1)} %get-tuple-element.53), channel_id=1, source_target_pairs={{0,2},{2,4},{4,6},{6,8},{8,10},{10,12},{12,14},{14,0},{1,15},{3,1}... | collective-permute-start | bytes 786440 | tf_op jit(solution)/shard_map/ppermute | solution.py:410
  66.3 2.6 %all-to-all-done.1.second_ref = f32[16,24,128]{2,1,0:T(8,128)S(1)} async-done(((f32[16,24,128]{2,1,0:T(8,128)}), f32[16,24,128]{2,1,0:T(8,128)S(1)}, u32[]{:S(2)}, u32[]{:S(2)}) %all-to-all-start.1) | async-done | bytes 196640 | tf_op jit(solution)/shard_map/all_to_all | solution.py:413
  68.9 0.6 div.26
  69.6 0.4 collective-permute-done.5.hop4_ref
  69.9 0.3 copy-done.11
  70.3 1.0 copy-done
  71.3 5.2 %slopes.1 = (bf16[512,2048]{1,0:T(8,128)(2,1)}, f32[8,16,128]{2,1,0:T(8,128)}) custom-call(s32[29]{0:T(128)} %stack.101.at_ref, bf16[64,4096]{1,0:T(8,128)(2,1)} %copy-done.15, bf16[64,4096]{1,0:T(8,128)(2,1)} %copy-done.14, bf16[64,4096]{1,0:T(8,128)(2,1)} %collective-permute-done.3.hop2_ref, bf16[64,4096]{1,0:T(8,128)(2,1)} %copy-done.8, ...), custom_call_target="tpu_custom_call" | custom-call | flops 2200000000 | bytes 8000000 | tf_op jit(solution)/shard_map/slopes/pallas_call | solution.py:143
  76.5 1.8 copy.14.b_ref
  78.3 6.2 %forward.1 = (bf16[32,4096]{1,0:T(8,128)(2,1)}, f32[64,4096]{1,0:T(8,128)}, f32[64,4096]{1,0:T(8,128)}, f32[64,4096]{1,0:T(8,128)}, f32[32,4096]{1,0:T(8,128)}) custom-call(s32[29]{0:T(128)} %stack.101.at_ref, bf16[512,256]{1,0:T(8,128)(2,1)} %a_ref.2, bf16[512,256]{1,0:T(8,128)(2,1)} %copy.14.b_ref, bf16[256,4096]{1,0:T(8,128)(2,1)} %get-tuple-element.27.wo_ref.wa_ref, ...), custom_call_target="tpu_custom_call" | custom-call | flops 1073741824 | bytes 5000000 | tf_op jit(solution)/shard_map/forward/pallas_call | solution.py:103
  84.5 5.2 %collective-permute-start.8 = (bf16[32,4096]{1,0:T(8,128)(2,1)}, bf16[32,4096]{1,0:T(8,128)(2,1)S(1)}, u32[]{:S(2)}, u32[]{:S(2)}) collective-permute-start(bf16[32,4096]{1,0:T(8,128)(2,1)} %get-tuple-element.34), channel_id=1, source_target_pairs={{0,2},{2,4},{4,6},{6,8},{8,10},{10,12},{12,14},{14,0},{1,15},{3,1}... | collective-permute-start | bytes 786440 | tf_op jit(solution)/shard_map/ppermute | solution.py:410
  89.7 1.1 slice.29
  90.7 2.5 %collective-permute-done.8 = bf16[32,4096]{1,0:T(8,128)(2,1)S(1)} collective-permute-done((bf16[32,4096]{1,0:T(8,128)(2,1)}, bf16[32,4096]{1,0:T(8,128)(2,1)S(1)}, u32[]{:S(2)}, u32[]{:S(2)}) %collective-permute-start.8) | collective-permute-done | bytes 262176 | tf_op jit(solution)/shard_map/ppermute | solution.py:410
  93.3 1.1 add_convert_fusion.3
  94.4 4.9 %collective-permute-start.9 = (bf16[64,4096]{1,0:T(8,128)(2,1)S(1)}, bf16[64,4096]{1,0:T(8,128)(2,1)S(1)}, u32[]{:S(2)}, u32[]{:S(2)}) collective-permute-start(bf16[64,4096]{1,0:T(8,128)(2,1)S(1)} %pad_maximum_fusion.1), channel_id=1, source_target_pairs={{0,2},{2,4},{4,6},{6,8},{8,10},{10,12},{12,14},{14,0},{1,15},{3,1}... | collective-permute-start | bytes 1572872 | tf_op jit(solution)/shard_map/ppermute | solution.py:410
  99.3 6.1 %collective-permute-done.9 = bf16[64,4096]{1,0:T(8,128)(2,1)S(1)} collective-permute-done((bf16[64,4096]{1,0:T(8,128)(2,1)S(1)}, bf16[64,4096]{1,0:T(8,128)(2,1)S(1)}, u32[]{:S(2)}, u32[]{:S(2)}) %collective-permute-start.9) | collective-permute-done | bytes 524320 | tf_op jit(solution)/shard_map/ppermute | solution.py:410
  105.5 5.0 %collective-permute-start.10 = (bf16[64,4096]{1,0:T(8,128)(2,1)S(1)}, bf16[64,4096]{1,0:T(8,128)(2,1)S(1)}, u32[]{:S(2)}, u32[]{:S(2)}) collective-permute-start(bf16[64,4096]{1,0:T(8,128)(2,1)S(1)} %add_convert_fusion.1), channel_id=1, source_target_pairs={{0,2},{2,4},{4,6},{6,8},{8,10},{10,12},{12,14},{14,0},{1,15},{3,1}... | collective-permute-start | bytes 1572872 | tf_op jit(solution)/shard_map/ppermute | solution.py:410
  110.6 4.2 %all-to-all-start.2 = ((f32[8,16,128]{2,1,0:T(8,128)}), f32[8,16,128]{2,1,0:T(8,128)S(1)}, u32[]{:S(2)}, u32[]{:S(2)}) async-start(f32[8,16,128]{2,1,0:T(8,128)} %get-tuple-element.38), calls=%async_computation.2 | async-start | bytes 131072 | tf_op jit(solution)/shard_map/all_to_all | solution.py:413
  114.8 7.7 %backward.1 = (f32[512,256]{1,0:T(8,128)}, bf16[512,256]{1,0:T(8,128)(2,1)}, bf16[32,48,128]{2,1,0:T(8,128)(2,1)}) custom-call(s32[29]{0:T(128)} %stack.101.at_ref, bf16[512,2048]{1,0:T(8,128)(2,1)} %get-tuple-element.35.scaled_ref, bf16[256,4096]{1,0:T(8,128)(2,1)} %get-tuple-element.27.wo_ref.wa_ref, bf16[256,4096]{1,0:T(8,128)(2,1)} %copy-done, ...), custom_call_target="tpu_custom_call" | custom-call | flops 3000000000 | bytes 6000000 | tf_op jit(solution)/shard_map/backward/pallas_call | solution.py:222
  122.5 0.6 copy-done.12
  123.2 1.5 pack.1
  124.7 11.7 %all-to-all-start.3 = ((bf16[32,48,128]{2,1,0:T(8,128)(2,1)}), bf16[32,48,128]{2,1,0:T(8,128)(2,1)S(1)}, u32[]{:S(2)}, u32[]{:S(2)}) async-start(bf16[32,48,128]{2,1,0:T(8,128)(2,1)} %pack.1), calls=%async_computation.3 | async-start | bytes 786432 | tf_op jit(solution)/shard_map/all_to_all | solution.py:413
  136.5 4.7 %collective-permute-start.11 = (bf16[64,4096]{1,0:T(8,128)(2,1)S(1)}, bf16[64,4096]{1,0:T(8,128)(2,1)S(1)}, u32[]{:S(2)}, u32[]{:S(2)}) collective-permute-start(bf16[64,4096]{1,0:T(8,128)(2,1)S(1)} %add_convert_fusion), channel_id=1, source_target_pairs={{0,2},{2,4},{4,6},{6,8},{8,10},{10,12},{12,14},{14,0},{1,15},{3,1}... | collective-permute-start | bytes 1572872 | tf_op jit(solution)/shard_map/ppermute | solution.py:410
  141.2 0.6 add_sqrt_fusion.norm_ref
  141.9 5.9 %all-to-all-done.3.got_ref = bf16[32,48,128]{2,1,0:T(8,128)(2,1)S(1)} async-done(((bf16[32,48,128]{2,1,0:T(8,128)(2,1)}), bf16[32,48,128]{2,1,0:T(8,128)(2,1)S(1)}, u32[]{:S(2)}, u32[]{:S(2)}) %all-to-all-start.3) | async-done | bytes 393248 | tf_op jit(solution)/shard_map/all_to_all | solution.py:413
  147.8 0.8 copy-done.3
  148.5 2.6 %combine.1 = bf16[32,48,128]{2,1,0:T(8,128)(2,1)} custom-call(s32[29]{0:T(128)} %stack.101.at_ref, bf16[32,48,128]{2,1,0:T(8,128)(2,1)} %copy-done.3, f32[16,24,128]{2,1,0:T(8,128)} %copy-done.6, f32[1,4096]{1,0:T(1,128)} %add_sqrt_fusion.norm_ref, f32[1,4096]{1,0:T(1,128)} %bitcast.41), custom_call_target="tpu_custom_call" | custom-call | flops 2000000 | bytes 700000 | tf_op jit(solution)/shard_map/combine/pallas_call | solution.py:296
  151.2 3.9 %all-to-all-start.4 = ((bf16[32,48,128]{2,1,0:T(8,128)(2,1)}), bf16[32,48,128]{2,1,0:T(8,128)(2,1)S(1)}, u32[]{:S(2)}, u32[]{:S(2)}) async-start(bf16[32,48,128]{2,1,0:T(8,128)(2,1)} %combine.1), calls=%async_computation.4 | async-start | bytes 786432 | tf_op jit(solution)/shard_map/all_to_all | solution.py:413
  155.1 8.1 %collective-permute-start.13 = (bf16[512,256]{1,0:T(8,128)(2,1)}, bf16[512,256]{1,0:T(8,128)(2,1)S(1)}, u32[]{:S(2)}, u32[]{:S(2)}) collective-permute-start(bf16[512,256]{1,0:T(8,128)(2,1)} %get-tuple-element.37), channel_id=1, source_target_pairs={{0,1},{1,0},{2,3},{3,2},{4,5},{5,4},{6,7},{7,6},{8,9},{9,8},{10,11... | collective-permute-start | bytes 786440 | tf_op jit(solution)/shard_map/ppermute | solution.py:407
  163.2 1.9 %collective-permute-start.12 = (bf16[32,4096]{1,0:T(8,128)(2,1)S(1)}, bf16[32,4096]{1,0:T(8,128)(2,1)S(1)}, u32[]{:S(2)}, u32[]{:S(2)}) collective-permute-start(bf16[32,4096]{1,0:T(8,128)(2,1)S(1)} %slice.24), channel_id=1, source_target_pairs={{0,1},{1,0},{2,3},{3,2},{4,5},{5,4},{6,7},{7,6},{8,9},{9,8},{10,11... | collective-permute-start | bytes 786440 | tf_op jit(solution)/shard_map/ppermute | solution.py:407
  165.2 0.8 add_convert_fusion.2
  165.9 0.6 all-to-all-done.4.got_ref
  166.5 0.7 copy-done.2
  167.3 4.3 %finish.1 = (f32[72,2304]{1,0:T(8,128)}, f32[64,256]{1,0:T(8,128)}) custom-call(s32[29]{0:T(128)} %stack.101.at_ref, bf16[32,48,128]{2,1,0:T(8,128)(2,1)} %copy-done.2, bf16[256,4096]{1,0:T(8,128)(2,1)} %get-tuple-element.27.wo_ref.wa_ref, bf16[256,4096]{1,0:T(8,128)(2,1)} %copy-done, f32[64,4096]{1,0:T(8,128)} %a_ref.3, f32[1,4096]{1,0:T(1,128)} %add_sqrt_fusion.norm_ref, ...), custom_call_target="tpu_custom_call" | custom-call | flops 600000000 | bytes 3000000 | tf_op jit(solution)/shard_map/finish/pallas_call | solution.py:349
  171.6 9.3 %collective-permute-start.14 = (f32[72,2304]{1,0:T(8,128)}, f32[72,2304]{1,0:T(8,128)S(1)}, u32[]{:S(2)}, u32[]{:S(2)}) collective-permute-start(f32[72,2304]{1,0:T(8,128)} %get-tuple-element.42.mine_ref), channel_id=1, source_target_pairs={{0,1},{1,0},{2,3},{3,2},{4,5},{5,4},{6,7},{7,6},{8,9},{9,8},{10,11... | collective-permute-start | bytes 1990664 | tf_op jit(solution)/shard_map/ppermute | solution.py:407
  181.0 0.8 multiply_convert_fusion
  181.8 1.1 collective-permute-done.14.other_ref
  182.9 0.8 copy-done.7
  183.7 3.0 %join.1 = (f32[64,4096]{1,0:T(8,128)}, f32[1,4096]{1,0:T(1,128)}, f32[256,64]{1,0:T(8,128)}) custom-call(s32[29]{0:T(128)} %stack.101.at_ref, f32[72,2304]{1,0:T(8,128)} %get-tuple-element.42.mine_ref, f32[72,2304]{1,0:T(8,128)} %copy-done.7, f32[64,256]{1,0:T(8,128)} %get-tuple-element.43.own_ref), custom_call_target="tpu_custom_call" | custom-call | flops 100000 | bytes 2500000 | tf_op jit(solution)/shard_map/join/pallas_call | solution.py:383
  186.7 1.6 copy.15
  (46 shorter events, 0.5 us)
Async XLA Ops:
  0.6 14.5 %copy-start.1 = (bf16[512,256]{1,0:T(8,128)(2,1)S(1)}, bf16[512,256]{1,0:T(8,128)(2,1)}, u32[]{:S(2)}) copy-start(bf16[512,256]{1,0:T(8,128)(2,1)} %a_ref.2) | copy-start | bytes 786436
  0.6 10.2 %collective-permute-start.1 = (bf16[32,4096]{1,0:T(8,128)(2,1)}, bf16[32,4096]{1,0:T(8,128)(2,1)S(1)}, u32[]{:S(2)}, u32[]{:S(2)}) collective-permute-start(bf16[32,4096]{1,0:T(8,128)(2,1)} %param.11), channel_id=1, source_target_pairs={{0,1},{1,0},{2,3},{3,2},{4,5},{5,4},{6,7},{7,6},{8,9},{9,8},{10,11... | collective-permute-start | bytes 786440 | tf_op jit(solution)/shard_map/ppermute | solution.py:407
  10.9 19.3 %copy-start.15 = (bf16[64,4096]{1,0:T(8,128)(2,1)}, bf16[64,4096]{1,0:T(8,128)(2,1)S(1)}, u32[]{:S(2)}) copy-start(bf16[64,4096]{1,0:T(8,128)(2,1)S(1)} %constant_dynamic-update-slice_fusion.block_ref) | copy-start | bytes 1572868
  10.9 10.2 %collective-permute-start.2 = (bf16[64,4096]{1,0:T(8,128)(2,1)S(1)}, bf16[64,4096]{1,0:T(8,128)(2,1)S(1)}, u32[]{:S(2)}, u32[]{:S(2)}) collective-permute-start(bf16[64,4096]{1,0:T(8,128)(2,1)S(1)} %constant_dynamic-update-slice_fusion.block_ref), channel_id=1, source_target_pairs={{0,2},{2,4},{4,6},{6,8},{8,10},{10,12},{12,14},{14,0},{1,15},{3,1}... | collective-permute-start | bytes 1572872 | tf_op jit(solution)/shard_map/ppermute | solution.py:410
  21.1 9.1 %copy-start.14 = (bf16[64,4096]{1,0:T(8,128)(2,1)}, bf16[64,4096]{1,0:T(8,128)(2,1)S(1)}, u32[]{:S(2)}) copy-start(bf16[64,4096]{1,0:T(8,128)(2,1)S(1)} %collective-permute-done.2.hop1_ref) | copy-start | bytes 1572868
  21.1 12.5 %collective-permute-start.3 = (bf16[64,4096]{1,0:T(8,128)(2,1)S(1)}, bf16[64,4096]{1,0:T(8,128)(2,1)}, u32[]{:S(2)}, u32[]{:S(2)}) collective-permute-start(bf16[64,4096]{1,0:T(8,128)(2,1)S(1)} %collective-permute-done.2.hop1_ref), channel_id=1, source_target_pairs={{0,2},{2,4},{4,6},{6,8},{8,10},{10,12},{12,14},{14,0},{1,15},{3,1}... | collective-permute-start | bytes 1572872 | tf_op jit(solution)/shard_map/ppermute | solution.py:410
  30.2 39.7 %collective-permute-start.7 = (bf16[256,4096]{1,0:T(8,128)(2,1)}, bf16[256,4096]{1,0:T(8,128)(2,1)S(1)}, u32[]{:S(2)}, u32[]{:S(2)}) collective-permute-start(bf16[256,4096]{1,0:T(8,128)(2,1)} %get-tuple-element.27.wo_ref.wa_ref), channel_id=1, source_target_pairs={{0,1},{1,0},{2,3},{3,2},{4,5},{5,4},{6,7},{7,6},{8,9},{9,8},{10,11... | collective-permute-start | bytes 6291464 | tf_op jit(solution)/shard_map/ppermute | solution.py:407
  33.7 14.4 %collective-permute-start.4 = (bf16[64,4096]{1,0:T(8,128)(2,1)}, bf16[64,4096]{1,0:T(8,128)(2,1)S(1)}, u32[]{:S(2)}, u32[]{:S(2)}) collective-permute-start(bf16[64,4096]{1,0:T(8,128)(2,1)} %collective-permute-done.3.hop2_ref), channel_id=1, source_target_pairs={{0,2},{2,4},{4,6},{6,8},{8,10},{10,12},{12,14},{14,0},{1,15},{3,1}... | collective-permute-start | bytes 1572872 | tf_op jit(solution)/shard_map/ppermute | solution.py:410
  38.5 16.0 %all-to-all-start = ((f32[16,24,128]{2,1,0:T(8,128)}), f32[16,24,128]{2,1,0:T(8,128)S(1)}, u32[]{:S(2)}, u32[]{:S(2)}) async-start(f32[16,24,128]{2,1,0:T(8,128)} %get-tuple-element.26), calls=%async_computation | async-start | bytes 393216 | tf_op jit(solution)/shard_map/all_to_all | solution.py:413
  48.1 1.0 copy-start.8
  49.0 19.9 %copy-start.13 = (f32[4096]{0:T(1024)S(1)}, f32[4096]{0:T(1024)}, u32[]{:S(2)}) copy-start(f32[4096]{0:T(1024)} %param.10) | copy-start | bytes 49156
  49.1 20.8 %collective-permute-start.6 = (bf16[192,2048]{1,0:T(8,128)(2,1)S(1)}, bf16[192,2048]{1,0:T(8,128)(2,1)}, u32[]{:S(2)}, u32[]{:S(2)}) collective-permute-start(bf16[192,2048]{1,0:T(8,128)(2,1)S(1)} %pad_maximum_fusion), channel_id=1, source_target_pairs={{0,1},{1,0},{2,3},{3,2},{4,5},{5,4},{6,7},{7,6},{8,9},{9,8},{10,11... | collective-permute-start | bytes 2359304 | tf_op jit(solution)/shard_map/ppermute | solution.py:407
  55.3 13.6 %all-to-all-start.1 = ((f32[16,24,128]{2,1,0:T(8,128)}), f32[16,24,128]{2,1,0:T(8,128)S(1)}, u32[]{:S(2)}, u32[]{:S(2)}) async-start(f32[16,24,128]{2,1,0:T(8,128)} %broadcast_in_dim.3), calls=%async_computation.1 | async-start | bytes 393216 | tf_op jit(solution)/shard_map/all_to_all | solution.py:413
  59.6 10.0 %collective-permute-start = (bf16[256,512]{1,0:T(8,128)(2,1)}, bf16[256,512]{1,0:T(8,128)(2,1)S(1)}, u32[]{:S(2)}, u32[]{:S(2)}) collective-permute-start(bf16[256,512]{1,0:T(8,128)(2,1)} %bitcast.37), channel_id=1, source_target_pairs={{0,1},{1,0},{2,3},{3,2},{4,5},{5,4},{6,7},{7,6},{8,9},{9,8},{10,11... | collective-permute-start | bytes 786440 | tf_op jit(solution)/shard_map/ppermute | solution.py:407
  61.6 8.4 %collective-permute-start.5 = (bf16[64,2048]{1,0:T(8,128)(2,1)}, bf16[64,2048]{1,0:T(8,128)(2,1)}, u32[]{:S(2)}, u32[]{:S(2)}) collective-permute-start(bf16[64,2048]{1,0:T(8,128)(2,1)} %get-tuple-element.53), channel_id=1, source_target_pairs={{0,2},{2,4},{4,6},{6,8},{8,10},{10,12},{12,14},{14,0},{1,15},{3,1}... | collective-permute-start | bytes 786440 | tf_op jit(solution)/shard_map/ppermute | solution.py:410
  68.9 15.6 %copy-start.6 = (f32[16,24,128]{2,1,0:T(8,128)}, f32[16,24,128]{2,1,0:T(8,128)S(1)}, u32[]{:S(2)}) copy-start(f32[16,24,128]{2,1,0:T(8,128)S(1)} %all-to-all-done.1.second_ref) | copy-start | bytes 589828
  69.6 0.7 copy-start.11
  69.9 1.3 copy-start
  84.5 21.0 %copy-start.5 = (f32[64,4096]{1,0:T(8,128)S(1)}, f32[64,4096]{1,0:T(8,128)}, u32[]{:S(2)}) copy-start(f32[64,4096]{1,0:T(8,128)} %get-tuple-element.32) | copy-start | bytes 3145732
  84.5 8.8 %collective-permute-start.8 = (bf16[32,4096]{1,0:T(8,128)(2,1)}, bf16[32,4096]{1,0:T(8,128)(2,1)S(1)}, u32[]{:S(2)}, u32[]{:S(2)}) collective-permute-start(bf16[32,4096]{1,0:T(8,128)(2,1)} %get-tuple-element.34), channel_id=1, source_target_pairs={{0,2},{2,4},{4,6},{6,8},{8,10},{10,12},{12,14},{14,0},{1,15},{3,1}... | collective-permute-start | bytes 786440 | tf_op jit(solution)/shard_map/ppermute | solution.py:410
  94.4 11.0 %collective-permute-start.9 = (bf16[64,4096]{1,0:T(8,128)(2,1)S(1)}, bf16[64,4096]{1,0:T(8,128)(2,1)S(1)}, u32[]{:S(2)}, u32[]{:S(2)}) collective-permute-start(bf16[64,4096]{1,0:T(8,128)(2,1)S(1)} %pad_maximum_fusion.1), channel_id=1, source_target_pairs={{0,2},{2,4},{4,6},{6,8},{8,10},{10,12},{12,14},{14,0},{1,15},{3,1}... | collective-permute-start | bytes 1572872 | tf_op jit(solution)/shard_map/ppermute | solution.py:410
  105.5 30.8 %collective-permute-start.10 = (bf16[64,4096]{1,0:T(8,128)(2,1)S(1)}, bf16[64,4096]{1,0:T(8,128)(2,1)S(1)}, u32[]{:S(2)}, u32[]{:S(2)}) collective-permute-start(bf16[64,4096]{1,0:T(8,128)(2,1)S(1)} %add_convert_fusion.1), channel_id=1, source_target_pairs={{0,2},{2,4},{4,6},{6,8},{8,10},{10,12},{12,14},{14,0},{1,15},{3,1}... | collective-permute-start | bytes 1572872 | tf_op jit(solution)/shard_map/ppermute | solution.py:410
  110.6 12.0 %all-to-all-start.2 = ((f32[8,16,128]{2,1,0:T(8,128)}), f32[8,16,128]{2,1,0:T(8,128)S(1)}, u32[]{:S(2)}, u32[]{:S(2)}) async-start(f32[8,16,128]{2,1,0:T(8,128)} %get-tuple-element.38), calls=%async_computation.2 | async-start | bytes 131072 | tf_op jit(solution)/shard_map/all_to_all | solution.py:413
  122.5 13.8 %copy-start.4 = (f32[64,4096]{1,0:T(8,128)S(1)}, f32[64,4096]{1,0:T(8,128)}, u32[]{:S(2)}) copy-start(f32[64,4096]{1,0:T(8,128)} %get-tuple-element.31) | copy-start | bytes 3145732
  122.5 0.6 copy-start.12
  124.7 23.1 %all-to-all-start.3 = ((bf16[32,48,128]{2,1,0:T(8,128)(2,1)}), bf16[32,48,128]{2,1,0:T(8,128)(2,1)S(1)}, u32[]{:S(2)}, u32[]{:S(2)}) async-start(bf16[32,48,128]{2,1,0:T(8,128)(2,1)} %pack.1), calls=%async_computation.3 | async-start | bytes 786432 | tf_op jit(solution)/shard_map/all_to_all | solution.py:413
  136.4 28.7 %copy-start.9 = (f32[512,256]{1,0:T(8,128)S(1)}, f32[512,256]{1,0:T(8,128)}, u32[]{:S(2)}) copy-start(f32[512,256]{1,0:T(8,128)} %get-tuple-element.36) | copy-start | bytes 1572868
  136.5 26.7 %collective-permute-start.11 = (bf16[64,4096]{1,0:T(8,128)(2,1)S(1)}, bf16[64,4096]{1,0:T(8,128)(2,1)S(1)}, u32[]{:S(2)}, u32[]{:S(2)}) collective-permute-start(bf16[64,4096]{1,0:T(8,128)(2,1)S(1)} %add_convert_fusion), channel_id=1, source_target_pairs={{0,2},{2,4},{4,6},{6,8},{8,10},{10,12},{12,14},{14,0},{1,15},{3,1}... | collective-permute-start | bytes 1572872 | tf_op jit(solution)/shard_map/ppermute | solution.py:410
  147.8 0.8 copy-start.3
  151.2 15.4 %all-to-all-start.4 = ((bf16[32,48,128]{2,1,0:T(8,128)(2,1)}), bf16[32,48,128]{2,1,0:T(8,128)(2,1)S(1)}, u32[]{:S(2)}, u32[]{:S(2)}) async-start(bf16[32,48,128]{2,1,0:T(8,128)(2,1)} %combine.1), calls=%async_computation.4 | async-start | bytes 786432 | tf_op jit(solution)/shard_map/all_to_all | solution.py:413
  155.1 10.1 %collective-permute-start.13 = (bf16[512,256]{1,0:T(8,128)(2,1)}, bf16[512,256]{1,0:T(8,128)(2,1)S(1)}, u32[]{:S(2)}, u32[]{:S(2)}) collective-permute-start(bf16[512,256]{1,0:T(8,128)(2,1)} %get-tuple-element.37), channel_id=1, source_target_pairs={{0,1},{1,0},{2,3},{3,2},{4,5},{5,4},{6,7},{7,6},{8,9},{9,8},{10,11... | collective-permute-start | bytes 786440 | tf_op jit(solution)/shard_map/ppermute | solution.py:407
  163.2 17.7 %collective-permute-start.12 = (bf16[32,4096]{1,0:T(8,128)(2,1)S(1)}, bf16[32,4096]{1,0:T(8,128)(2,1)S(1)}, u32[]{:S(2)}, u32[]{:S(2)}) collective-permute-start(bf16[32,4096]{1,0:T(8,128)(2,1)S(1)} %slice.24), channel_id=1, source_target_pairs={{0,1},{1,0},{2,3},{3,2},{4,5},{5,4},{6,7},{7,6},{8,9},{9,8},{10,11... | collective-permute-start | bytes 786440 | tf_op jit(solution)/shard_map/ppermute | solution.py:407
  165.9 15.0 %copy-start.10 = (f32[32,4096]{1,0:T(8,128)S(1)}, f32[32,4096]{1,0:T(8,128)}, u32[]{:S(2)}) copy-start(f32[32,4096]{1,0:T(8,128)} %get-tuple-element.30) | copy-start | bytes 1572868
  165.9 15.0 %copy-start.16 = (f32[4096]{0:T(1024)S(1)}, f32[4096]{0:T(1024)}, u32[]{:S(2)}) copy-start(f32[4096]{0:T(1024)} %div.26) | copy-start | bytes 49156
  166.5 0.7 copy-start.2
  171.6 11.3 %collective-permute-start.14 = (f32[72,2304]{1,0:T(8,128)}, f32[72,2304]{1,0:T(8,128)S(1)}, u32[]{:S(2)}, u32[]{:S(2)}) collective-permute-start(f32[72,2304]{1,0:T(8,128)} %get-tuple-element.42.mine_ref), channel_id=1, source_target_pairs={{0,1},{1,0},{2,3},{3,2},{4,5},{5,4},{6,7},{7,6},{8,9},{9,8},{10,11... | collective-permute-start | bytes 1990664 | tf_op jit(solution)/shard_map/ppermute | solution.py:407
  182.9 0.9 copy-start.7

commit v5 on v4

--- a/solution.py
+++ b/solution.py
@@ -77,7 +77,9 @@
     )(at, base, wide, pair, adapter_out, z)
 
 
-def forward_kernel(at_ref, a_ref, b_ref, wa_ref, wb_ref, r4_ref, r3_ref, r2_ref, r1_ref, r0_ref, acts):
+def forward_kernel(at_ref, a_ref, b_ref, wa_ref, wb_ref, *rest):
+    refs, acts = rest[-7:-1], rest[-1]
+
     @pl.when(pl.program_id(0) == 0)
     def _():
         for k in range(8):
@@ -86,33 +88,32 @@
             acts[32 * k : 32 * k + 32, 256:] = b_ref[rows, :]
 
     part = contract(acts[...], jnp.concatenate([wa_ref[...], wb_ref[...]], 0), (1, 0))
-    r4_ref[...] = part[0:32].astype(BF16)
-    r3_ref[...] = part[32:96]
-    r2_ref[...] = part[96:160]
-    r1_ref[...] = part[160:224]
-    r0_ref[...] = part[224:256]
-
-
-def forward(at, act_own, act_peer, w_own, w_peer):
+    refs[0][...] = part[0:32].astype(BF16)
+    for ref, low, high in zip(refs[1:], (32, 64, 96, 160, 224), (64, 96, 160, 224, 256)):
+        ref[...] = part[low:high]
+
+
+def forward(at, act_own, act_peer, w_own, w_peer, begin, held=()):
     tokens, feats = act_own.shape
     cols = w_own.shape[1]
+    steps = cols // 2048
     whole = pl.BlockSpec((tokens, feats), lambda i, c: (0, 0))
-    tile = lambda rows: pl.BlockSpec((rows, 1024), lambda i, c: (0, i))
-    rows = (32, 64, 64, 64, 32)
-    kinds = (BF16, F32, F32, F32, F32)
+    tile = lambda rows: pl.BlockSpec((rows, 1024), lambda i, c: (0, i + begin))
+    rows = (32, 32, 32, 64, 64, 32)
+    kinds = (BF16, F32, F32, F32, F32, F32)
     return pl.pallas_call(
         forward_kernel,
         out_shape=tuple(jax.ShapeDtypeStruct((r, cols), k) for r, k in zip(rows, kinds)),
         grid_spec=pltpu.PrefetchScalarGridSpec(
             num_scalar_prefetch=1,
-            grid=(cols // 1024,),
-            in_specs=[whole, whole, tile(feats), tile(feats)],
+            grid=(steps,),
+            in_specs=[whole, whole, tile(feats), tile(feats)] + [pl.BlockSpec(memory_space=pl.ANY)] * len(held),
             out_specs=tuple(tile(r) for r in rows),
             scratch_shapes=[pltpu.VMEM((256, 512), BF16)],
         ),
-        cost_estimate=pl.CostEstimate(flops=2 * tokens * feats * cols, bytes_accessed=5000000, transcendentals=0),
-        name="forward",
-    )(at, act_own, act_peer, w_own, w_peer)
+        input_output_aliases={5 + k: k for k in range(len(held))},
+        cost_estimate=pl.CostEstimate(flops=tokens * feats * cols, bytes_accessed=4000000, transcendentals=0),
+    )(at, act_own, act_peer, w_own, w_peer, *held)
 
 
 def slope_kernel(
@@ -374,12 +375,12 @@
         span = pl.ds(pl.multiple_of(side * cols, cols), cols)
         out_ref[:, span] = ref[0:64, 0:cols]
         mag_ref[:, span] = ref[64:65, 0:cols]
-    in_ref[...] = (own_ref[...] + other_ref[0:64, cols:]).T
+    in_ref[...] = own_ref[...] + other_ref[0:64, cols:]
 
 
 def join(at, mine, other, own):
     block = pl.BlockSpec(mine.shape, lambda i, c: (0, 0))
-    shapes = ((64, 4096), (1, 4096), (256, 64))
+    shapes = ((64, 4096), (1, 4096), own.shape)
     return pl.pallas_call(
         join_kernel,
         out_shape=tuple(jax.ShapeDtypeStruct(s, F32) for s in shapes),
@@ -439,8 +440,7 @@
     at = [core] + near + far + rows + [window // 8, lax.rem(window, 8), window, part]
     at = jnp.stack(at).astype(jnp.int32)
 
-    at_own = activations.T
-    at_peer = swap(at_own)
+    adapter_in, block = lax.optimization_barrier((adapter_in, block))
     high = lax.reduce_precision(adapter_in, 8, 7)
     rest = (adapter_in - high).astype(BF16)
     high = high.astype(BF16)
@@ -448,6 +448,9 @@
     pair = jnp.concatenate([high.T, rest.T], 0)
     z = contract(pair, activations, (1, 1))
     w_own, first = merge(at, base_weight, wide, pair, adapter_out, z)
+    late, first = lax.optimization_barrier((activations, first))
+    at_own = late.T
+    at_peer = swap(at_own)
     w_peer = swap(w_own)
     first = jnp.sum(exchange(first, TENSOR), axis=0)
     second = spread(first, TENSOR)
@@ -457,16 +460,16 @@
     square_sum = second[:, 16:18].reshape(1, 2 * half)
     magnitude = magnitude.reshape(1, 2 * half)
     col_scale = magnitude / jnp.sqrt(square_sum + epsilon)
-    scaled, slope = slopes(at, block, (hop1, hop2, hop3), hop4, crossed, col_scale, w_own, w_peer, at_own, at_peer)
-    turned, slope = lax.optimization_barrier((at_peer, slope))
-    r4, r3, r2, r1, r0 = forward(at, activations, turned.T, w_own, w_peer)
+    act_peer = at_peer.T
+    held = forward(at, activations, act_peer, w_own, w_peer, 0)
+    r4, r3a, r3b, r2, r1, r0 = forward(at, activations, act_peer, w_own, w_peer, 2, held)
     got = shift(r4).astype(F32)
-    got = shift(jnp.concatenate([r3[:32] + got, r3[32:]], 0).astype(BF16)).astype(F32)
+    got = shift(jnp.concatenate([r3a + got, r3b], 0).astype(BF16)).astype(F32)
     got = shift((r2 + got).astype(BF16)).astype(F32)
     got = shift((r1 + got).astype(BF16))
     summed = r0 + got[:32].astype(F32) + swap(got[32:]).astype(F32)
     output = (summed * col_scale).astype(BF16)
-
+    scaled, slope = slopes(at, block, (hop1, hop2, hop3), hop4, crossed, col_scale, w_own, w_peer, at_own, at_peer)
     slope = exchange(slope, "y")
     square_sum, slope = lax.optimization_barrier((square_sum, slope))
     col_norm = jnp.sqrt(square_sum + epsilon)
@@ -477,7 +480,7 @@
     payload, in_own = finish(at, low, w_own, w_peer, adapter_out, col_norm, magnitude)
     last = swap(payload)
     grad_out, grad_mag, grad_in = join(at, payload, last, in_own)
-    grad_mag = grad_mag.reshape(2 * half)
+    grad_mag, grad_in = grad_mag.reshape(2 * half), grad_in.T
     grad_act = (act_own + act_add.astype(F32)).astype(BF16)
     return (output, grad_act, grad_in, grad_out, grad_mag)
 

time: 190 us -> 164 us (0.86)
  starting transfers between devices: 100 us -> 86.1 us
  waiting for transfers between devices: 28.4 us -> 20.7 us
  local copies, waits for them, and re-layouts: 15.7 us -> 11 us
    ppermute x7, starting transfers between devices: 39.1 us -> 26.1 us  [swap(): return lax.ppermute(value, 'core', [(0, 1), (1, 0)])]
    ppermute x8, waiting for transfers between devices: 17.9 us -> 5.01 us  [shift(): return lax.ppermute(value, TENSOR, hops)]
    all_to_all x5, waiting for transfers between devices: 9.11 us -> 14.6 us  [exchange(): return lax.all_to_all(value, axes, 0, 0)]
    ppermute x8, starting transfers between devices: 34.2 us -> 29.1 us  [shift(): return lax.ppermute(value, TENSOR, hops)]
    all_to_all x5, starting transfers between devices: 27.1 us -> 30.9 us  [exchange(): return lax.all_to_all(value, axes, 0, 0)]
    unnamed x37 -> x45, local copies, waits for them, and re-layouts: 7.92 us -> 6.08 us
    pallas_call x1 -> x2, Pallas kernels: 6.18 us -> 7.76 us  [forward(): pl.pallas_call(forward_kernel, out_shape=tuple((jax.ShapeDtypeStruct((r,...]
  transfers between devices with their start and end apart: 20 -> 20, of which waited for: 10 -> 5; matrix products, arithmetic and copies ran while one was open for 7% -> 5% of each run, Pallas kernels for 12% -> 18%
where the time goes in v5:
time: 164 us; the launch traced here: 163 us
  starting transfers between devices  86.1 us (52%)
  Pallas kernels  37.8 us (23%)
  waiting for transfers between devices  20.7 us (13%)
  local copies, waits for them, and re-layouts  11 us (7%)
  other arithmetic  4.81 us (3%)
    all_to_all x5, starting transfers between devices, exchange(): return lax.all_to_all(value, axes, 0, 0)  30.9 us
    ppermute x8, starting transfers between devices, shift(): return lax.ppermute(value, TENSOR, hops)  29.1 us
    ppermute x7, starting transfers between devices, swap(): return lax.ppermute(value, 'core', [(0, 1), (1, 0)])  26.1 us
    all_to_all x5, waiting for transfers between devices, exchange(): return lax.all_to_all(value, axes, 0, 0)  14.6 us
    pallas_call x2, Pallas kernels, forward(): pl.pallas_call(forward_kernel, out_shape=tuple((jax.ShapeDtypeStruct((r,...  7.76 us
    pallas_call x1, Pallas kernels, backward(): pl.pallas_call(backward_kernel, out_shape=(jax.ShapeDtypeStruct((tokens,...  7.73 us
    unnamed x45, local copies, waits for them, and re-layouts  6.08 us
    pallas_call x1, Pallas kernels, merge(): pl.pallas_call(merge_kernel, out_shape=(jax.ShapeDtypeStruct((rows, cols)...  5.67 us
  transfers between devices with their start and end apart: 20, of which 5 were waited for; matrix products, arithmetic and copies ran while one was open for 5% of the time, Pallas kernels for 18%

profile of v5, /device:TPU:1, one launch (start us, length us, event | category | flops | bytes accessed | tf_op | source)
XLA Modules:
  0.0 162.7 jit_solution(1486171791070131543)
XLA Ops:
  0.6 0.0 copy-start.3
  0.6 8.9 %collective-permute-start = (bf16[32,4096]{1,0:T(8,128)(2,1)}, bf16[32,4096]{1,0:T(8,128)(2,1)S(1)}, u32[]{:S(2)}, u32[]{:S(2)}) collective-permute-start(bf16[32,4096]{1,0:T(8,128)(2,1)} %param.11), channel_id=1, source_target_pairs={{0,1},{1,0},{2,3},{3,2},{4,5},{5,4},{6,7},{7,6},{8,9},{9,8},{10,11... | collective-permute-start | bytes 786440 | tf_op jit(solution)/shard_map/ppermute | solution.py:408
  9.6 0.7 stack.101.at_ref
  10.3 1.0 constant_dynamic-update-slice_fusion.1
  11.3 0.9 reduce-precision_convert_fusion
  12.3 0.8 copy.18.wide_ref
  13.0 0.6 pad_maximum_fusion.3.pair_ref
  13.7 0.9 fusion.1.z_ref
  14.6 5.7 %merge.1 = (bf16[256,4096]{1,0:T(8,128)(2,1)}, f32[16,24,128]{2,1,0:T(8,128)}) custom-call(s32[29]{0:T(128)} %stack.101.at_ref, bf16[256,4096]{1,0:T(8,128)(2,1)} %base_ref.1, bf16[256,256]{1,0:T(8,128)(2,1)} %copy.18.wide_ref, bf16[128,256]{1,0:T(8,128)(2,1)} %pad_maximum_fusion.3.pair_ref, f32[64,4096]{1,0:T(8,128)} %a_ref.5, f32[128,512]{1,0:T(8,128)} %fusion.1.z_ref), custom_call_target="tpu_custom_call" | custom-call | flops 1400000000 | bytes 7000000 | tf_op jit(solution)/shard_map/merge/pallas_call | solution.py:57
  20.3 1.9 %collective-permute-start.2 = (bf16[256,4096]{1,0:T(8,128)(2,1)}, bf16[256,4096]{1,0:T(8,128)(2,1)S(1)}, u32[]{:S(2)}, u32[]{:S(2)}) collective-permute-start(bf16[256,4096]{1,0:T(8,128)(2,1)} %get-tuple-element.38.wa_ref.wo_ref), channel_id=1, source_target_pairs={{0,1},{1,0},{2,3},{3,2},{4,5},{5,4},{6,7},{7,6},{8,9},{9,8},{10,11... | collective-permute-start | bytes 6291464 | tf_op jit(solution)/shard_map/ppermute | solution.py:408
  22.2 1.9 %collective-permute-start.8 = (bf16[64,4096]{1,0:T(8,128)(2,1)}, bf16[64,4096]{1,0:T(8,128)(2,1)S(1)}, u32[]{:S(2)}, u32[]{:S(2)}) collective-permute-start(bf16[64,4096]{1,0:T(8,128)(2,1)} %copy-done.18), channel_id=1, source_target_pairs={{0,2},{2,4},{4,6},{6,8},{8,10},{10,12},{12,14},{14,0},{1,15},{3,1}... | collective-permute-start | bytes 1572872 | tf_op jit(solution)/shard_map/ppermute | solution.py:411
  24.1 0.1 copy.19
  24.3 2.4 %collective-permute-start.1 = (bf16[256,512]{1,0:T(8,128)(2,1)S(1)}, bf16[256,512]{1,0:T(8,128)(2,1)S(1)}, u32[]{:S(2)}, u32[]{:S(2)}) collective-permute-start(bf16[256,512]{1,0:T(8,128)(2,1)S(1)} %bitcast.38), channel_id=1, source_target_pairs={{0,1},{1,0},{2,3},{3,2},{4,5},{5,4},{6,7},{7,6},{8,9},{9,8},{10,11... | collective-permute-start | bytes 786440 | tf_op jit(solution)/shard_map/ppermute | solution.py:408
  26.7 4.6 %all-to-all-start = ((f32[16,24,128]{2,1,0:T(8,128)}), f32[16,24,128]{2,1,0:T(8,128)S(1)}, u32[]{:S(2)}, u32[]{:S(2)}) async-start(f32[16,24,128]{2,1,0:T(8,128)} %get-tuple-element.51), calls=%async_computation | async-start | bytes 393216 | tf_op jit(solution)/shard_map/all_to_all | solution.py:414
  31.3 1.3 collective-permute-done.8.hop1_ref
  32.6 3.2 %collective-permute-start.9 = (bf16[64,4096]{1,0:T(8,128)(2,1)S(1)}, bf16[64,4096]{1,0:T(8,128)(2,1)}, u32[]{:S(2)}, u32[]{:S(2)}) collective-permute-start(bf16[64,4096]{1,0:T(8,128)(2,1)S(1)} %collective-permute-done.8.hop1_ref), channel_id=1, source_target_pairs={{0,2},{2,4},{4,6},{6,8},{8,10},{10,12},{12,14},{14,0},{1,15},{3,1}... | collective-permute-start | bytes 1572872 | tf_op jit(solution)/shard_map/ppermute | solution.py:411
  35.8 0.8 copy.21.b_ref
  36.7 1.4 copy-done
  38.1 3.9 %shard_map.101 = (bf16[32,4096]{1,0:T(8,128)(2,1)}, f32[32,4096]{1,0:T(8,128)}, f32[32,4096]{1,0:T(8,128)}, f32[64,4096]{1,0:T(8,128)}, f32[64,4096]{1,0:T(8,128)}, /*index=5*/f32[32,4096]{1,0:T(8,128)}) custom-call(s32[29]{0:T(128)} %stack.101.at_ref, bf16[512,256]{1,0:T(8,128)(2,1)} %a_ref.4, bf16[512,256]{1,0:T(8,128)(2,1)} %copy.21.b_ref, ...), custom_call_target="tpu_custom_call" | custom-call | flops 536870912 | bytes 4000000 | tf_op jit(solution)/shard_map/pallas_call | solution.py:104
  41.9 3.9 %shard_map.102 = (bf16[32,4096]{1,0:T(8,128)(2,1)}, f32[32,4096]{1,0:T(8,128)}, f32[32,4096]{1,0:T(8,128)}, f32[64,4096]{1,0:T(8,128)}, f32[64,4096]{1,0:T(8,128)}, /*index=5*/f32[32,4096]{1,0:T(8,128)}) custom-call(s32[29]{0:T(128)} %stack.101.at_ref, ...), custom_call_target="tpu_custom_call", output_to_operand_aliasing={{0}: (5, {}), {1}: (6, {}), {2}: (7, {}), {3}: (8, {}), {4}... | custom-call | flops 536870912 | bytes 4000000 | tf_op jit(solution)/shard_map/pallas_call | solution.py:104
  45.8 3.2 %collective-permute-start.3 = (bf16[32,4096]{1,0:T(8,128)(2,1)}, bf16[32,4096]{1,0:T(8,128)(2,1)S(1)}, u32[]{:S(2)}, u32[]{:S(2)}) collective-permute-start(bf16[32,4096]{1,0:T(8,128)(2,1)} %get-tuple-element.49), channel_id=1, source_target_pairs={{0,2},{2,4},{4,6},{6,8},{8,10},{10,12},{12,14},{14,0},{1,15},{3,1}... | collective-permute-start | bytes 786440 | tf_op jit(solution)/shard_map/ppermute | solution.py:411
  49.1 0.7 broadcast_in_dim.3
  49.8 6.1 %all-to-all-start.1 = ((f32[16,24,128]{2,1,0:T(8,128)}), f32[16,24,128]{2,1,0:T(8,128)S(1)}, u32[]{:S(2)}, u32[]{:S(2)}) async-start(f32[16,24,128]{2,1,0:T(8,128)} %broadcast_in_dim.3), calls=%async_computation.1 | async-start | bytes 393216 | tf_op jit(solution)/shard_map/all_to_all | solution.py:414
  55.9 4.5 %collective-permute-start.10 = (bf16[64,4096]{1,0:T(8,128)(2,1)}, bf16[64,4096]{1,0:T(8,128)(2,1)S(1)}, u32[]{:S(2)}, u32[]{:S(2)}) collective-permute-start(bf16[64,4096]{1,0:T(8,128)(2,1)} %collective-permute-done.9.hop2_ref), channel_id=1, source_target_pairs={{0,2},{2,4},{4,6},{6,8},{8,10},{10,12},{12,14},{14,0},{1,15},{3,1}... | collective-permute-start | bytes 1572872 | tf_op jit(solution)/shard_map/ppermute | solution.py:411
  60.6 0.0 copy-start.1
  60.6 3.2 %collective-permute-start.4 = (bf16[64,4096]{1,0:T(8,128)(2,1)S(1)}, bf16[64,4096]{1,0:T(8,128)(2,1)S(1)}, u32[]{:S(2)}, u32[]{:S(2)}) collective-permute-start(bf16[64,4096]{1,0:T(8,128)(2,1)S(1)} %pad_maximum_fusion.1), channel_id=1, source_target_pairs={{0,2},{2,4},{4,6},{6,8},{8,10},{10,12},{12,14},{14,0},{1,15},{3,1}... | collective-permute-start | bytes 1572872 | tf_op jit(solution)/shard_map/ppermute | solution.py:411
  63.8 1.0 constant_dynamic-slice_fusion.1
  64.8 3.7 %collective-permute-done.10.hop3_ref = bf16[64,4096]{1,0:T(8,128)(2,1)S(1)} collective-permute-done((bf16[64,4096]{1,0:T(8,128)(2,1)}, bf16[64,4096]{1,0:T(8,128)(2,1)S(1)}, u32[]{:S(2)}, u32[]{:S(2)}) %collective-permute-start.10) | collective-permute-done | bytes 524320 | tf_op jit(solution)/shard_map/ppermute | solution.py:411
  68.5 0.8 constant_dynamic-slice_fusion
  69.3 3.7 %collective-permute-start.11 = (bf16[64,2048]{1,0:T(8,128)(2,1)}, bf16[64,2048]{1,0:T(8,128)(2,1)S(1)}, u32[]{:S(2)}, u32[]{:S(2)}) collective-permute-start(bf16[64,2048]{1,0:T(8,128)(2,1)} %get-tuple-element.66), channel_id=1, source_target_pairs={{0,2},{2,4},{4,6},{6,8},{8,10},{10,12},{12,14},{14,0},{1,15},{3,1}... | collective-permute-start | bytes 786440 | tf_op jit(solution)/shard_map/ppermute | solution.py:411
  73.1 0.0 copy-start.16
  73.1 0.1 pad_maximum_fusion
  73.1 1.9 %collective-permute-start.12 = (bf16[192,2048]{1,0:T(8,128)(2,1)S(1)}, bf16[192,2048]{1,0:T(8,128)(2,1)}, u32[]{:S(2)}, u32[]{:S(2)}) collective-permute-start(bf16[192,2048]{1,0:T(8,128)(2,1)S(1)} %pad_maximum_fusion), channel_id=1, source_target_pairs={{0,1},{1,0},{2,3},{3,2},{4,5},{5,4},{6,7},{7,6},{8,9},{9,8},{10,11... | collective-permute-start | bytes 2359304 | tf_op jit(solution)/shard_map/ppermute | solution.py:408
  75.1 0.1 add_convert_fusion.1
  75.2 4.6 %collective-permute-start.5 = (bf16[64,4096]{1,0:T(8,128)(2,1)S(1)}, bf16[64,4096]{1,0:T(8,128)(2,1)S(1)}, u32[]{:S(2)}, u32[]{:S(2)}) collective-permute-start(bf16[64,4096]{1,0:T(8,128)(2,1)S(1)} %add_convert_fusion.1), channel_id=1, source_target_pairs={{0,2},{2,4},{4,6},{6,8},{8,10},{10,12},{12,14},{14,0},{1,15},{3,1}... | collective-permute-start | bytes 1572872 | tf_op jit(solution)/shard_map/ppermute | solution.py:411
  79.8 0.0 copy-start.9
  79.9 0.6 div.26
  80.5 0.7 copy-done.21
  81.2 5.2 %slopes.1 = (bf16[512,2048]{1,0:T(8,128)(2,1)}, f32[8,16,128]{2,1,0:T(8,128)}) custom-call(s32[29]{0:T(128)} %stack.101.at_ref, bf16[64,4096]{1,0:T(8,128)(2,1)} %copy-done.18, bf16[64,4096]{1,0:T(8,128)(2,1)} %copy-done.17, bf16[64,4096]{1,0:T(8,128)(2,1)} %collective-permute-done.9.hop2_ref, bf16[64,4096]{1,0:T(8,128)(2,1)} %copy-done.11, ...), custom_call_target="tpu_custom_call" | custom-call | flops 2200000000 | bytes 8000000 | tf_op jit(solution)/shard_map/slopes/pallas_call | solution.py:144
  86.4 5.2 %all-to-all-start.2 = ((f32[8,16,128]{2,1,0:T(8,128)}), f32[8,16,128]{2,1,0:T(8,128)S(1)}, u32[]{:S(2)}, u32[]{:S(2)}) async-start(f32[8,16,128]{2,1,0:T(8,128)} %get-tuple-element.56), calls=%async_computation.2 | async-start | bytes 131072 | tf_op jit(solution)/shard_map/all_to_all | solution.py:414
  91.7 7.7 %backward.1 = (f32[512,256]{1,0:T(8,128)}, bf16[512,256]{1,0:T(8,128)(2,1)}, bf16[32,48,128]{2,1,0:T(8,128)(2,1)}) custom-call(s32[29]{0:T(128)} %stack.101.at_ref, bf16[512,2048]{1,0:T(8,128)(2,1)} %get-tuple-element.53.scaled_ref, bf16[256,4096]{1,0:T(8,128)(2,1)} %get-tuple-element.38.wa_ref.wo_ref, bf16[256,4096]{1,0:T(8,128)(2,1)} %copy-done, ...), custom_call_target="tpu_custom_call" | custom-call | flops 3000000000 | bytes 6000000 | tf_op jit(solution)/shard_map/backward/pallas_call | solution.py:223
  99.4 0.0 copy-start.15
  99.4 0.6 copy-done.15
  100.1 1.5 pack.1
  101.6 9.8 %all-to-all-start.3 = ((bf16[32,48,128]{2,1,0:T(8,128)(2,1)}), bf16[32,48,128]{2,1,0:T(8,128)(2,1)S(1)}, u32[]{:S(2)}, u32[]{:S(2)}) async-start(bf16[32,48,128]{2,1,0:T(8,128)(2,1)} %pack.1), calls=%async_computation.3 | async-start | bytes 786432 | tf_op jit(solution)/shard_map/all_to_all | solution.py:414
  111.4 0.0 copy-start.20
  111.4 0.1 add_convert_fusion
  111.5 4.7 %collective-permute-start.6 = (bf16[64,4096]{1,0:T(8,128)(2,1)S(1)}, bf16[64,4096]{1,0:T(8,128)(2,1)S(1)}, u32[]{:S(2)}, u32[]{:S(2)}) collective-permute-start(bf16[64,4096]{1,0:T(8,128)(2,1)S(1)} %add_convert_fusion), channel_id=1, source_target_pairs={{0,2},{2,4},{4,6},{6,8},{8,10},{10,12},{12,14},{14,0},{1,15},{3,1}... | collective-permute-start | bytes 1572872 | tf_op jit(solution)/shard_map/ppermute | solution.py:411
  116.2 0.6 add_sqrt_fusion.norm_ref
  116.9 8.2 %all-to-all-done.3.got_ref = bf16[32,48,128]{2,1,0:T(8,128)(2,1)S(1)} async-done(((bf16[32,48,128]{2,1,0:T(8,128)(2,1)}), bf16[32,48,128]{2,1,0:T(8,128)(2,1)S(1)}, u32[]{:S(2)}, u32[]{:S(2)}) %all-to-all-start.3) | async-done | bytes 393248 | tf_op jit(solution)/shard_map/all_to_all | solution.py:414
  125.1 0.8 copy-done.8
  125.9 2.6 %combine.1 = bf16[32,48,128]{2,1,0:T(8,128)(2,1)} custom-call(s32[29]{0:T(128)} %stack.101.at_ref, bf16[32,48,128]{2,1,0:T(8,128)(2,1)} %copy-done.8, f32[16,24,128]{2,1,0:T(8,128)} %copy-done.9, f32[1,4096]{1,0:T(1,128)} %add_sqrt_fusion.norm_ref, f32[1,4096]{1,0:T(1,128)} %bitcast.42), custom_call_target="tpu_custom_call" | custom-call | flops 2000000 | bytes 700000 | tf_op jit(solution)/shard_map/combine/pallas_call | solution.py:297
  128.5 5.1 %all-to-all-start.4 = ((bf16[32,48,128]{2,1,0:T(8,128)(2,1)}), bf16[32,48,128]{2,1,0:T(8,128)(2,1)S(1)}, u32[]{:S(2)}, u32[]{:S(2)}) async-start(bf16[32,48,128]{2,1,0:T(8,128)(2,1)} %combine.1), calls=%async_computation.4 | async-start | bytes 786432 | tf_op jit(solution)/shard_map/all_to_all | solution.py:414
  133.6 3.6 %collective-permute-start.13 = (bf16[512,256]{1,0:T(8,128)(2,1)S(1)}, bf16[512,256]{1,0:T(8,128)(2,1)S(1)}, u32[]{:S(2)}, u32[]{:S(2)}) collective-permute-start(bf16[512,256]{1,0:T(8,128)(2,1)S(1)} %copy-done.20), channel_id=1, source_target_pairs={{0,1},{1,0},{2,3},{3,2},{4,5},{5,4},{6,7},{7,6},{8,9},{9,8},{10,11... | collective-permute-start | bytes 786440 | tf_op jit(solution)/shard_map/ppermute | solution.py:408
  137.3 1.9 %collective-permute-start.7 = (bf16[32,4096]{1,0:T(8,128)(2,1)S(1)}, bf16[32,4096]{1,0:T(8,128)(2,1)S(1)}, u32[]{:S(2)}, u32[]{:S(2)}) collective-permute-start(bf16[32,4096]{1,0:T(8,128)(2,1)S(1)} %slice.13), channel_id=1, source_target_pairs={{0,1},{1,0},{2,3},{3,2},{4,5},{5,4},{6,7},{7,6},{8,9},{9,8},{10,11... | collective-permute-start | bytes 786440 | tf_op jit(solution)/shard_map/ppermute | solution.py:408
  139.2 0.8 add_convert_fusion.2
  140.0 6.4 %all-to-all-done.4.got_ref = bf16[32,48,128]{2,1,0:T(8,128)(2,1)S(1)} async-done(((bf16[32,48,128]{2,1,0:T(8,128)(2,1)}), bf16[32,48,128]{2,1,0:T(8,128)(2,1)S(1)}, u32[]{:S(2)}, u32[]{:S(2)}) %all-to-all-start.4) | async-done | bytes 393248 | tf_op jit(solution)/shard_map/all_to_all | solution.py:414
  146.3 0.7 copy-done.7
  147.1 4.3 %finish.1 = (f32[72,2304]{1,0:T(8,128)}, f32[64,256]{1,0:T(8,128)}) custom-call(s32[29]{0:T(128)} %stack.101.at_ref, bf16[32,48,128]{2,1,0:T(8,128)(2,1)} %copy-done.7, bf16[256,4096]{1,0:T(8,128)(2,1)} %get-tuple-element.38.wa_ref.wo_ref, bf16[256,4096]{1,0:T(8,128)(2,1)} %copy-done, f32[64,4096]{1,0:T(8,128)} %a_ref.5, f32[1,4096]{1,0:T(1,128)} %add_sqrt_fusion.norm_ref, ...), custom_call_target="tpu_custom_call" | custom-call | flops 600000000 | bytes 3000000 | tf_op jit(solution)/shard_map/finish/pallas_call | solution.py:350
  151.4 5.5 %collective-permute-start.14 = (f32[72,2304]{1,0:T(8,128)}, f32[72,2304]{1,0:T(8,128)S(1)}, u32[]{:S(2)}, u32[]{:S(2)}) collective-permute-start(f32[72,2304]{1,0:T(8,128)} %get-tuple-element.60.mine_ref), channel_id=1, source_target_pairs={{0,1},{1,0},{2,3},{3,2},{4,5},{5,4},{6,7},{7,6},{8,9},{9,8},{10,11... | collective-permute-start | bytes 1990664 | tf_op jit(solution)/shard_map/ppermute | solution.py:408
  156.9 0.8 multiply_convert_fusion
  157.7 1.1 collective-permute-done.14.other_ref
  158.8 0.8 copy-done.10
  159.7 3.0 %join.1 = (f32[64,4096]{1,0:T(8,128)}, f32[1,4096]{1,0:T(1,128)}, f32[64,256]{1,0:T(8,128)}) custom-call(s32[29]{0:T(128)} %stack.101.at_ref, f32[72,2304]{1,0:T(8,128)} %get-tuple-element.60.mine_ref, f32[72,2304]{1,0:T(8,128)} %copy-done.10, f32[64,256]{1,0:T(8,128)} %get-tuple-element.61.own_ref), custom_call_target="tpu_custom_call" | custom-call | flops 100000 | bytes 2500000 | tf_op jit(solution)/shard_map/join/pallas_call | solution.py:384
  (56 shorter events, 0.3 us)
Async XLA Ops:
  0.6 13.0 %copy-start.3 = (bf16[512,256]{1,0:T(8,128)(2,1)S(1)}, bf16[512,256]{1,0:T(8,128)(2,1)}, u32[]{:S(2)}) copy-start(bf16[512,256]{1,0:T(8,128)(2,1)} %a_ref.4) | copy-start | bytes 786436
  0.6 10.6 %collective-permute-start = (bf16[32,4096]{1,0:T(8,128)(2,1)}, bf16[32,4096]{1,0:T(8,128)(2,1)S(1)}, u32[]{:S(2)}, u32[]{:S(2)}) collective-permute-start(bf16[32,4096]{1,0:T(8,128)(2,1)} %param.11), channel_id=1, source_target_pairs={{0,1},{1,0},{2,3},{3,2},{4,5},{5,4},{6,7},{7,6},{8,9},{9,8},{10,11... | collective-permute-start | bytes 786440 | tf_op jit(solution)/shard_map/ppermute | solution.py:408
  11.3 0.9 copy-start.18
  20.3 16.4 %collective-permute-start.2 = (bf16[256,4096]{1,0:T(8,128)(2,1)}, bf16[256,4096]{1,0:T(8,128)(2,1)S(1)}, u32[]{:S(2)}, u32[]{:S(2)}) collective-permute-start(bf16[256,4096]{1,0:T(8,128)(2,1)} %get-tuple-element.38.wa_ref.wo_ref), channel_id=1, source_target_pairs={{0,1},{1,0},{2,3},{3,2},{4,5},{5,4},{6,7},{7,6},{8,9},{9,8},{10,11... | collective-permute-start | bytes 6291464 | tf_op jit(solution)/shard_map/ppermute | solution.py:408
  22.2 10.4 %collective-permute-start.8 = (bf16[64,4096]{1,0:T(8,128)(2,1)}, bf16[64,4096]{1,0:T(8,128)(2,1)S(1)}, u32[]{:S(2)}, u32[]{:S(2)}) collective-permute-start(bf16[64,4096]{1,0:T(8,128)(2,1)} %copy-done.18), channel_id=1, source_target_pairs={{0,2},{2,4},{4,6},{6,8},{8,10},{10,12},{12,14},{14,0},{1,15},{3,1}... | collective-permute-start | bytes 1572872 | tf_op jit(solution)/shard_map/ppermute | solution.py:411
  24.3 17.7 %copy-start.13 = (bf16[512,256]{0,1:T(8,128)(2,1)}, bf16[512,256]{0,1:T(8,128)(2,1)S(1)}, u32[]{:S(2)}) copy-start(bf16[512,256]{0,1:T(8,128)(2,1)S(1)} %copy.19) | copy-start | bytes 786436
  24.3 11.6 %collective-permute-start.1 = (bf16[256,512]{1,0:T(8,128)(2,1)S(1)}, bf16[256,512]{1,0:T(8,128)(2,1)S(1)}, u32[]{:S(2)}, u32[]{:S(2)}) collective-permute-start(bf16[256,512]{1,0:T(8,128)(2,1)S(1)} %bitcast.38), channel_id=1, source_target_pairs={{0,1},{1,0},{2,3},{3,2},{4,5},{5,4},{6,7},{7,6},{8,9},{9,8},{10,11... | collective-permute-start | bytes 786440 | tf_op jit(solution)/shard_map/ppermute | solution.py:408
  26.7 22.4 %all-to-all-start = ((f32[16,24,128]{2,1,0:T(8,128)}), f32[16,24,128]{2,1,0:T(8,128)S(1)}, u32[]{:S(2)}, u32[]{:S(2)}) async-start(f32[16,24,128]{2,1,0:T(8,128)} %get-tuple-element.51), calls=%async_computation | async-start | bytes 393216 | tf_op jit(solution)/shard_map/all_to_all | solution.py:414
  32.6 23.3 %copy-start.17 = (bf16[64,4096]{1,0:T(8,128)(2,1)}, bf16[64,4096]{1,0:T(8,128)(2,1)S(1)}, u32[]{:S(2)}) copy-start(bf16[64,4096]{1,0:T(8,128)(2,1)S(1)} %collective-permute-done.8.hop1_ref) | copy-start | bytes 1572868
  32.6 23.3 %collective-permute-start.9 = (bf16[64,4096]{1,0:T(8,128)(2,1)S(1)}, bf16[64,4096]{1,0:T(8,128)(2,1)}, u32[]{:S(2)}, u32[]{:S(2)}) collective-permute-start(bf16[64,4096]{1,0:T(8,128)(2,1)S(1)} %collective-permute-done.8.hop1_ref), channel_id=1, source_target_pairs={{0,2},{2,4},{4,6},{6,8},{8,10},{10,12},{12,14},{14,0},{1,15},{3,1}... | collective-permute-start | bytes 1572872 | tf_op jit(solution)/shard_map/ppermute | solution.py:411
  35.8 6.1 %copy-start.14 = (bf16[256,512]{1,0:T(8,128)(2,1)}, bf16[256,512]{1,0:T(8,128)(2,1)S(1)}, u32[]{:S(2)}) copy-start(bf16[256,512]{1,0:T(8,128)(2,1)S(1)} %collective-permute-done.1.atp_ref) | copy-start | bytes 786436
  36.7 1.4 copy-start
  45.8 14.6 %copy-start.5 = (f32[32,4096]{1,0:T(8,128)S(1)}, f32[32,4096]{1,0:T(8,128)}, u32[]{:S(2)}) copy-start(f32[32,4096]{1,0:T(8,128)} %get-tuple-element.50) | copy-start | bytes 1572868
  45.8 14.7 %copy-start.4 = (f32[32,4096]{1,0:T(8,128)S(1)}, f32[32,4096]{1,0:T(8,128)}, u32[]{:S(2)}) copy-start(f32[32,4096]{1,0:T(8,128)} %get-tuple-element.48) | copy-start | bytes 1572868
  45.8 14.6 %collective-permute-start.3 = (bf16[32,4096]{1,0:T(8,128)(2,1)}, bf16[32,4096]{1,0:T(8,128)(2,1)S(1)}, u32[]{:S(2)}, u32[]{:S(2)}) collective-permute-start(bf16[32,4096]{1,0:T(8,128)(2,1)} %get-tuple-element.49), channel_id=1, source_target_pairs={{0,2},{2,4},{4,6},{6,8},{8,10},{10,12},{12,14},{14,0},{1,15},{3,1}... | collective-permute-start | bytes 786440 | tf_op jit(solution)/shard_map/ppermute | solution.py:411
  49.8 30.0 %all-to-all-start.1 = ((f32[16,24,128]{2,1,0:T(8,128)}), f32[16,24,128]{2,1,0:T(8,128)S(1)}, u32[]{:S(2)}, u32[]{:S(2)}) async-start(f32[16,24,128]{2,1,0:T(8,128)} %broadcast_in_dim.3), calls=%async_computation.1 | async-start | bytes 393216 | tf_op jit(solution)/shard_map/all_to_all | solution.py:414
  55.9 12.6 %collective-permute-start.10 = (bf16[64,4096]{1,0:T(8,128)(2,1)}, bf16[64,4096]{1,0:T(8,128)(2,1)S(1)}, u32[]{:S(2)}, u32[]{:S(2)}) collective-permute-start(bf16[64,4096]{1,0:T(8,128)(2,1)} %collective-permute-done.9.hop2_ref), channel_id=1, source_target_pairs={{0,2},{2,4},{4,6},{6,8},{8,10},{10,12},{12,14},{14,0},{1,15},{3,1}... | collective-permute-start | bytes 1572872 | tf_op jit(solution)/shard_map/ppermute | solution.py:411
  60.6 14.5 %copy-start.1 = (f32[64,4096]{1,0:T(8,128)S(1)}, f32[64,4096]{1,0:T(8,128)}, u32[]{:S(2)}) copy-start(f32[64,4096]{1,0:T(8,128)} %get-tuple-element.47) | copy-start | bytes 3145732
  60.6 14.5 %collective-permute-start.4 = (bf16[64,4096]{1,0:T(8,128)(2,1)S(1)}, bf16[64,4096]{1,0:T(8,128)(2,1)S(1)}, u32[]{:S(2)}, u32[]{:S(2)}) collective-permute-start(bf16[64,4096]{1,0:T(8,128)(2,1)S(1)} %pad_maximum_fusion.1), channel_id=1, source_target_pairs={{0,2},{2,4},{4,6},{6,8},{8,10},{10,12},{12,14},{14,0},{1,15},{3,1}... | collective-permute-start | bytes 1572872 | tf_op jit(solution)/shard_map/ppermute | solution.py:411
  68.5 6.7 %copy-start.11 = (bf16[64,4096]{1,0:T(8,128)(2,1)}, bf16[64,4096]{1,0:T(8,128)(2,1)S(1)}, u32[]{:S(2)}) copy-start(bf16[64,4096]{1,0:T(8,128)(2,1)S(1)} %collective-permute-done.10.hop3_ref) | copy-start | bytes 1572868
  69.3 11.2 %collective-permute-start.11 = (bf16[64,2048]{1,0:T(8,128)(2,1)}, bf16[64,2048]{1,0:T(8,128)(2,1)S(1)}, u32[]{:S(2)}, u32[]{:S(2)}) collective-permute-start(bf16[64,2048]{1,0:T(8,128)(2,1)} %get-tuple-element.66), channel_id=1, source_target_pairs={{0,2},{2,4},{4,6},{6,8},{8,10},{10,12},{12,14},{14,0},{1,15},{3,1}... | collective-permute-start | bytes 786440 | tf_op jit(solution)/shard_map/ppermute | solution.py:411
  73.1 6.8 %copy-start.16 = (f32[4096]{0:T(1024)S(1)}, f32[4096]{0:T(1024)}, u32[]{:S(2)}) copy-start(f32[4096]{0:T(1024)} %param.10) | copy-start | bytes 49156
  73.1 7.4 %collective-permute-start.12 = (bf16[192,2048]{1,0:T(8,128)(2,1)S(1)}, bf16[192,2048]{1,0:T(8,128)(2,1)}, u32[]{:S(2)}, u32[]{:S(2)}) collective-permute-start(bf16[192,2048]{1,0:T(8,128)(2,1)S(1)} %pad_maximum_fusion), channel_id=1, source_target_pairs={{0,1},{1,0},{2,3},{3,2},{4,5},{5,4},{6,7},{7,6},{8,9},{9,8},{10,11... | collective-permute-start | bytes 2359304 | tf_op jit(solution)/shard_map/ppermute | solution.py:408
  75.2 36.2 %collective-permute-start.5 = (bf16[64,4096]{1,0:T(8,128)(2,1)S(1)}, bf16[64,4096]{1,0:T(8,128)(2,1)S(1)}, u32[]{:S(2)}, u32[]{:S(2)}) collective-permute-start(bf16[64,4096]{1,0:T(8,128)(2,1)S(1)} %add_convert_fusion.1), channel_id=1, source_target_pairs={{0,2},{2,4},{4,6},{6,8},{8,10},{10,12},{12,14},{14,0},{1,15},{3,1}... | collective-permute-start | bytes 1572872 | tf_op jit(solution)/shard_map/ppermute | solution.py:411
  79.8 6.6 %copy-start.9 = (f32[16,24,128]{2,1,0:T(8,128)}, f32[16,24,128]{2,1,0:T(8,128)S(1)}, u32[]{:S(2)}) copy-start(f32[16,24,128]{2,1,0:T(8,128)S(1)} %all-to-all-done.1.second_ref) | copy-start | bytes 589828
  80.5 0.7 copy-start.21
  86.4 13.0 %all-to-all-start.2 = ((f32[8,16,128]{2,1,0:T(8,128)}), f32[8,16,128]{2,1,0:T(8,128)S(1)}, u32[]{:S(2)}, u32[]{:S(2)}) async-start(f32[8,16,128]{2,1,0:T(8,128)} %get-tuple-element.56), calls=%async_computation.2 | async-start | bytes 131072 | tf_op jit(solution)/shard_map/all_to_all | solution.py:414
  99.4 12.0 %copy-start.2 = (f32[64,4096]{1,0:T(8,128)S(1)}, f32[64,4096]{1,0:T(8,128)}, u32[]{:S(2)}) copy-start(f32[64,4096]{1,0:T(8,128)} %get-tuple-element.46) | copy-start | bytes 3145732
  99.4 0.6 copy-start.15
  101.6 23.6 %all-to-all-start.3 = ((bf16[32,48,128]{2,1,0:T(8,128)(2,1)}), bf16[32,48,128]{2,1,0:T(8,128)(2,1)S(1)}, u32[]{:S(2)}, u32[]{:S(2)}) async-start(bf16[32,48,128]{2,1,0:T(8,128)(2,1)} %pack.1), calls=%async_computation.3 | async-start | bytes 786432 | tf_op jit(solution)/shard_map/all_to_all | solution.py:414
  111.4 22.2 %copy-start.20 = (bf16[512,256]{1,0:T(8,128)(2,1)S(1)}, bf16[512,256]{1,0:T(8,128)(2,1)}, u32[]{:S(2)}) copy-start(bf16[512,256]{1,0:T(8,128)(2,1)} %get-tuple-element.55) | copy-start | bytes 786436
  111.5 27.7 %copy-start.12 = (f32[512,256]{1,0:T(8,128)S(1)}, f32[512,256]{1,0:T(8,128)}, u32[]{:S(2)}) copy-start(f32[512,256]{1,0:T(8,128)} %get-tuple-element.54) | copy-start | bytes 1572868
  111.5 25.7 %collective-permute-start.6 = (bf16[64,4096]{1,0:T(8,128)(2,1)S(1)}, bf16[64,4096]{1,0:T(8,128)(2,1)S(1)}, u32[]{:S(2)}, u32[]{:S(2)}) collective-permute-start(bf16[64,4096]{1,0:T(8,128)(2,1)S(1)} %add_convert_fusion), channel_id=1, source_target_pairs={{0,2},{2,4},{4,6},{6,8},{8,10},{10,12},{12,14},{14,0},{1,15},{3,1}... | collective-permute-start | bytes 1572872 | tf_op jit(solution)/shard_map/ppermute | solution.py:411
  125.1 0.8 copy-start.8
  128.5 17.8 %all-to-all-start.4 = ((bf16[32,48,128]{2,1,0:T(8,128)(2,1)}), bf16[32,48,128]{2,1,0:T(8,128)(2,1)S(1)}, u32[]{:S(2)}, u32[]{:S(2)}) async-start(bf16[32,48,128]{2,1,0:T(8,128)(2,1)} %combine.1), calls=%async_computation.4 | async-start | bytes 786432 | tf_op jit(solution)/shard_map/all_to_all | solution.py:414
  133.6 5.6 %collective-permute-start.13 = (bf16[512,256]{1,0:T(8,128)(2,1)S(1)}, bf16[512,256]{1,0:T(8,128)(2,1)S(1)}, u32[]{:S(2)}, u32[]{:S(2)}) collective-permute-start(bf16[512,256]{1,0:T(8,128)(2,1)S(1)} %copy-done.20), channel_id=1, source_target_pairs={{0,1},{1,0},{2,3},{3,2},{4,5},{5,4},{6,7},{7,6},{8,9},{9,8},{10,11... | collective-permute-start | bytes 786440 | tf_op jit(solution)/shard_map/ppermute | solution.py:408
  137.3 19.6 %collective-permute-start.7 = (bf16[32,4096]{1,0:T(8,128)(2,1)S(1)}, bf16[32,4096]{1,0:T(8,128)(2,1)S(1)}, u32[]{:S(2)}, u32[]{:S(2)}) collective-permute-start(bf16[32,4096]{1,0:T(8,128)(2,1)S(1)} %slice.13), channel_id=1, source_target_pairs={{0,1},{1,0},{2,3},{3,2},{4,5},{5,4},{6,7},{7,6},{8,9},{9,8},{10,11... | collective-permute-start | bytes 786440 | tf_op jit(solution)/shard_map/ppermute | solution.py:408
  140.0 16.9 %copy-start.6 = (f32[32,4096]{1,0:T(8,128)S(1)}, f32[32,4096]{1,0:T(8,128)}, u32[]{:S(2)}) copy-start(f32[32,4096]{1,0:T(8,128)} %get-tuple-element.45) | copy-start | bytes 1572868
  140.0 16.9 %copy-start.19 = (f32[4096]{0:T(1024)S(1)}, f32[4096]{0:T(1024)}, u32[]{:S(2)}) copy-start(f32[4096]{0:T(1024)} %div.26) | copy-start | bytes 49156
  146.3 0.7 copy-start.7
  151.4 7.4 %collective-permute-start.14 = (f32[72,2304]{1,0:T(8,128)}, f32[72,2304]{1,0:T(8,128)S(1)}, u32[]{:S(2)}, u32[]{:S(2)}) collective-permute-start(f32[72,2304]{1,0:T(8,128)} %get-tuple-element.60.mine_ref), channel_id=1, source_target_pairs={{0,1},{1,0},{2,3},{3,2},{4,5},{5,4},{6,7},{7,6},{8,9},{9,8},{10,11... | collective-permute-start | bytes 1990664 | tf_op jit(solution)/shard_map/ppermute | solution.py:408
  158.8 0.9 copy-start.10

commit v6 on v4

--- a/solution.py
+++ b/solution.py
@@ -87,7 +87,7 @@
 
     part = contract(acts[...], jnp.concatenate([wa_ref[...], wb_ref[...]], 0), (1, 0))
     r4_ref[...] = part[0:32].astype(BF16)
-    r3_ref[...] = part[32:96]
+    r3_ref[...] = part[32:96].astype(BF16)
     r2_ref[...] = part[96:160]
     r1_ref[...] = part[160:224]
     r0_ref[...] = part[224:256]
@@ -99,7 +99,7 @@
     whole = pl.BlockSpec((tokens, feats), lambda i, c: (0, 0))
     tile = lambda rows: pl.BlockSpec((rows, 1024), lambda i, c: (0, i))
     rows = (32, 64, 64, 64, 32)
-    kinds = (BF16, F32, F32, F32, F32)
+    kinds = (BF16, BF16, F32, F32, F32)
     return pl.pallas_call(
         forward_kernel,
         out_shape=tuple(jax.ShapeDtypeStruct((r, cols), k) for r, k in zip(rows, kinds)),
@@ -124,8 +124,9 @@
     for k, (part, r) in enumerate(parts):
         cots[pl.ds(pl.multiple_of(at_ref[1 + k] * 32, 32), 32), :] = part[r : r + 32, :]
     cot = cots[...]
-    slope = jnp.sum(contract(ato_ref[...], cot, (1, 0)) * wo_ref[...].astype(F32), axis=0, keepdims=True)
-    slope = slope + jnp.sum(contract(atp_ref[...], cot, (1, 0)) * wp_ref[...].astype(F32), axis=0, keepdims=True)
+    weight = jnp.concatenate([wo_ref[...], wp_ref[...]], 0).astype(F32)
+    slope = contract(jnp.concatenate([ato_ref[...], atp_ref[...]], 0), cot, (1, 0)) * weight
+    slope = jnp.sum(slope, axis=0, keepdims=True)
     scaled_ref[...] = (cot.astype(F32) * scale_ref[...]).astype(BF16)
     for q in range(8):
         row = slope[:, 128 * q : 128 * q + 128]
@@ -374,12 +375,12 @@
         span = pl.ds(pl.multiple_of(side * cols, cols), cols)
         out_ref[:, span] = ref[0:64, 0:cols]
         mag_ref[:, span] = ref[64:65, 0:cols]
-    in_ref[...] = (own_ref[...] + other_ref[0:64, cols:]).T
+    in_ref[...] = own_ref[...] + other_ref[0:64, cols:]
 
 
 def join(at, mine, other, own):
     block = pl.BlockSpec(mine.shape, lambda i, c: (0, 0))
-    shapes = ((64, 4096), (1, 4096), (256, 64))
+    shapes = ((64, 4096), (1, 4096), own.shape)
     return pl.pallas_call(
         join_kernel,
         out_shape=tuple(jax.ShapeDtypeStruct(s, F32) for s in shapes),
@@ -439,8 +440,7 @@
     at = [core] + near + far + rows + [window // 8, lax.rem(window, 8), window, part]
     at = jnp.stack(at).astype(jnp.int32)
 
-    at_own = activations.T
-    at_peer = swap(at_own)
+    adapter_in, block = lax.optimization_barrier((adapter_in, block))
     high = lax.reduce_precision(adapter_in, 8, 7)
     rest = (adapter_in - high).astype(BF16)
     high = high.astype(BF16)
@@ -448,6 +448,9 @@
     pair = jnp.concatenate([high.T, rest.T], 0)
     z = contract(pair, activations, (1, 1))
     w_own, first = merge(at, base_weight, wide, pair, adapter_out, z)
+    late, first = lax.optimization_barrier((activations, first))
+    at_own = late.T
+    at_peer = swap(at_own)
     w_peer = swap(w_own)
     first = jnp.sum(exchange(first, TENSOR), axis=0)
     second = spread(first, TENSOR)
@@ -457,16 +460,15 @@
     square_sum = second[:, 16:18].reshape(1, 2 * half)
     magnitude = magnitude.reshape(1, 2 * half)
     col_scale = magnitude / jnp.sqrt(square_sum + epsilon)
-    scaled, slope = slopes(at, block, (hop1, hop2, hop3), hop4, crossed, col_scale, w_own, w_peer, at_own, at_peer)
-    turned, slope = lax.optimization_barrier((at_peer, slope))
-    r4, r3, r2, r1, r0 = forward(at, activations, turned.T, w_own, w_peer)
-    got = shift(r4).astype(F32)
-    got = shift(jnp.concatenate([r3[:32] + got, r3[32:]], 0).astype(BF16)).astype(F32)
+    act_peer = at_peer.T
+    r4, r3, r2, r1, r0 = forward(at, activations, act_peer, w_own, w_peer)
+    got = shift(r3).astype(F32)
     got = shift((r2 + got).astype(BF16)).astype(F32)
     got = shift((r1 + got).astype(BF16))
-    summed = r0 + got[:32].astype(F32) + swap(got[32:]).astype(F32)
+    across = lax.ppermute(r4, "y", [(s, (s + sides // 2) % sides) for s in range(sides)])
+    summed = r0 + across.astype(F32) + got[:32].astype(F32) + swap(got[32:]).astype(F32)
     output = (summed * col_scale).astype(BF16)
-
+    scaled, slope = slopes(at, block, (hop1, hop2, hop3), hop4, crossed, col_scale, w_own, w_peer, at_own, at_peer)
     slope = exchange(slope, "y")
     square_sum, slope = lax.optimization_barrier((square_sum, slope))
     col_norm = jnp.sqrt(square_sum + epsilon)
@@ -477,7 +479,7 @@
     payload, in_own = finish(at, low, w_own, w_peer, adapter_out, col_norm, magnitude)
     last = swap(payload)
     grad_out, grad_mag, grad_in = join(at, payload, last, in_own)
-    grad_mag = grad_mag.reshape(2 * half)
+    grad_mag, grad_in = grad_mag.reshape(2 * half), grad_in.T
     grad_act = (act_own + act_add.astype(F32)).astype(BF16)
     return (output, grad_act, grad_in, grad_out, grad_mag)
 

time: 190 us -> 168 us (0.88)
  starting transfers between devices: 100 us -> 87.9 us
  waiting for transfers between devices: 28.4 us -> 22.4 us
  local copies, waits for them, and re-layouts: 15.7 us -> 11.9 us
    ppermute x7, starting transfers between devices: 39.1 us -> 24.8 us  [swap(): return lax.ppermute(value, 'core', [(0, 1), (1, 0)])]
    ppermute x8 -> x7, starting transfers between devices: 34.2 us -> 24.2 us  [shift(): return lax.ppermute(value, TENSOR, hops)]
    ppermute x8 -> x7, waiting for transfers between devices: 17.9 us -> 8.87 us  [shift(): return lax.ppermute(value, TENSOR, hops)]
    ppermute x0 -> x1, starting transfers between devices: none -> 7.25 us  [program(): lax.ppermute(r4, 'y', [(s, (s + sides // 2) % sides) for s in range(sides)])]
    all_to_all x5, starting transfers between devices: 27.1 us -> 31.7 us  [exchange(): return lax.all_to_all(value, axes, 0, 0)]
    all_to_all x5, waiting for transfers between devices: 9.11 us -> 11 us  [exchange(): return lax.all_to_all(value, axes, 0, 0)]
    unnamed x37, local copies, waits for them, and re-layouts: 7.92 us -> 6.01 us
  transfers between devices with their start and end apart: 20 -> 20, of which waited for: 10 -> 6; matrix products, arithmetic and copies ran while one was open for 7% -> 6% of each run, Pallas kernels for 12% -> 17%
where the time goes in v6:
time: 168 us; the launch traced here: 166 us
  starting transfers between devices  87.9 us (52%)
  Pallas kernels  36.3 us (22%)
  waiting for transfers between devices  22.4 us (13%)
  local copies, waits for them, and re-layouts  11.9 us (7%)
  other arithmetic  5.76 us (3%)
    all_to_all x5, starting transfers between devices, exchange(): return lax.all_to_all(value, axes, 0, 0)  31.7 us
    ppermute x7, starting transfers between devices, swap(): return lax.ppermute(value, 'core', [(0, 1), (1, 0)])  24.8 us
    ppermute x7, starting transfers between devices, shift(): return lax.ppermute(value, TENSOR, hops)  24.2 us
    all_to_all x5, waiting for transfers between devices, exchange(): return lax.all_to_all(value, axes, 0, 0)  11 us
    ppermute x7, waiting for transfers between devices, shift(): return lax.ppermute(value, TENSOR, hops)  8.87 us
    pallas_call x1, Pallas kernels, backward(): pl.pallas_call(backward_kernel, out_shape=(jax.ShapeDtypeStruct((tokens,...  7.75 us
    ppermute x1, starting transfers between devices, program(): lax.ppermute(r4, 'y', [(s, (s + sides // 2) % sides) for s in range(sides)])  7.25 us
    unnamed x37, local copies, waits for them, and re-layouts  6.01 us
  transfers between devices with their start and end apart: 20, of which 6 were waited for; matrix products, arithmetic and copies ran while one was open for 6% of the time, Pallas kernels for 17%

profile of v6, /device:TPU:1, one launch (start us, length us, event | category | flops | bytes accessed | tf_op | source)
XLA Modules:
  0.0 166.4 jit_solution(13001888237457639322)
XLA Ops:
  0.6 0.0 copy-start.1
  0.6 8.9 %collective-permute-start = (bf16[32,4096]{1,0:T(8,128)(2,1)}, bf16[32,4096]{1,0:T(8,128)(2,1)S(1)}, u32[]{:S(2)}, u32[]{:S(2)}) collective-permute-start(bf16[32,4096]{1,0:T(8,128)(2,1)} %param.11), channel_id=1, source_target_pairs={{0,1},{1,0},{2,3},{3,2},{4,5},{5,4},{6,7},{7,6},{8,9},{9,8},{10,11... | collective-permute-start | bytes 786440 | tf_op jit(solution)/shard_map/ppermute | solution.py:408
  9.6 0.6 stack.101.at_ref
  10.2 1.0 constant_dynamic-update-slice_fusion.1
  11.2 0.0 collective-permute-done
  11.3 0.9 reduce-precision_convert_fusion
  12.2 0.6 pad_maximum_fusion.2.pair_ref
  12.8 0.9 fusion.1.z_ref
  13.8 0.8 copy.12.wide_ref
  14.5 5.6 %merge.1 = (bf16[256,4096]{1,0:T(8,128)(2,1)}, f32[16,24,128]{2,1,0:T(8,128)}) custom-call(s32[29]{0:T(128)} %stack.101.at_ref, bf16[256,4096]{1,0:T(8,128)(2,1)} %base_ref.1, bf16[256,256]{1,0:T(8,128)(2,1)} %copy.12.wide_ref, bf16[128,256]{1,0:T(8,128)(2,1)} %pad_maximum_fusion.2.pair_ref, f32[64,4096]{1,0:T(8,128)} %a_ref.3, f32[128,512]{1,0:T(8,128)} %fusion.1.z_ref), custom_call_target="tpu_custom_call" | custom-call | flops 1400000000 | bytes 7000000 | tf_op jit(solution)/shard_map/merge/pallas_call | solution.py:57
  20.1 1.9 %collective-permute-start.2 = (bf16[256,4096]{1,0:T(8,128)(2,1)}, bf16[256,4096]{1,0:T(8,128)(2,1)S(1)}, u32[]{:S(2)}, u32[]{:S(2)}) collective-permute-start(bf16[256,4096]{1,0:T(8,128)(2,1)} %get-tuple-element.31.wa_ref.wo_ref), channel_id=1, source_target_pairs={{0,1},{1,0},{2,3},{3,2},{4,5},{5,4},{6,7},{7,6},{8,9},{9,8},{10,11... | collective-permute-start | bytes 6291464 | tf_op jit(solution)/shard_map/ppermute | solution.py:408
  22.1 1.9 %collective-permute-start.8 = (bf16[64,4096]{1,0:T(8,128)(2,1)S(1)}, bf16[64,4096]{1,0:T(8,128)(2,1)}, u32[]{:S(2)}, u32[]{:S(2)}) collective-permute-start(bf16[64,4096]{1,0:T(8,128)(2,1)S(1)} %constant_dynamic-update-slice_fusion.block_ref), channel_id=1, source_target_pairs={{0,2},{2,4},{4,6},{6,8},{8,10},{10,12},{12,14},{14,0},{1,15},{3,1}... | collective-permute-start | bytes 1572872 | tf_op jit(solution)/shard_map/ppermute | solution.py:411
  24.0 8.4 %collective-permute-done.8.hop1_ref = bf16[64,4096]{1,0:T(8,128)(2,1)} collective-permute-done((bf16[64,4096]{1,0:T(8,128)(2,1)S(1)}, bf16[64,4096]{1,0:T(8,128)(2,1)}, u32[]{:S(2)}, u32[]{:S(2)}) %collective-permute-start.8) | collective-permute-done | bytes 524320 | tf_op jit(solution)/shard_map/ppermute | solution.py:411
  32.4 2.8 %collective-permute-start.9 = (bf16[64,4096]{1,0:T(8,128)(2,1)}, bf16[64,4096]{1,0:T(8,128)(2,1)}, u32[]{:S(2)}, u32[]{:S(2)}) collective-permute-start(bf16[64,4096]{1,0:T(8,128)(2,1)} %collective-permute-done.8.hop1_ref), channel_id=1, source_target_pairs={{0,2},{2,4},{4,6},{6,8},{8,10},{10,12},{12,14},{14,0},{1,15},{3,1}... | collective-permute-start | bytes 1572872 | tf_op jit(solution)/shard_map/ppermute | solution.py:411
  35.2 6.2 %all-to-all-start = ((f32[16,24,128]{2,1,0:T(8,128)}), f32[16,24,128]{2,1,0:T(8,128)S(1)}, u32[]{:S(2)}, u32[]{:S(2)}) async-start(f32[16,24,128]{2,1,0:T(8,128)} %get-tuple-element.37), calls=%async_computation | async-start | bytes 393216 | tf_op jit(solution)/shard_map/all_to_all | solution.py:414
  41.4 0.1 copy.13
  41.5 2.0 %collective-permute-start.1 = (bf16[256,512]{1,0:T(8,128)(2,1)S(1)}, bf16[256,512]{1,0:T(8,128)(2,1)S(1)}, u32[]{:S(2)}, u32[]{:S(2)}) collective-permute-start(bf16[256,512]{1,0:T(8,128)(2,1)S(1)} %bitcast.38), channel_id=1, source_target_pairs={{0,1},{1,0},{2,3},{3,2},{4,5},{5,4},{6,7},{7,6},{8,9},{9,8},{10,11... | collective-permute-start | bytes 786440 | tf_op jit(solution)/shard_map/ppermute | solution.py:408
  43.6 1.4 collective-permute-done.1.atp_ref
  45.0 0.8 copy.14.b_ref
  45.8 5.7 %all-to-all-done = f32[16,24,128]{2,1,0:T(8,128)S(1)} async-done(((f32[16,24,128]{2,1,0:T(8,128)}), f32[16,24,128]{2,1,0:T(8,128)S(1)}, u32[]{:S(2)}, u32[]{:S(2)}) %all-to-all-start) | async-done | bytes 196640 | tf_op jit(solution)/shard_map/all_to_all | solution.py:414
  51.5 0.7 broadcast_in_dim.3
  52.2 3.4 %all-to-all-start.1 = ((f32[16,24,128]{2,1,0:T(8,128)}), f32[16,24,128]{2,1,0:T(8,128)S(1)}, u32[]{:S(2)}, u32[]{:S(2)}) async-start(f32[16,24,128]{2,1,0:T(8,128)} %broadcast_in_dim.3), calls=%async_computation.1 | async-start | bytes 393216 | tf_op jit(solution)/shard_map/all_to_all | solution.py:414
  55.7 4.4 %collective-permute-start.10 = (bf16[64,4096]{1,0:T(8,128)(2,1)}, bf16[64,4096]{1,0:T(8,128)(2,1)S(1)}, u32[]{:S(2)}, u32[]{:S(2)}) collective-permute-start(bf16[64,4096]{1,0:T(8,128)(2,1)} %collective-permute-done.9.hop2_ref), channel_id=1, source_target_pairs={{0,2},{2,4},{4,6},{6,8},{8,10},{10,12},{12,14},{14,0},{1,15},{3,1}... | collective-permute-start | bytes 1572872 | tf_op jit(solution)/shard_map/ppermute | solution.py:411
  60.1 1.0 constant_dynamic-slice_fusion.2
  61.1 1.3 copy-done
  62.5 6.0 %forward.1 = (bf16[32,4096]{1,0:T(8,128)(2,1)}, bf16[64,4096]{1,0:T(8,128)(2,1)}, f32[64,4096]{1,0:T(8,128)}, f32[64,4096]{1,0:T(8,128)}, f32[32,4096]{1,0:T(8,128)}) custom-call(s32[29]{0:T(128)} %stack.101.at_ref, bf16[512,256]{1,0:T(8,128)(2,1)} %a_ref.2, bf16[512,256]{1,0:T(8,128)(2,1)} %copy.14.b_ref, ...), custom_call_target="tpu_custom_call" | custom-call | flops 1073741824 | bytes 5000000 | tf_op jit(solution)/shard_map/forward/pallas_call | solution.py:103
  68.5 0.0 copy-start.5
  68.5 3.2 %collective-permute-start.4 = (bf16[64,4096]{1,0:T(8,128)(2,1)}, bf16[64,4096]{1,0:T(8,128)(2,1)S(1)}, u32[]{:S(2)}, u32[]{:S(2)}) collective-permute-start(bf16[64,4096]{1,0:T(8,128)(2,1)} %get-tuple-element.36), channel_id=1, source_target_pairs={{0,2},{2,4},{4,6},{6,8},{8,10},{10,12},{12,14},{14,0},{1,15},{3,1}... | collective-permute-start | bytes 1572872 | tf_op jit(solution)/shard_map/ppermute | solution.py:411
  71.7 1.0 constant_dynamic-slice_fusion.1
  72.7 0.8 constant_dynamic-slice_fusion
  73.5 0.1 pad_maximum_fusion
  73.6 1.9 %collective-permute-start.12 = (bf16[192,2048]{1,0:T(8,128)(2,1)S(1)}, bf16[192,2048]{1,0:T(8,128)(2,1)}, u32[]{:S(2)}, u32[]{:S(2)}) collective-permute-start(bf16[192,2048]{1,0:T(8,128)(2,1)S(1)} %pad_maximum_fusion), channel_id=1, source_target_pairs={{0,1},{1,0},{2,3},{3,2},{4,5},{5,4},{6,7},{7,6},{8,9},{9,8},{10,11... | collective-permute-start | bytes 2359304 | tf_op jit(solution)/shard_map/ppermute | solution.py:408
  75.5 3.1 %collective-permute-start.11 = (bf16[64,2048]{1,0:T(8,128)(2,1)}, bf16[64,2048]{1,0:T(8,128)(2,1)S(1)}, u32[]{:S(2)}, u32[]{:S(2)}) collective-permute-start(bf16[64,2048]{1,0:T(8,128)(2,1)} %get-tuple-element.52), channel_id=1, source_target_pairs={{0,2},{2,4},{4,6},{6,8},{8,10},{10,12},{12,14},{14,0},{1,15},{3,1}... | collective-permute-start | bytes 786440 | tf_op jit(solution)/shard_map/ppermute | solution.py:411
  78.6 0.5 collective-permute-done.4
  79.0 0.1 add_convert_fusion.1
  79.1 4.0 %collective-permute-start.5 = (bf16[64,4096]{1,0:T(8,128)(2,1)S(1)}, bf16[64,4096]{1,0:T(8,128)(2,1)}, u32[]{:S(2)}, u32[]{:S(2)}) collective-permute-start(bf16[64,4096]{1,0:T(8,128)(2,1)S(1)} %add_convert_fusion.1), channel_id=1, source_target_pairs={{0,2},{2,4},{4,6},{6,8},{8,10},{10,12},{12,14},{14,0},{1,15},{3,1}... | collective-permute-start | bytes 1572872 | tf_op jit(solution)/shard_map/ppermute | solution.py:411
  83.2 0.6 div.26
  83.8 0.7 copy-done.17
  84.5 5.5 %slopes.1 = (bf16[512,2048]{1,0:T(8,128)(2,1)}, f32[8,16,128]{2,1,0:T(8,128)}) custom-call(s32[29]{0:T(128)} %stack.101.at_ref, bf16[64,4096]{1,0:T(8,128)(2,1)} %copy-done.15, bf16[64,4096]{1,0:T(8,128)(2,1)} %collective-permute-done.8.hop1_ref, bf16[64,4096]{1,0:T(8,128)(2,1)} %collective-permute-done.9.hop2_ref, bf16[64,4096]{1,0:T(8,128)(2,1)} %copy-done.9, ...), custom_call_target="tpu_custom_call" | custom-call | flops 2200000000 | bytes 8000000 | tf_op jit(solution)/shard_map/slopes/pallas_call | solution.py:144
  90.1 4.5 %all-to-all-start.2 = ((f32[8,16,128]{2,1,0:T(8,128)}), f32[8,16,128]{2,1,0:T(8,128)S(1)}, u32[]{:S(2)}, u32[]{:S(2)}) async-start(f32[8,16,128]{2,1,0:T(8,128)} %get-tuple-element.42), calls=%async_computation.2 | async-start | bytes 131072 | tf_op jit(solution)/shard_map/all_to_all | solution.py:414
  94.6 7.8 %backward.1 = (f32[512,256]{1,0:T(8,128)}, bf16[512,256]{1,0:T(8,128)(2,1)}, bf16[32,48,128]{2,1,0:T(8,128)(2,1)}) custom-call(s32[29]{0:T(128)} %stack.101.at_ref, bf16[512,2048]{1,0:T(8,128)(2,1)} %get-tuple-element.39.scaled_ref, bf16[256,4096]{1,0:T(8,128)(2,1)} %get-tuple-element.31.wa_ref.wo_ref, bf16[256,4096]{1,0:T(8,128)(2,1)} %copy-done, ...), custom_call_target="tpu_custom_call" | custom-call | flops 3000000000 | bytes 6000000 | tf_op jit(solution)/shard_map/backward/pallas_call | solution.py:223
  102.3 0.0 copy-start.13
  102.4 0.6 copy-done.13
  103.0 1.5 pack.1
  104.5 11.4 %all-to-all-start.3 = ((bf16[32,48,128]{2,1,0:T(8,128)(2,1)}), bf16[32,48,128]{2,1,0:T(8,128)(2,1)S(1)}, u32[]{:S(2)}, u32[]{:S(2)}) async-start(bf16[32,48,128]{2,1,0:T(8,128)(2,1)} %pack.1), calls=%async_computation.3 | async-start | bytes 786432 | tf_op jit(solution)/shard_map/all_to_all | solution.py:414
  115.9 1.1 add_convert_fusion
  117.1 0.0 copy-start.10
  117.1 4.7 %collective-permute-start.6 = (bf16[64,4096]{1,0:T(8,128)(2,1)S(1)}, bf16[64,4096]{1,0:T(8,128)(2,1)S(1)}, u32[]{:S(2)}, u32[]{:S(2)}) collective-permute-start(bf16[64,4096]{1,0:T(8,128)(2,1)S(1)} %add_convert_fusion), channel_id=1, source_target_pairs={{0,2},{2,4},{4,6},{6,8},{8,10},{10,12},{12,14},{14,0},{1,15},{3,1}... | collective-permute-start | bytes 1572872 | tf_op jit(solution)/shard_map/ppermute | solution.py:411
  121.8 0.6 add_sqrt_fusion.norm_ref
  122.4 5.3 %all-to-all-done.3.got_ref = bf16[32,48,128]{2,1,0:T(8,128)(2,1)S(1)} async-done(((bf16[32,48,128]{2,1,0:T(8,128)(2,1)}), bf16[32,48,128]{2,1,0:T(8,128)(2,1)S(1)}, u32[]{:S(2)}, u32[]{:S(2)}) %all-to-all-start.3) | async-done | bytes 393248 | tf_op jit(solution)/shard_map/all_to_all | solution.py:414
  127.8 0.7 copy-done.3
  128.5 2.6 %combine.1 = bf16[32,48,128]{2,1,0:T(8,128)(2,1)} custom-call(s32[29]{0:T(128)} %stack.101.at_ref, bf16[32,48,128]{2,1,0:T(8,128)(2,1)} %copy-done.3, f32[16,24,128]{2,1,0:T(8,128)} %copy-done.6, f32[1,4096]{1,0:T(1,128)} %add_sqrt_fusion.norm_ref, f32[1,4096]{1,0:T(1,128)} %bitcast.42), custom_call_target="tpu_custom_call" | custom-call | flops 2000000 | bytes 700000 | tf_op jit(solution)/shard_map/combine/pallas_call | solution.py:297
  131.1 6.2 %all-to-all-start.4 = ((bf16[32,48,128]{2,1,0:T(8,128)(2,1)}), bf16[32,48,128]{2,1,0:T(8,128)(2,1)S(1)}, u32[]{:S(2)}, u32[]{:S(2)}) async-start(bf16[32,48,128]{2,1,0:T(8,128)(2,1)} %combine.1), calls=%async_computation.4 | async-start | bytes 786432 | tf_op jit(solution)/shard_map/all_to_all | solution.py:414
  137.3 4.4 %collective-permute-start.13 = (bf16[512,256]{1,0:T(8,128)(2,1)}, bf16[512,256]{1,0:T(8,128)(2,1)S(1)}, u32[]{:S(2)}, u32[]{:S(2)}) collective-permute-start(bf16[512,256]{1,0:T(8,128)(2,1)} %get-tuple-element.41), channel_id=1, source_target_pairs={{0,1},{1,0},{2,3},{3,2},{4,5},{5,4},{6,7},{7,6},{8,9},{9,8},{10,11... | collective-permute-start | bytes 786440 | tf_op jit(solution)/shard_map/ppermute | solution.py:408
  141.8 7.3 %collective-permute-start.3 = (bf16[32,4096]{1,0:T(8,128)(2,1)}, bf16[32,4096]{1,0:T(8,128)(2,1)S(1)}, u32[]{:S(2)}, u32[]{:S(2)}) collective-permute-start(bf16[32,4096]{1,0:T(8,128)(2,1)} %get-tuple-element.33), channel_id=1, source_target_pairs={{0,8},{2,10},{4,12},{6,14},{8,0},{10,2},{12,4},{14,6},{1,9},{3,11}... | collective-permute-start | bytes 786440 | tf_op jit(solution)/shard_map/ppermute | solution.py:468
  149.1 2.2 %collective-permute-start.7 = (bf16[32,4096]{1,0:T(8,128)(2,1)S(1)}, bf16[32,4096]{1,0:T(8,128)(2,1)S(1)}, u32[]{:S(2)}, u32[]{:S(2)}) collective-permute-start(bf16[32,4096]{1,0:T(8,128)(2,1)S(1)} %slice.13), channel_id=1, source_target_pairs={{0,1},{1,0},{2,3},{3,2},{4,5},{5,4},{6,7},{7,6},{8,9},{9,8},{10,11... | collective-permute-start | bytes 786440 | tf_op jit(solution)/shard_map/ppermute | solution.py:408
  151.3 0.8 add_convert_fusion.2
  152.1 0.7 copy-done.2
  152.8 4.3 %finish.1 = (f32[72,2304]{1,0:T(8,128)}, f32[64,256]{1,0:T(8,128)}) custom-call(s32[29]{0:T(128)} %stack.101.at_ref, bf16[32,48,128]{2,1,0:T(8,128)(2,1)} %copy-done.2, bf16[256,4096]{1,0:T(8,128)(2,1)} %get-tuple-element.31.wa_ref.wo_ref, bf16[256,4096]{1,0:T(8,128)(2,1)} %copy-done, f32[64,4096]{1,0:T(8,128)} %a_ref.3, f32[1,4096]{1,0:T(1,128)} %add_sqrt_fusion.norm_ref, ...), custom_call_target="tpu_custom_call" | custom-call | flops 600000000 | bytes 3000000 | tf_op jit(solution)/shard_map/finish/pallas_call | solution.py:350
  157.1 3.5 %collective-permute-start.14 = (f32[72,2304]{1,0:T(8,128)}, f32[72,2304]{1,0:T(8,128)S(1)}, u32[]{:S(2)}, u32[]{:S(2)}) collective-permute-start(f32[72,2304]{1,0:T(8,128)} %get-tuple-element.46.mine_ref), channel_id=1, source_target_pairs={{0,1},{1,0},{2,3},{3,2},{4,5},{5,4},{6,7},{7,6},{8,9},{9,8},{10,11... | collective-permute-start | bytes 1990664 | tf_op jit(solution)/shard_map/ppermute | solution.py:408
  160.6 0.8 multiply_convert_fusion
  161.5 1.0 collective-permute-done.14.other_ref
  162.5 0.9 copy-done.7
  163.4 3.0 %join.1 = (f32[64,4096]{1,0:T(8,128)}, f32[1,4096]{1,0:T(1,128)}, f32[64,256]{1,0:T(8,128)}) custom-call(s32[29]{0:T(128)} %stack.101.at_ref, f32[72,2304]{1,0:T(8,128)} %get-tuple-element.46.mine_ref, f32[72,2304]{1,0:T(8,128)} %copy-done.7, f32[64,256]{1,0:T(8,128)} %get-tuple-element.47.own_ref), custom_call_target="tpu_custom_call" | custom-call | flops 100000 | bytes 2500000 | tf_op jit(solution)/shard_map/join/pallas_call | solution.py:384
  (44 shorter events, 0.2 us)
Async XLA Ops:
  0.6 12.2 %copy-start.1 = (bf16[512,256]{1,0:T(8,128)(2,1)S(1)}, bf16[512,256]{1,0:T(8,128)(2,1)}, u32[]{:S(2)}) copy-start(bf16[512,256]{1,0:T(8,128)(2,1)} %a_ref.2) | copy-start | bytes 786436
  0.6 10.6 %collective-permute-start = (bf16[32,4096]{1,0:T(8,128)(2,1)}, bf16[32,4096]{1,0:T(8,128)(2,1)S(1)}, u32[]{:S(2)}, u32[]{:S(2)}) collective-permute-start(bf16[32,4096]{1,0:T(8,128)(2,1)} %param.11), channel_id=1, source_target_pairs={{0,1},{1,0},{2,3},{3,2},{4,5},{5,4},{6,7},{7,6},{8,9},{9,8},{10,11... | collective-permute-start | bytes 786440 | tf_op jit(solution)/shard_map/ppermute | solution.py:408
  11.2 10.8 %copy-start.15 = (bf16[64,4096]{1,0:T(8,128)(2,1)}, bf16[64,4096]{1,0:T(8,128)(2,1)S(1)}, u32[]{:S(2)}) copy-start(bf16[64,4096]{1,0:T(8,128)(2,1)S(1)} %constant_dynamic-update-slice_fusion.block_ref) | copy-start | bytes 1572868
  20.1 41.0 %collective-permute-start.2 = (bf16[256,4096]{1,0:T(8,128)(2,1)}, bf16[256,4096]{1,0:T(8,128)(2,1)S(1)}, u32[]{:S(2)}, u32[]{:S(2)}) collective-permute-start(bf16[256,4096]{1,0:T(8,128)(2,1)} %get-tuple-element.31.wa_ref.wo_ref), channel_id=1, source_target_pairs={{0,1},{1,0},{2,3},{3,2},{4,5},{5,4},{6,7},{7,6},{8,9},{9,8},{10,11... | collective-permute-start | bytes 6291464 | tf_op jit(solution)/shard_map/ppermute | solution.py:408
  22.1 10.3 %collective-permute-start.8 = (bf16[64,4096]{1,0:T(8,128)(2,1)S(1)}, bf16[64,4096]{1,0:T(8,128)(2,1)}, u32[]{:S(2)}, u32[]{:S(2)}) collective-permute-start(bf16[64,4096]{1,0:T(8,128)(2,1)S(1)} %constant_dynamic-update-slice_fusion.block_ref), channel_id=1, source_target_pairs={{0,2},{2,4},{4,6},{6,8},{8,10},{10,12},{12,14},{14,0},{1,15},{3,1}... | collective-permute-start | bytes 1572872 | tf_op jit(solution)/shard_map/ppermute | solution.py:411
  32.4 23.3 %collective-permute-start.9 = (bf16[64,4096]{1,0:T(8,128)(2,1)}, bf16[64,4096]{1,0:T(8,128)(2,1)}, u32[]{:S(2)}, u32[]{:S(2)}) collective-permute-start(bf16[64,4096]{1,0:T(8,128)(2,1)} %collective-permute-done.8.hop1_ref), channel_id=1, source_target_pairs={{0,2},{2,4},{4,6},{6,8},{8,10},{10,12},{12,14},{14,0},{1,15},{3,1}... | collective-permute-start | bytes 1572872 | tf_op jit(solution)/shard_map/ppermute | solution.py:411
  35.2 16.3 %all-to-all-start = ((f32[16,24,128]{2,1,0:T(8,128)}), f32[16,24,128]{2,1,0:T(8,128)S(1)}, u32[]{:S(2)}, u32[]{:S(2)}) async-start(f32[16,24,128]{2,1,0:T(8,128)} %get-tuple-element.37), calls=%async_computation | async-start | bytes 393216 | tf_op jit(solution)/shard_map/all_to_all | solution.py:414
  41.5 10.7 %copy-start.11 = (bf16[512,256]{0,1:T(8,128)(2,1)}, bf16[512,256]{0,1:T(8,128)(2,1)S(1)}, u32[]{:S(2)}) copy-start(bf16[512,256]{0,1:T(8,128)(2,1)S(1)} %copy.13) | copy-start | bytes 786436
  41.5 3.4 %collective-permute-start.1 = (bf16[256,512]{1,0:T(8,128)(2,1)S(1)}, bf16[256,512]{1,0:T(8,128)(2,1)S(1)}, u32[]{:S(2)}, u32[]{:S(2)}) collective-permute-start(bf16[256,512]{1,0:T(8,128)(2,1)S(1)} %bitcast.38), channel_id=1, source_target_pairs={{0,1},{1,0},{2,3},{3,2},{4,5},{5,4},{6,7},{7,6},{8,9},{9,8},{10,11... | collective-permute-start | bytes 786440 | tf_op jit(solution)/shard_map/ppermute | solution.py:408
  45.0 23.5 %copy-start.12 = (bf16[256,512]{1,0:T(8,128)(2,1)}, bf16[256,512]{1,0:T(8,128)(2,1)S(1)}, u32[]{:S(2)}) copy-start(bf16[256,512]{1,0:T(8,128)(2,1)S(1)} %collective-permute-done.1.atp_ref) | copy-start | bytes 786436
  52.2 30.9 %all-to-all-start.1 = ((f32[16,24,128]{2,1,0:T(8,128)}), f32[16,24,128]{2,1,0:T(8,128)S(1)}, u32[]{:S(2)}, u32[]{:S(2)}) async-start(f32[16,24,128]{2,1,0:T(8,128)} %broadcast_in_dim.3), calls=%async_computation.1 | async-start | bytes 393216 | tf_op jit(solution)/shard_map/all_to_all | solution.py:414
  55.7 17.0 %collective-permute-start.10 = (bf16[64,4096]{1,0:T(8,128)(2,1)}, bf16[64,4096]{1,0:T(8,128)(2,1)S(1)}, u32[]{:S(2)}, u32[]{:S(2)}) collective-permute-start(bf16[64,4096]{1,0:T(8,128)(2,1)} %collective-permute-done.9.hop2_ref), channel_id=1, source_target_pairs={{0,2},{2,4},{4,6},{6,8},{8,10},{10,12},{12,14},{14,0},{1,15},{3,1}... | collective-permute-start | bytes 1572872 | tf_op jit(solution)/shard_map/ppermute | solution.py:411
  61.1 1.3 copy-start
  68.5 10.6 %copy-start.5 = (f32[64,4096]{1,0:T(8,128)S(1)}, f32[64,4096]{1,0:T(8,128)}, u32[]{:S(2)}) copy-start(f32[64,4096]{1,0:T(8,128)} %get-tuple-element.35) | copy-start | bytes 3145732
  68.5 10.6 %collective-permute-start.4 = (bf16[64,4096]{1,0:T(8,128)(2,1)}, bf16[64,4096]{1,0:T(8,128)(2,1)S(1)}, u32[]{:S(2)}, u32[]{:S(2)}) collective-permute-start(bf16[64,4096]{1,0:T(8,128)(2,1)} %get-tuple-element.36), channel_id=1, source_target_pairs={{0,2},{2,4},{4,6},{6,8},{8,10},{10,12},{12,14},{14,0},{1,15},{3,1}... | collective-permute-start | bytes 1572872 | tf_op jit(solution)/shard_map/ppermute | solution.py:411
  72.7 6.5 %copy-start.9 = (bf16[64,4096]{1,0:T(8,128)(2,1)}, bf16[64,4096]{1,0:T(8,128)(2,1)S(1)}, u32[]{:S(2)}) copy-start(bf16[64,4096]{1,0:T(8,128)(2,1)S(1)} %collective-permute-done.10.hop3_ref) | copy-start | bytes 1572868
  73.5 9.7 %copy-start.14 = (f32[4096]{0:T(1024)S(1)}, f32[4096]{0:T(1024)}, u32[]{:S(2)}) copy-start(f32[4096]{0:T(1024)} %param.10) | copy-start | bytes 49156
  73.6 10.3 %collective-permute-start.12 = (bf16[192,2048]{1,0:T(8,128)(2,1)S(1)}, bf16[192,2048]{1,0:T(8,128)(2,1)}, u32[]{:S(2)}, u32[]{:S(2)}) collective-permute-start(bf16[192,2048]{1,0:T(8,128)(2,1)S(1)} %pad_maximum_fusion), channel_id=1, source_target_pairs={{0,1},{1,0},{2,3},{3,2},{4,5},{5,4},{6,7},{7,6},{8,9},{9,8},{10,11... | collective-permute-start | bytes 2359304 | tf_op jit(solution)/shard_map/ppermute | solution.py:408
  75.5 8.3 %collective-permute-start.11 = (bf16[64,2048]{1,0:T(8,128)(2,1)}, bf16[64,2048]{1,0:T(8,128)(2,1)S(1)}, u32[]{:S(2)}, u32[]{:S(2)}) collective-permute-start(bf16[64,2048]{1,0:T(8,128)(2,1)} %get-tuple-element.52), channel_id=1, source_target_pairs={{0,2},{2,4},{4,6},{6,8},{8,10},{10,12},{12,14},{14,0},{1,15},{3,1}... | collective-permute-start | bytes 786440 | tf_op jit(solution)/shard_map/ppermute | solution.py:411
  79.1 36.8 %collective-permute-start.5 = (bf16[64,4096]{1,0:T(8,128)(2,1)S(1)}, bf16[64,4096]{1,0:T(8,128)(2,1)}, u32[]{:S(2)}, u32[]{:S(2)}) collective-permute-start(bf16[64,4096]{1,0:T(8,128)(2,1)S(1)} %add_convert_fusion.1), channel_id=1, source_target_pairs={{0,2},{2,4},{4,6},{6,8},{8,10},{10,12},{12,14},{14,0},{1,15},{3,1}... | collective-permute-start | bytes 1572872 | tf_op jit(solution)/shard_map/ppermute | solution.py:411
  83.2 6.9 %copy-start.6 = (f32[16,24,128]{2,1,0:T(8,128)}, f32[16,24,128]{2,1,0:T(8,128)S(1)}, u32[]{:S(2)}) copy-start(f32[16,24,128]{2,1,0:T(8,128)S(1)} %all-to-all-done.1.second_ref) | copy-start | bytes 589828
  83.8 0.7 copy-start.17
  90.1 12.2 %all-to-all-start.2 = ((f32[8,16,128]{2,1,0:T(8,128)}), f32[8,16,128]{2,1,0:T(8,128)S(1)}, u32[]{:S(2)}, u32[]{:S(2)}) async-start(f32[8,16,128]{2,1,0:T(8,128)} %get-tuple-element.42), calls=%async_computation.2 | async-start | bytes 131072 | tf_op jit(solution)/shard_map/all_to_all | solution.py:414
  102.3 13.6 %copy-start.4 = (f32[64,4096]{1,0:T(8,128)S(1)}, f32[64,4096]{1,0:T(8,128)}, u32[]{:S(2)}) copy-start(f32[64,4096]{1,0:T(8,128)} %get-tuple-element.34) | copy-start | bytes 3145732
  102.3 0.6 copy-start.13
  104.5 23.3 %all-to-all-start.3 = ((bf16[32,48,128]{2,1,0:T(8,128)(2,1)}), bf16[32,48,128]{2,1,0:T(8,128)(2,1)S(1)}, u32[]{:S(2)}, u32[]{:S(2)}) async-start(bf16[32,48,128]{2,1,0:T(8,128)(2,1)} %pack.1), calls=%async_computation.3 | async-start | bytes 786432 | tf_op jit(solution)/shard_map/all_to_all | solution.py:414
  117.1 34.2 %copy-start.10 = (f32[512,256]{1,0:T(8,128)S(1)}, f32[512,256]{1,0:T(8,128)}, u32[]{:S(2)}) copy-start(f32[512,256]{1,0:T(8,128)} %get-tuple-element.40) | copy-start | bytes 1572868
  117.1 31.9 %collective-permute-start.6 = (bf16[64,4096]{1,0:T(8,128)(2,1)S(1)}, bf16[64,4096]{1,0:T(8,128)(2,1)S(1)}, u32[]{:S(2)}, u32[]{:S(2)}) collective-permute-start(bf16[64,4096]{1,0:T(8,128)(2,1)S(1)} %add_convert_fusion), channel_id=1, source_target_pairs={{0,2},{2,4},{4,6},{6,8},{8,10},{10,12},{12,14},{14,0},{1,15},{3,1}... | collective-permute-start | bytes 1572872 | tf_op jit(solution)/shard_map/ppermute | solution.py:411
  127.8 0.7 copy-start.3
  131.1 20.9 %all-to-all-start.4 = ((bf16[32,48,128]{2,1,0:T(8,128)(2,1)}), bf16[32,48,128]{2,1,0:T(8,128)(2,1)S(1)}, u32[]{:S(2)}, u32[]{:S(2)}) async-start(bf16[32,48,128]{2,1,0:T(8,128)(2,1)} %combine.1), calls=%async_computation.4 | async-start | bytes 786432 | tf_op jit(solution)/shard_map/all_to_all | solution.py:414
  137.3 13.9 %collective-permute-start.13 = (bf16[512,256]{1,0:T(8,128)(2,1)}, bf16[512,256]{1,0:T(8,128)(2,1)S(1)}, u32[]{:S(2)}, u32[]{:S(2)}) collective-permute-start(bf16[512,256]{1,0:T(8,128)(2,1)} %get-tuple-element.41), channel_id=1, source_target_pairs={{0,1},{1,0},{2,3},{3,2},{4,5},{5,4},{6,7},{7,6},{8,9},{9,8},{10,11... | collective-permute-start | bytes 786440 | tf_op jit(solution)/shard_map/ppermute | solution.py:408
  141.8 18.8 %collective-permute-start.3 = (bf16[32,4096]{1,0:T(8,128)(2,1)}, bf16[32,4096]{1,0:T(8,128)(2,1)S(1)}, u32[]{:S(2)}, u32[]{:S(2)}) collective-permute-start(bf16[32,4096]{1,0:T(8,128)(2,1)} %get-tuple-element.33), channel_id=1, source_target_pairs={{0,8},{2,10},{4,12},{6,14},{8,0},{10,2},{12,4},{14,6},{1,9},{3,11}... | collective-permute-start | bytes 786440 | tf_op jit(solution)/shard_map/ppermute | solution.py:468
  149.1 11.5 %collective-permute-start.7 = (bf16[32,4096]{1,0:T(8,128)(2,1)S(1)}, bf16[32,4096]{1,0:T(8,128)(2,1)S(1)}, u32[]{:S(2)}, u32[]{:S(2)}) collective-permute-start(bf16[32,4096]{1,0:T(8,128)(2,1)S(1)} %slice.13), channel_id=1, source_target_pairs={{0,1},{1,0},{2,3},{3,2},{4,5},{5,4},{6,7},{7,6},{8,9},{9,8},{10,11... | collective-permute-start | bytes 786440 | tf_op jit(solution)/shard_map/ppermute | solution.py:408
  152.0 8.6 %copy-start.8 = (f32[32,4096]{1,0:T(8,128)S(1)}, f32[32,4096]{1,0:T(8,128)}, u32[]{:S(2)}) copy-start(f32[32,4096]{1,0:T(8,128)} %get-tuple-element.32) | copy-start | bytes 1572868
  152.0 8.6 %copy-start.16 = (f32[4096]{0:T(1024)S(1)}, f32[4096]{0:T(1024)}, u32[]{:S(2)}) copy-start(f32[4096]{0:T(1024)} %div.26) | copy-start | bytes 49156
  152.0 0.7 copy-start.2
  157.1 5.4 %collective-permute-start.14 = (f32[72,2304]{1,0:T(8,128)}, f32[72,2304]{1,0:T(8,128)S(1)}, u32[]{:S(2)}, u32[]{:S(2)}) collective-permute-start(f32[72,2304]{1,0:T(8,128)} %get-tuple-element.46.mine_ref), channel_id=1, source_target_pairs={{0,1},{1,0},{2,3},{3,2},{4,5},{5,4},{6,7},{7,6},{8,9},{9,8},{10,11... | collective-permute-start | bytes 1990664 | tf_op jit(solution)/shard_map/ppermute | solution.py:408
  162.5 0.9 copy-start.7
